TPU v7x, 32 devices: a whole 2x2x4 slice. The times are simulated.
32 devices in a mesh: rep: 8 (over z, y), fsdp: 4 (over x, core).
Axes of the slice: x: 2, y: 2, z: 4, core: 2. Of those that a mesh axis runs over, the one named last changes fastest.
Arguments:
- tokens: bfloat16 [4096, 576], P(('rep', 'fsdp')), may hold values from -6 to 6
- positions: int32 [4096], P(('rep', 'fsdp')), may hold values from 0 to 1212, as said below
- seq_count: int32 [32], P(('rep', 'fsdp')), may hold values from 0 to 2, as said below
- w_query: bfloat16 [1, 576, 576], P(None, 'fsdp'), may hold values from -0.25 to 0.25
- w_keyval: bfloat16 [1, 576, 384], P(None, 'fsdp'), may hold values from -0.25 to 0.25
- w_out: bfloat16 [1, 576, 576], P(None, 'fsdp'), may hold values from -0.75 to 0.75
- w_gateup: bfloat16 [1, 576, 3072], P(None, 'fsdp'), may hold values from -0.25 to 0.25
- w_down: bfloat16 [1, 1536, 576], P(None, 'fsdp'), may hold values from -0.15625 to 0.15625
- gain_attn: bfloat16 [1, 576], P(None, 'fsdp'), may hold values from 0.099609375 to 1.8984375
- gain_mlp: bfloat16 [1, 576], P(None, 'fsdp'), may hold values from 0.099609375 to 1.8984375
- out_grad: bfloat16 [4096, 576], P(('rep', 'fsdp')), may hold values from -6 to 6
Outputs:
- out_act: float32 [4096, 576], P(('rep', 'fsdp'))
- in_grad: float32 [4096, 576], P(('rep', 'fsdp'))
- grad_query: float32 [1, 576, 576], P(None, 'fsdp')
- grad_keyval: float32 [1, 576, 384], P(None, 'fsdp')
- grad_out: float32 [1, 576, 576], P(None, 'fsdp')
- grad_gateup: float32 [1, 576, 3072], P(None, 'fsdp')
- grad_down: float32 [1, 1536, 576], P(None, 'fsdp')
- grad_gain_attn: float32 [1, 576], P(None, 'fsdp')
- grad_gain_mlp: float32 [1, 576], P(None, 'fsdp')
Inputs may be any that keep to these rules, and one draw needn't show every extreme that they name: Device d (rep index times 4 plus fsdp index) holds live sequences in its first seq_count[d] slots; the others hold data that no output may use. Some device fills all 2 slots. Within a sequence the positions rise by 1 to 3 from one token to the next; some sequence reaches the most.
All inputs are finite; a program needn't handle non-finite values.
Results may differ from a plain program's by a relative error of at most 0.015.
Values may be sent and summed in bfloat16 or wider, within the bound.
No kernel may reach another device: no remote copies, remote signals or barrier semaphores. Data moves between devices by JAX's collectives and lax.ppermute only.
A program may use at most 128 MiB of HBM per device.

v0:
```python
import jax
import jax.numpy as jnp
from jax import lax
from jax.sharding import PartitionSpec as P

HEADS = 9
KVH = 3
HD = 64
LAYERS = 1
LEN = 64


norm_eps = 1e-05
rope_base = 100000.0


def shortened(value):

    def short(part):
        return part.astype(jnp.bfloat16) if part.dtype == jnp.float32 else part

    return jax.tree.map(short, value)


def inverse_rms(stream):
    return lax.rsqrt(jnp.mean(stream * stream, axis=-1, keepdims=True) + norm_eps)


def rope_tables(positions):
    half_size = HD // 2
    frequency = rope_base ** (-(jnp.arange(half_size, dtype=jnp.float32) * 2.0 / HD))
    angle_table = positions.astype(jnp.float32)[:, None] * frequency[None, :]
    angle_table = jnp.concatenate([angle_table, angle_table], axis=-1)[:, None, :]
    return (jnp.cos(angle_table), jnp.sin(angle_table))


def rotate(values, cosine, sine_table):
    half_size = values.shape[-1] // 2
    turned = jnp.concatenate([-values[..., half_size:], values[..., :half_size]], axis=-1)
    return values * cosine + turned * sine_table


def rotate_back(grad_rot, cosine, sine_table):
    half_size = grad_rot.shape[-1] // 2
    scaled = grad_rot * sine_table
    turned = jnp.concatenate([scaled[..., half_size:], -scaled[..., :half_size]], axis=-1)
    return grad_rot * cosine + turned


def masked_scores(query_rot, key_rot, causal):
    scores = jnp.einsum(
        "sqkgd,spkd->skgqp", query_rot, key_rot, preferred_element_type=jnp.float32
    ) * HD ** (-0.5)
    return jnp.where(causal, scores, -1e30)


def forward_layer(stream, weights, cosine, sine_table, causal, seq_total):
    w_query, w_keyval, w_out, w_gateup, w_down, gain_attn, gain_mlp = weights
    row_count = stream.shape[0]
    seq_len = row_count // seq_total
    kv_width = KVH * HD
    inv_attn = inverse_rms(stream)
    normed = (stream * inv_attn * gain_attn.astype(jnp.float32)).astype(jnp.bfloat16)
    query_raw = jnp.dot(normed, w_query, preferred_element_type=jnp.float32)
    keyval = jnp.dot(normed, w_keyval, preferred_element_type=jnp.float32)
    query_rot = rotate(query_raw.reshape(row_count, HEADS, HD), cosine, sine_table).astype(
        jnp.bfloat16
    )
    query_rot = query_rot.reshape(seq_total, seq_len, KVH, HEADS // KVH, HD)
    key_rot = rotate(keyval[:, :kv_width].reshape(row_count, KVH, HD), cosine, sine_table).astype(
        jnp.bfloat16
    )
    key_rot = key_rot.reshape(seq_total, seq_len, KVH, HD)
    value_part = keyval[:, kv_width:].astype(jnp.bfloat16).reshape(seq_total, seq_len, KVH, HD)
    scores = masked_scores(query_rot, key_rot, causal)
    row_peak = jnp.max(scores, axis=-1, keepdims=True)
    exponent = jnp.exp(scores - row_peak)
    row_total = jnp.sum(exponent, axis=-1, keepdims=True)
    probs = (exponent / row_total).astype(jnp.bfloat16)
    log_total = row_peak + jnp.log(row_total)
    mixed_out = jnp.einsum(
        "skgqp,spkd->sqkgd", probs, value_part, preferred_element_type=jnp.float32
    )
    mixed_out = mixed_out.reshape(row_count, HEADS * HD).astype(jnp.bfloat16)
    stream_mid = stream + jnp.dot(mixed_out, w_out, preferred_element_type=jnp.float32)
    inv_mlp = inverse_rms(stream_mid)
    normed_mid = (stream_mid * inv_mlp * gain_mlp.astype(jnp.float32)).astype(jnp.bfloat16)
    gateup = jnp.dot(normed_mid, w_gateup, preferred_element_type=jnp.float32)
    ff_width = gateup.shape[1] // 2
    hidden = (jax.nn.silu(gateup[:, :ff_width]) * gateup[:, ff_width:]).astype(jnp.bfloat16)
    result = stream_mid + jnp.dot(hidden, w_down, preferred_element_type=jnp.float32)
    kept = (
        stream,
        inv_attn,
        normed,
        query_rot,
        key_rot,
        value_part,
        log_total,
        mixed_out,
        stream_mid,
        inv_mlp,
        normed_mid,
        gateup,
        hidden,
    )
    return (result, kept)


def backward_mlp(d_stream, kept, weights):
    (
        stream,
        inv_attn,
        normed,
        query_rot,
        key_rot,
        value_part,
        log_total,
        mixed_out,
        stream_mid,
        inv_mlp,
        normed_mid,
        gateup,
        hidden,
    ) = kept
    w_query, w_keyval, w_out, w_gateup, w_down, gain_attn, gain_mlp = weights
    ff_width = gateup.shape[1] // 2
    d_branch = d_stream.astype(jnp.bfloat16)
    grad_down = jnp.einsum("nf,nd->fd", hidden, d_branch, preferred_element_type=jnp.float32)
    d_hidden = jnp.einsum("nd,fd->nf", d_branch, w_down, preferred_element_type=jnp.float32)
    gate_part = gateup[:, :ff_width]
    up_part = gateup[:, ff_width:]
    sigmoid_gate = jax.nn.sigmoid(gate_part)
    d_gate = d_hidden * up_part * sigmoid_gate * (1.0 + gate_part * (1.0 - sigmoid_gate))
    d_up = d_hidden * gate_part * sigmoid_gate
    d_gateup = jnp.concatenate([d_gate, d_up], axis=1).astype(jnp.bfloat16)
    grad_gateup = jnp.einsum("nd,nf->df", normed_mid, d_gateup, preferred_element_type=jnp.float32)
    d_normed_mid = jnp.einsum("nf,df->nd", d_gateup, w_gateup, preferred_element_type=jnp.float32)
    grad_gain_mlp = jnp.sum(d_normed_mid * stream_mid * inv_mlp, axis=0)
    scaled_mid = d_normed_mid * gain_mlp.astype(jnp.float32)
    d_mid = (
        d_stream
        + inv_mlp * scaled_mid
        - inv_mlp**3 * stream_mid * jnp.mean(scaled_mid * stream_mid, axis=-1, keepdims=True)
    )
    return (d_mid, (grad_gateup, grad_down, grad_gain_mlp))


def backward_attn(d_mid, kept, weights, cosine, sine_table, causal):
    (
        stream,
        inv_attn,
        normed,
        query_rot,
        key_rot,
        value_part,
        log_total,
        mixed_out,
        stream_mid,
        inv_mlp,
        normed_mid,
        gateup,
        hidden,
    ) = kept
    w_query, w_keyval, w_out, w_gateup, w_down, gain_attn, gain_mlp = weights
    row_count = stream.shape[0]
    d_attn = d_mid.astype(jnp.bfloat16)
    grad_out = jnp.einsum("nd,ne->de", mixed_out, d_attn, preferred_element_type=jnp.float32)
    d_mixed = jnp.einsum("ne,de->nd", d_attn, w_out, preferred_element_type=jnp.float32).astype(
        jnp.bfloat16
    )
    d_mixed = d_mixed.reshape(query_rot.shape)
    soft = jnp.exp(masked_scores(query_rot, key_rot, causal) - log_total)
    probs = soft.astype(jnp.bfloat16)
    d_value = jnp.einsum("skgqp,sqkgd->spkd", probs, d_mixed, preferred_element_type=jnp.float32)
    d_probs = jnp.einsum(
        "sqkgd,spkd->skgqp", d_mixed, value_part, preferred_element_type=jnp.float32
    )
    d_scores = (soft * (d_probs - jnp.sum(d_probs * soft, axis=-1, keepdims=True))).astype(
        jnp.bfloat16
    )
    d_query_rot = jnp.einsum(
        "skgqp,spkd->sqkgd", d_scores, key_rot, preferred_element_type=jnp.float32
    ) * HD ** (-0.5)
    d_key_rot = jnp.einsum(
        "skgqp,sqkgd->spkd", d_scores, query_rot, preferred_element_type=jnp.float32
    ) * HD ** (-0.5)
    d_query = rotate_back(d_query_rot.reshape(row_count, HEADS, HD), cosine, sine_table)
    d_query = d_query.reshape(row_count, HEADS * HD).astype(jnp.bfloat16)
    d_key = rotate_back(d_key_rot.reshape(row_count, KVH, HD), cosine, sine_table).reshape(
        row_count, KVH * HD
    )
    d_keyval = jnp.concatenate([d_key, d_value.reshape(row_count, KVH * HD)], axis=1).astype(
        jnp.bfloat16
    )
    grad_query = jnp.einsum("nd,ne->de", normed, d_query, preferred_element_type=jnp.float32)
    grad_keyval = jnp.einsum("nd,ne->de", normed, d_keyval, preferred_element_type=jnp.float32)
    d_normed = jnp.einsum("ne,de->nd", d_query, w_query, preferred_element_type=jnp.float32)
    d_normed = d_normed + jnp.einsum(
        "ne,de->nd", d_keyval, w_keyval, preferred_element_type=jnp.float32
    )
    grad_gain_attn = jnp.sum(d_normed * stream * inv_attn, axis=0)
    scaled_in = d_normed * gain_attn.astype(jnp.float32)
    d_input = (
        d_mid
        + inv_attn * scaled_in
        - inv_attn**3 * stream * jnp.mean(scaled_in * stream, axis=-1, keepdims=True)
    )
    return (d_input, (grad_query, grad_keyval, grad_out, grad_gain_attn))


def on_device(
    tokens,
    positions,
    seq_count,
    w_query,
    w_keyval,
    w_out,
    w_gateup,
    w_down,
    gain_attn,
    gain_mlp,
    out_grad,
):
    row_count = tokens.shape[0]
    seq_total = row_count // LEN
    live_seqs = (jnp.arange(seq_total, dtype=jnp.int32) < seq_count[0]).astype(jnp.float32)
    live_rows = jnp.repeat(live_seqs, LEN)[:, None]
    gathered = (
        lax.all_gather(w_query, "fsdp", axis=1, tiled=True),
        lax.all_gather(w_keyval, "fsdp", axis=1, tiled=True),
        lax.all_gather(w_out, "fsdp", axis=1, tiled=True),
        lax.all_gather(w_gateup, "fsdp", axis=1, tiled=True),
        lax.all_gather(w_down, "fsdp", axis=1, tiled=True),
        lax.all_gather(gain_attn, "fsdp", axis=1, tiled=True),
        lax.all_gather(gain_mlp, "fsdp", axis=1, tiled=True),
    )
    cosine, sine_table = rope_tables(positions)
    causal = jnp.arange(LEN)[:, None] >= jnp.arange(LEN)[None, :]
    stream = tokens.astype(jnp.float32)
    layer_index = 0
    layer_weights = tuple((weight[layer_index] for weight in gathered))
    stream, kept = forward_layer(stream, layer_weights, cosine, sine_table, causal, seq_total)
    kept_list = [kept]
    out_act = stream * live_rows
    gathered = (
        lax.all_gather(w_query, "fsdp", axis=1, tiled=True),
        lax.all_gather(w_keyval, "fsdp", axis=1, tiled=True),
        lax.all_gather(w_out, "fsdp", axis=1, tiled=True),
        lax.all_gather(w_gateup, "fsdp", axis=1, tiled=True),
        lax.all_gather(w_down, "fsdp", axis=1, tiled=True),
        lax.all_gather(gain_attn, "fsdp", axis=1, tiled=True),
        lax.all_gather(gain_mlp, "fsdp", axis=1, tiled=True),
    )
    d_stream = out_grad.astype(jnp.float32) * live_rows
    grad_list = [None] * LAYERS
    for layer_index in reversed(range(LAYERS)):
        layer_weights = tuple((weight[layer_index] for weight in gathered))
        d_mid, mlp_grads = backward_mlp(d_stream, kept_list[layer_index], layer_weights)
        d_stream, attn_grads = backward_attn(
            d_mid, kept_list[layer_index], layer_weights, cosine, sine_table, causal
        )
        grad_list[layer_index] = (
            attn_grads[0],
            attn_grads[1],
            attn_grads[2],
            mlp_grads[0],
            mlp_grads[1],
            attn_grads[3],
            mlp_grads[2],
        )
    stacked = tuple((jnp.stack([entry[member] for entry in grad_list]) for member in range(7)))
    shared = jax.tree.map(
        lambda part: part.astype(jnp.float32),
        lax.psum_scatter(shortened(stacked), "fsdp", scatter_dimension=1, tiled=True),
    )
    stacked = lax.psum(shared, "rep")
    return (out_act, d_stream) + tuple(stacked)


def solution(mesh):
    placed = (
        P(("rep", "fsdp"), None),
        P(("rep", "fsdp")),
        P(("rep", "fsdp")),
        P(None, "fsdp", None),
        P(None, "fsdp", None),
        P(None, "fsdp", None),
        P(None, "fsdp", None),
        P(None, "fsdp", None),
        P(None, "fsdp"),
        P(None, "fsdp"),
        P(("rep", "fsdp"), None),
    )
    return jax.shard_map(
        on_device,
        mesh=mesh,
        in_specs=placed,
        out_specs=(
            P(("rep", "fsdp"), None),
            P(("rep", "fsdp"), None),
            P(None, "fsdp", None),
            P(None, "fsdp", None),
            P(None, "fsdp", None),
            P(None, "fsdp", None),
            P(None, "fsdp", None),
            P(None, "fsdp"),
            P(None, "fsdp"),
        ),
        check_vma=False,
    )
```

profile of v0, /device:TPU:0, one launch (start us, length us, event | category | flops | bytes accessed | tf_op | source)
XLA Modules:
  0.0 433.5 jit_solution(7675057205242785737)
XLA Ops:
  11.5 1.0 fusion.37
  13.0 1.2 dynamic-slice
  15.3 8.3 %all-reduce.3 = (bf16[576]{0:T(1024)(128)(2,1)S(1)}, bf16[576]{0:T(1024)(128)(2,1)S(1)}) all-reduce(bf16[576]{0:T(1024)(128)(2,1)S(1)} %dynamic-update-slice, bf16[576]{0:T(1024)(128)(2,1)S(1)} %dynamic-update-slice.1), channel_id=1, replica_groups=mesh['rep'=8,'fsdp'=4] {'fsdp'}, use_global_device_ids=true, to_apply=%add | all-reduce | flops 1152 | bytes 4608
  23.8 9.4 %all_gather.29 = bf16[1,576,384]{2,1,0:T(8,128)(2,1)S(1)} all-gather(bf16[1,144,384]{2,1,0:T(8,128)(2,1)} %param.15), channel_id=1, replica_groups=mesh['rep'=8,'fsdp'=4] {'fsdp'}, dimensions={1}, use_global_device_ids=true | all-gather | bytes 552960 | tf_op jit(solution)/shard_map/all_gather | solution.py:231
  33.8 12.8 %all_gather.30 = bf16[1,576,576]{2,1,0:T(8,128)(2,1)S(1)} all-gather(bf16[1,144,576]{2,1,0:T(8,128)(2,1)S(1)} %copy-done.23), channel_id=1, replica_groups=mesh['rep'=8,'fsdp'=4] {'fsdp'}, dimensions={1}, use_global_device_ids=true | all-gather | bytes 829440 | tf_op jit(solution)/shard_map/all_gather | solution.py:230
  49.4 1.1 fusion.67
  52.1 8.7 %all_gather.31 = bf16[1,576,576]{2,1,0:T(8,128)(2,1)S(1)} all-gather(bf16[1,144,576]{2,1,0:T(8,128)(2,1)} %param.16), channel_id=1, replica_groups=mesh['rep'=8,'fsdp'=4] {'fsdp'}, dimensions={1}, use_global_device_ids=true | all-gather | bytes 829440 | tf_op jit(solution)/shard_map/all_gather | solution.py:232
  62.4 4.1 fusion.3
  66.5 5.3 %all-gather.5.cloned.1.call-done = bf16[1,1536,576]{1,2,0:T(8,128)(2,1)} async-done(((bf16[1,384,576]{1,2,0:T(8,128)(2,1)}), bf16[1,1536,576]{1,2,0:T(8,128)(2,1)}) %all-gather.5.cloned.1.call-update) | async-done | bytes 1769488 | tf_op jit(solution)/shard_map/all_gather | solution.py:234
  71.8 3.6 multiply_convert_fusion.1
  75.5 1.8 multiply_reduce_fusion.1
  77.4 1.0 convolution_convert_fusion.6
  78.5 1.1 reshape.234
  79.5 1.6 fusion.26
  81.1 1.1 multiply_reduce_fusion
  88.5 1.1 fusion.15
  89.6 1.2 fusion.11
  91.4 1.3 fusion.10
  93.3 6.0 %copy.98 = bf16[1,1536,576]{2,0,1:T(2,128)(2,1)} copy(bf16[1,1536,576]{1,2,0:T(8,128)(2,1)S(1)} %fusion.5) | data formatting | bytes 3538944
  99.3 3.8 copy.124
  103.2 0.9 copy-done.19
  104.2 2.9 fusion
  107.7 0.9 fusion.41
  108.6 1.3 fusion.20
  110.8 16.5 %reduce-scatter.24.cloned.1.call-done = bf16[144,1]{1,0:T(8,128)(2,1)} async-done(((bf16[576,1]{1,0:T(8,128)(2,1)}), bf16[144,1]{1,0:T(8,128)(2,1)}) %reduce-scatter.24.cloned.1.call-update) | async-done | bytes 304
  128.1 22.7 %reduce-scatter.16.cloned.1.call-done = bf16[1,144,384]{2,1,0:T(8,128)(2,1)} async-done(((bf16[1,576,384]{2,1,0:T(8,128)(2,1)}), bf16[1,144,384]{2,1,0:T(8,128)(2,1)}) %reduce-scatter.16.cloned.1.call-update) | async-done | bytes 110608 | tf_op jit(solution)/shard_map/reduce_scatter | solution.py:275
  150.8 26.0 %reduce-scatter.18.cloned.1.call-done = bf16[1,144,576]{2,1,0:T(8,128)(2,1)} async-done(((bf16[1,576,576]{2,1,0:T(8,128)(2,1)}), bf16[1,144,576]{2,1,0:T(8,128)(2,1)}) %reduce-scatter.18.cloned.1.call-update) | async-done | bytes 165904 | tf_op jit(solution)/shard_map/reduce_scatter | solution.py:275
  176.8 26.3 %reduce-scatter.14.cloned.1.call-done = bf16[1,144,576]{2,1,0:T(8,128)(2,1)} async-done(((bf16[1,576,576]{2,1,0:T(8,128)(2,1)}), bf16[1,144,576]{2,1,0:T(8,128)(2,1)}) %reduce-scatter.14.cloned.1.call-update) | async-done | bytes 165904 | tf_op jit(solution)/shard_map/reduce_scatter | solution.py:275
  203.1 33.2 %reduce-scatter.22.cloned.1.call-done = bf16[384,576]{1,0:T(8,128)(2,1)} async-done(((bf16[1536,576]{1,0:T(8,128)(2,1)}), bf16[384,576]{1,0:T(8,128)(2,1)}) %reduce-scatter.22.cloned.1.call-update) | async-done | bytes 442384
  236.3 1.5 reshape_bitcast_fusion
  238.5 41.0 %reduce-scatter.20.cloned.1.call-done = bf16[1,144,3072]{2,1,0:T(8,128)(2,1)} async-done(((bf16[1,576,3072]{2,1,0:T(8,128)(2,1)}), bf16[1,144,3072]{2,1,0:T(8,128)(2,1)}) %reduce-scatter.20.cloned.1.call-update) | async-done | bytes 884752 | tf_op jit(solution)/shard_map/reduce_scatter | solution.py:275
  279.5 147.5 %all-reduce.5 = (f32[1,144,576]{2,1,0:T(8,128)}, f32[1,144,384]{2,1,0:T(8,128)}, f32[1,144,576]{2,1,0:T(8,128)}, f32[1,144,3072]{2,1,0:T(8,128)}, f32[1,384,576]...) all-reduce(bf16[1,144,576]{2,1,0:T(8,128)(2,1)S(1)} %copy-done.25, ...), channel_id=1, replica_groups=mesh['rep'=8,'fsdp'=4] {'rep'}, use_global_device_ids=true, to_apply=%region_8.9 | all-reduce | flops 885024 | bytes 5310144 | tf_op jit(solution)/shard_map/psum | solution.py:277
  (157 shorter events, 21.6 us)
Async XLA Ops:
  7.2 26.0 %copy-start = (bf16[128,576]{0,1:T(8,128)(2,1)S(1)}, bf16[128,576]{0,1:T(8,128)(2,1)}, u32[]{:S(2)}) copy-start(bf16[128,576]{0,1:T(8,128)(2,1)} %param.11) | copy-start | bytes 442372
  7.2 26.6 %copy-start.23 = (bf16[1,144,576]{2,1,0:T(8,128)(2,1)S(1)}, bf16[1,144,576]{2,1,0:T(8,128)(2,1)}, u32[]{:S(2)}) copy-start(bf16[1,144,576]{2,1,0:T(8,128)(2,1)} %param.14) | copy-start | bytes 497668
  7.2 55.2 %all-gather.3.cloned.1.call-start = ((), (), s32[]{:S(2)}) async-start(), calls=%async_computation.7 | async-start | bytes 4423680 | tf_op jit(solution)/shard_map/all_gather | solution.py:233
  7.9 63.9 %all-gather.5.cloned.1.call-start = ((), (), s32[]{:S(2)}) async-start(), calls=%async_computation.8 | async-start | bytes 2211840 | tf_op jit(solution)/shard_map/all_gather | solution.py:234
  8.7 101.3 %reduce-scatter.26.cloned.1.call-start = ((), (), s32[]{:S(2)}) async-start(), calls=%async_computation.15 | async-start | bytes 184320
  23.8 23.6 %copy-start.8 = (f32[128,64]{0,1:T(8,128)}, f32[128,64]{0,1:T(8,128)S(1)}, u32[]{:S(2)}) copy-start(f32[128,64]{0,1:T(8,128)S(1)} %get-tuple-element.37) | copy-start | bytes 98308
  23.8 23.6 %copy-start.13 = (f32[128,64]{0,1:T(8,128)}, f32[128,64]{0,1:T(8,128)S(1)}, u32[]{:S(2)}) copy-start(f32[128,64]{0,1:T(8,128)S(1)} %get-tuple-element.38) | copy-start | bytes 98308
  48.9 2.7 copy-start.15
  52.1 14.4 %copy-start.4 = (bf16[128,576]{0,1:T(8,128)(2,1)}, bf16[128,576]{0,1:T(8,128)(2,1)S(1)}, u32[]{:S(2)}) copy-start(bf16[128,576]{0,1:T(8,128)(2,1)S(1)} %convert_element_type.167) | copy-start | bytes 442372
  62.4 9.4 %copy-start.10 = (bf16[128,576]{0,1:T(8,128)(2,1)S(1)}, bf16[128,576]{0,1:T(8,128)(2,1)}, u32[]{:S(2)}) copy-start(bf16[128,576]{0,1:T(8,128)(2,1)} %param.21) | copy-start | bytes 442372
  71.8 3.6 copy-start.1
  75.4 1.8 copy-start.18
  75.4 1.8 copy-start.20
  75.5 1.8 copy-start.11
  75.5 1.8 copy-start.27
  75.5 1.8 copy-start.31
  78.5 3.8 copy-start.22
  82.5 2.7 copy-start.17
  82.5 2.9 copy-start.14
  84.9 42.3 %reduce-scatter.24.cloned.1.call-start = ((), (), s32[]{:S(2)}) async-start(), calls=%async_computation.14 | async-start | bytes 184320
  86.8 2.9 copy-start.5
  88.4 62.4 %reduce-scatter.16.cloned.1.call-start = ((), (), s32[]{:S(2)}) async-start(), calls=%async_computation.10 | async-start | bytes 552960 | tf_op jit(solution)/shard_map/reduce_scatter | solution.py:275
  89.6 87.2 %reduce-scatter.18.cloned.1.call-start = ((), (), s32[]{:S(2)}) async-start(), calls=%async_computation.11 | async-start | bytes 921600 | tf_op jit(solution)/shard_map/reduce_scatter | solution.py:275
  90.9 1.8 copy-start.3
  90.9 1.8 copy-start.12
  90.9 1.8 copy-start.28
  90.9 112.1 %reduce-scatter.14.cloned.1.call-start = ((), (), s32[]{:S(2)}) async-start(), calls=%async_computation.9 | async-start | bytes 921600 | tf_op jit(solution)/shard_map/reduce_scatter | solution.py:275
  92.7 143.6 %reduce-scatter.22.cloned.1.call-start = ((), (), s32[]{:S(2)}) async-start(), calls=%async_computation.13 | async-start | bytes 2457600
  103.1 176.4 %reduce-scatter.20.cloned.1.call-start = ((), (), s32[]{:S(2)}) async-start(), calls=%async_computation.12 | async-start | bytes 4423680 | tf_op jit(solution)/shard_map/reduce_scatter | solution.py:275
  150.8 128.7 %copy-start.26 = (bf16[1,144,384]{2,1,0:T(8,128)(2,1)S(1)}, bf16[1,144,384]{2,1,0:T(8,128)(2,1)}, u32[]{:S(2)}) copy-start(bf16[1,144,384]{2,1,0:T(8,128)(2,1)} %reduce-scatter.16.cloned.1.call-done) | copy-start | bytes 331780
  176.8 102.7 %copy-start.24 = (bf16[1,144,576]{2,1,0:T(8,128)(2,1)S(1)}, bf16[1,144,576]{2,1,0:T(8,128)(2,1)}, u32[]{:S(2)}) copy-start(bf16[1,144,576]{2,1,0:T(8,128)(2,1)} %reduce-scatter.18.cloned.1.call-done) | copy-start | bytes 497668
  203.1 76.4 %copy-start.25 = (bf16[1,144,576]{2,1,0:T(8,128)(2,1)S(1)}, bf16[1,144,576]{2,1,0:T(8,128)(2,1)}, u32[]{:S(2)}) copy-start(bf16[1,144,576]{2,1,0:T(8,128)(2,1)} %reduce-scatter.14.cloned.1.call-done) | copy-start | bytes 497668
  (9 other events, 10.1 us)
Sparse Core Ops, SparseCore 0:
  9.6 39.8 all-gather.2
  51.0 20.7 all-gather.4
  85.0 19.6 reduce-scatter.25
  107.6 19.6 reduce-scatter.23
  129.6 21.1 reduce-scatter.15
  153.8 22.9 reduce-scatter.17
  180.1 22.9 reduce-scatter.13
  205.6 30.6 reduce-scatter.21
  239.0 40.4 reduce-scatter.19
where the time goes:
time: 434 us
  blocking collectives  187 us (43%)
  waiting for transfers between devices  172 us (40%)
  local copies, waits for them, and re-layouts  25.4 us (6%)
  matrix products  24.8 us (6%)
  between operations  15.8 us (4%)
  other arithmetic  7.81 us (2%)
    psum x1, blocking collectives, on_device(): stacked = lax.psum(shared, 'rep')  147 us
    reduce_scatter x4, waiting for transfers between devices, on_device(): lax.psum_scatter(shortened(stacked), 'fsdp', scatter_dimension=1, tiled=T...  116 us
    unnamed x12, waiting for transfers between devices  51.2 us
    unnamed x77, local copies, waits for them, and re-layouts  19.3 us
    all_gather x1, blocking collectives, on_device(): lax.all_gather(w_query, 'fsdp', axis=1, tiled=True)  12.8 us
    all_gather x1, blocking collectives, on_device(): lax.all_gather(w_keyval, 'fsdp', axis=1, tiled=True)  9.39 us
  transfers between devices with their start and end apart: 9, of which 7 were waited for; matrix products, arithmetic and copies ran while one was open for 10% of the time, Pallas kernels for 0%

commit v1 on v0

v1 whole, which is shorter than its diff:
```python
import functools

import jax
import jax.numpy as jnp
from jax import lax
from jax.experimental import pallas as pl
from jax.experimental.pallas import tpu as pltpu
from jax.sharding import PartitionSpec as P

HEADS = 9
KVH = 3
HD = 64
LEN = 64
norm_eps = 1e-05
rope_base = 100000.0

BLOCK = 128
PAIRS = 5
QW = PAIRS * 128
F32 = jnp.float32
BF16 = jnp.bfloat16


def mm(left, right):
    return jnp.dot(left, right, preferred_element_type=F32)


def mm_nt(left, right):
    return lax.dot_general(left, right, (((1,), (1,)), ((), ())), preferred_element_type=F32)


def mm_tn(left, right):
    return lax.dot_general(left, right, (((0,), (0,)), ((), ())), preferred_element_type=F32)


def inverse_rms(stream):
    return lax.rsqrt(jnp.mean(stream * stream, axis=-1, keepdims=True) + norm_eps)


def lane_index(shape):
    return lax.broadcasted_iota(jnp.int32, shape, 1)


def own_columns(shard, rows, width):
    row = lax.broadcasted_iota(jnp.int32, (rows, width), 0)
    column = lax.broadcasted_iota(jnp.int32, (rows, width), 1)
    return (row == column + shard * width).astype(BF16)


def swapped(values, first_half):
    return jnp.where(first_half, pltpu.roll(values, 96, 1), pltpu.roll(values, 32, 1))


def split_heads(keyval):
    low = lane_index((BLOCK, 128)) < HD
    slices = [keyval[:, 128 * part : 128 * part + 128].astype(F32) for part in range(3)]

    def pair(piece, is_low):
        kept = jnp.where(low, piece, 0.0) if is_low else jnp.where(low, 0.0, piece)
        moved = pltpu.roll(kept, HD, 1)
        kept, moved = kept.astype(BF16), moved.astype(BF16)
        return (kept, moved) if is_low else (moved, kept)

    keys = [pair(slices[0], True), pair(slices[0], False), pair(slices[1], True)]
    values = [pair(slices[1], False), pair(slices[2], True), pair(slices[2], False)]
    return keys, values


def pair_operand(parts, pair):
    first = parts[(2 * pair) * KVH // HEADS][0]
    if 2 * pair + 1 >= HEADS:
        return first
    return jnp.concatenate([first, parts[(2 * pair + 1) * KVH // HEADS][1]], axis=0)


def attention_mask():
    query = lax.broadcasted_iota(jnp.int32, (BLOCK, BLOCK), 0)
    key = lax.broadcasted_iota(jnp.int32, (BLOCK, BLOCK), 1)
    return (query // LEN == key // LEN) & (query >= key)


def soft_rows(scores, allowed):
    halves = []
    for start in range(0, scores.shape[1], BLOCK):
        part = jnp.where(allowed, scores[:, start : start + BLOCK] * HD ** (-0.5), -1e30)
        part = jnp.exp(part - jnp.max(part, axis=-1, keepdims=True))
        halves.append(part / jnp.sum(part, axis=-1, keepdims=True))
    return halves


def joined(halves):
    return halves[0] if len(halves) == 1 else jnp.concatenate(halves, axis=1)


def attn_forward_kernel(n_shard, idx, *refs):
    tok = refs[:n_shard]
    small = refs[n_shard : 2 * n_shard]
    wq = refs[2 * n_shard : 3 * n_shard]
    wkv = refs[3 * n_shard : 4 * n_shard]
    wo = refs[4 * n_shard : 5 * n_shard]
    (x_ref, nrm_ref, q_ref, kv_ref, mix_ref, mid_ref, nmid_ref, cos_ref, sin_ref, gain_ref,
     wq_full, wkv_full, wo_full) = refs[5 * n_shard :]
    shard = idx[0]
    width = wq[0].shape[0]
    model = x_ref.shape[1]
    wq_full[:, model:] = jnp.zeros((model, QW - model), BF16)
    wo_full[model:, :] = jnp.zeros((QW - model, model), BF16)
    gains = jnp.zeros((16, model), F32)
    for part in range(n_shard):
        at = pl.multiple_of((shard ^ part) * width, 16)
        wq_full[pl.ds(at, width), :model] = wq[part][...]
        wkv_full[pl.ds(at, width), :] = wkv[part][...]
        wo_full[pl.ds(at, width), :] = wo[part][...]
        row = lax.broadcasted_iota(jnp.int32, (256, model), 0)
        column = lax.broadcasted_iota(jnp.int32, (256, model), 1)
        place = ((column == row + at) & (row < width)).astype(BF16)
        gains = gains + mm(small[part][...], place)
    gain_ref[...] = gains
    half = HD // 2
    step = lax.broadcasted_iota(jnp.int32, (half, 1), 0).astype(F32)
    frequency = jnp.exp(step * (-2.0 / HD * jnp.log(F32(rope_base))))
    for part in range(n_shard):
        codes = small[part][...].astype(F32)
        position = codes[0:1, :BLOCK] * 64.0 + codes[1:2, :BLOCK]
        angle = frequency * position
        rows = pl.ds(part * BLOCK, BLOCK)
        cos_ref[rows, :] = jnp.concatenate([jnp.cos(angle)] * 4, axis=0).T
        sin_ref[rows, :] = jnp.concatenate([jnp.sin(angle)] * 4, axis=0).T
        x_ref[rows, :] = tok[part][...]
    allowed = attention_mask()
    lane = lane_index((BLOCK, 128))
    first_half = lane % HD < half
    gain_attn = gains[2:3, :]
    gain_mlp = gains[3:4, :]

    def body(block, carry):
        rows = pl.ds(pl.multiple_of(block * BLOCK, BLOCK), BLOCK)
        stream = x_ref[rows, :].astype(F32)
        normed = (stream * inverse_rms(stream) * gain_attn).astype(BF16)
        nrm_ref[rows, :] = normed
        cosine = cos_ref[rows, :]
        sine = sin_ref[rows, :]
        sine = jnp.where(first_half, -sine, sine)
        query_raw = mm(normed, wq_full[...])
        keyval = mm(normed, wkv_full[...])

        def rope(values):
            return values * cosine + swapped(values, first_half) * sine

        key_first = rope(keyval[:, :128])
        key_second = jnp.where(lane < HD, rope(keyval[:, 128:256]), keyval[:, 128:256])
        keyval = jnp.concatenate([key_first, key_second, keyval[:, 256:]], axis=1).astype(BF16)
        kv_ref[rows, :] = keyval
        keys, values = split_heads(keyval)
        mixed = []
        for pair in range(PAIRS):
            query = rope(query_raw[:, 128 * pair : 128 * pair + 128]).astype(BF16)
            q_ref[rows, 128 * pair : 128 * pair + 128] = query
            soft = soft_rows(mm_nt(query, pair_operand(keys, pair)), allowed)
            mixed.append(mm(joined(soft).astype(BF16), pair_operand(values, pair)).astype(BF16))
        mixed = jnp.concatenate(mixed, axis=1)
        mix_ref[rows, :] = mixed
        stream_mid = stream + mm(mixed, wo_full[...])
        mid_ref[rows, :] = stream_mid
        nmid_ref[rows, :] = (stream_mid * inverse_rms(stream_mid) * gain_mlp).astype(BF16)
        return carry

    lax.fori_loop(0, n_shard, body, 0)


def bit_reverse(value, total):
    result = jnp.zeros_like(value)
    bit = 1
    while bit < total:
        result = result * 2 + (value & 1)
        value = value >> 1
        bit *= 2
    return result


def mlp_kernel(n_shard, n_rep, idx, *refs):
    nmid_ref, mid_ref, live_ref = refs[:3]
    cot = refs[3 : 3 + n_shard]
    wgu = refs[3 + n_shard : 3 + 2 * n_shard]
    wd = refs[3 + 2 * n_shard : 3 + 3 * n_shard]
    (act_ref, dn_ref, down_lo, down_hi, gu_lo, gu_hi, dcot_ref, w_full, down_all, gu_all) = refs[3 + 3 * n_shard :]
    shard = idx[0]
    member = idx[1]
    width = wgu[0].shape[0]
    ff = wgu[0].shape[1] // 2
    chunk = ff // n_shard
    for part in range(n_shard):
        at = pl.multiple_of((shard ^ part) * width, 16)
        w_full[pl.ds(at, width), :] = wgu[part][...]
        dcot_ref[pl.ds(part * BLOCK, BLOCK), :] = cot[part][...]
    normed_mid = nmid_ref[...]
    own_mid = mm(normed_mid, own_columns(shard, normed_mid.shape[1], width)).astype(BF16)
    d_branch = dcot_ref[...]
    result = mid_ref[...]
    gu_rows = gu_all.shape[1]
    groups = width // gu_rows
    down_rows = down_all.shape[1]
    for part in range(n_shard):
        place = shard ^ part
        gate_at = pl.ds(pl.multiple_of(place * chunk, 128), chunk)
        up_at = pl.ds(pl.multiple_of(place * chunk + ff, 128), chunk)
        gate = mm(normed_mid, w_full[:, gate_at])
        up = mm(normed_mid, w_full[:, up_at])
        d_hidden = mm_nt(d_branch, wd[part][...])
        sigmoid = 1.0 / (1.0 + jnp.exp(-gate))
        silu = gate * sigmoid
        hidden = (silu * up).astype(BF16)
        d_gate = (d_hidden * up * sigmoid * (1.0 + gate * (1.0 - sigmoid))).astype(BF16)
        d_up = (d_hidden * silu).astype(BF16)
        d_normed = mm_nt(d_gate, w_full[:, gate_at]) + mm_nt(d_up, w_full[:, up_at])
        if part == 0:
            dn_ref[...] = d_normed
            grad_down = mm_tn(hidden, d_branch)
            for slab in range(n_rep):
                to = bit_reverse(member ^ slab, n_rep)
                down_all[to] = grad_down[slab * down_rows : (slab + 1) * down_rows].astype(BF16)
        else:
            dn_ref[...] += d_normed
        result = result + mm(hidden[:BLOCK], wd[part][...])
        for offset, piece in ((0, d_gate), (n_shard, d_up)):
            grad = mm_tn(own_mid, piece)
            for group in range(groups):
                to = bit_reverse(member ^ ((place + offset) * groups + group), n_rep)
                gu_all[to] = grad[group * gu_rows : (group + 1) * gu_rows].astype(BF16)
    act_ref[...] = result * live_ref[...]
    middle = n_rep // 2
    down_lo[...] = down_all[:middle]
    down_hi[...] = down_all[middle:]
    gu_lo[...] = gu_all[:middle]
    gu_hi[...] = gu_all[middle:]


def attn_backward_kernel(n_shard, n_rep, idx, x_ref, nrm_ref, q_ref, kv_ref, mix_ref, mid_ref, cos_ref, sin_ref,
                         gain_ref, wq_full, wkv_full, wo_full, dn_ref, dcot_ref,
                         din_ref, a_lo, a_hi, dattn_all, dq_all, dkv_all, a_all):
    shard = idx[0]
    member = idx[1]
    model = x_ref.shape[1]
    width = model // n_shard
    half = HD // 2
    allowed = attention_mask()
    lane = lane_index((BLOCK, 128))
    first_half = lane % HD < half
    low = lane < HD
    gain_attn = gain_ref[2:3, :]
    gain_mlp = gain_ref[3:4, :]

    def body(block, carry):
        sum_attn, sum_mlp = carry
        rows = pl.ds(pl.multiple_of(block * BLOCK, BLOCK), BLOCK)
        stream = x_ref[rows, :].astype(F32)
        stream_mid = mid_ref[rows, :]
        inv_mlp = inverse_rms(stream_mid)
        d_normed_mid = dn_ref[rows, :]
        sum_mlp = sum_mlp + jnp.sum(d_normed_mid * stream_mid * inv_mlp, axis=0, keepdims=True)
        scaled = d_normed_mid * gain_mlp
        d_mid = (
            dcot_ref[rows, :].astype(F32)
            + inv_mlp * scaled
            - inv_mlp**3 * stream_mid * jnp.mean(scaled * stream_mid, axis=-1, keepdims=True)
        )
        d_attn = d_mid.astype(BF16)
        dattn_all[rows, :] = d_attn
        d_mixed = mm_nt(d_attn, wo_full[...]).astype(BF16)
        cosine = cos_ref[rows, :]
        sine = sin_ref[rows, :]
        sine = jnp.where(first_half, sine, -sine)

        def rope_back(grad):
            return grad * cosine + swapped(grad, first_half) * sine

        keyval = kv_ref[rows, :]
        keys, values = split_heads(keyval)
        d_keys = [[None, None] for _ in range(KVH)]
        d_values = [[None, None] for _ in range(KVH)]
        d_query = []

        def add_to(store, head, side, piece):
            held = store[head * KVH // HEADS][side]
            store[head * KVH // HEADS][side] = piece if held is None else held + piece

        for pair in range(PAIRS):
            columns = slice(128 * pair, 128 * pair + 128)
            query = q_ref[rows, columns]
            key_pair = pair_operand(keys, pair)
            d_mixed_pair = d_mixed[:, columns]
            soft = soft_rows(mm_nt(query, key_pair), allowed)
            d_probs = mm_nt(d_mixed_pair, pair_operand(values, pair))
            probs = joined(soft).astype(BF16)
            d_scores = []
            for side, part in enumerate(soft):
                d_part = d_probs[:, side * BLOCK : (side + 1) * BLOCK]
                d_scores.append(part * (d_part - jnp.sum(d_part * part, axis=-1, keepdims=True)))
            d_scores = joined(d_scores).astype(BF16)
            d_query.append(rope_back(mm(d_scores, key_pair) * HD ** (-0.5)).astype(BF16))
            d_key_pair = mm_tn(d_scores, query)
            d_value_pair = mm_tn(probs, d_mixed_pair)
            for side in range(len(soft)):
                here = slice(side * BLOCK, (side + 1) * BLOCK)
                add_to(d_keys, 2 * pair + side, side, d_key_pair[here])
                add_to(d_values, 2 * pair + side, side, d_value_pair[here])
        d_query = jnp.concatenate(d_query, axis=1)

        def placed(pieces, to_low):
            low_piece, high_piece = pieces
            if to_low:
                total = jnp.where(low, low_piece, 0.0)
                return total if high_piece is None else total + jnp.where(low, pltpu.roll(high_piece, HD, 1), 0.0)
            total = jnp.where(low, 0.0, pltpu.roll(low_piece, HD, 1))
            return total if high_piece is None else total + jnp.where(low, 0.0, high_piece)

        scale = HD ** (-0.5)
        first = rope_back((placed(d_keys[0], True) + placed(d_keys[1], False)) * scale)
        second = rope_back(placed(d_keys[2], True) * scale) + placed(d_values[0], False)
        third = placed(d_values[1], True) + placed(d_values[2], False)
        d_keyval = jnp.concatenate([first, second, third], axis=1).astype(BF16)
        dq_all[rows, :] = d_query
        dkv_all[rows, :] = d_keyval
        d_normed = mm_nt(d_query, wq_full[...]) + mm_nt(d_keyval, wkv_full[...])
        inv_attn = inverse_rms(stream)
        sum_attn = sum_attn + jnp.sum(d_normed * stream * inv_attn, axis=0, keepdims=True)

        @pl.when(block == 0)
        def _():
            scaled_in = d_normed * gain_attn
            din_ref[...] = (
                d_mid
                + inv_attn * scaled_in
                - inv_attn**3 * stream * jnp.mean(scaled_in * stream, axis=-1, keepdims=True)
            )

        return (sum_attn, sum_mlp)

    zero = jnp.zeros((1, model), F32)
    sum_attn, sum_mlp = lax.fori_loop(0, n_shard, body, (zero, zero))
    chosen = own_columns(shard, model, width)
    own_normed = mm(nrm_ref[...], chosen).astype(BF16)
    own_mixed = mm(mix_ref[:, :model], chosen).astype(BF16)
    kv_width = dkv_all.shape[1]
    a_all[:width, :] = mm_tn(own_normed, dq_all[:, :model])
    a_all[width : 2 * width, :] = mm_tn(own_mixed, dattn_all[...])
    a_all[2 * width : 3 * width, :kv_width] = mm_tn(own_normed, dkv_all[...])
    a_all[2 * width : 3 * width, kv_width:] = jnp.zeros((width, model - kv_width), F32)
    tail = a_all.shape[0] - 3 * width
    row = lax.broadcasted_iota(jnp.int32, (tail, model), 0)
    a_all[3 * width :, :] = jnp.where(row == 0, sum_attn, jnp.where(row == 1, sum_mlp, 0.0))
    rows = a_all.shape[0] // n_rep
    middle = n_rep // 2
    for slab in range(n_rep):
        to = bit_reverse(member ^ slab, n_rep)
        piece = a_all[slab * rows : (slab + 1) * rows, :].astype(BF16)

        @pl.when(to < middle)
        def _():
            a_lo[to] = piece

        @pl.when(to >= middle)
        def _():
            a_hi[to - middle] = piece


def unpack_down_kernel(n_rep, idx, first, second, out_ref):
    member = idx[1]
    middle = n_rep // 2
    rows = first.shape[1]
    for slab in range(n_rep):
        at = bit_reverse(member ^ slab, n_rep)
        here = pl.ds(slab * rows, rows)

        @pl.when(at < middle)
        def _():
            out_ref[here, :] = first[at].astype(F32)

        @pl.when(at >= middle)
        def _():
            out_ref[here, :] = second[at - middle].astype(F32)


def unpack_gateup_kernel(n_rep, idx, first, second, out_ref):
    member = idx[1]
    middle = n_rep // 2
    rows, columns = first.shape[1:]
    groups = out_ref.shape[0] // rows
    for slab in range(n_rep):
        at = bit_reverse(member ^ slab, n_rep)
        down = pl.ds((slab % groups) * rows, rows)
        across = pl.ds((slab // groups) * columns, columns)

        @pl.when(at < middle)
        def _():
            out_ref[down, across] = first[at].astype(F32)

        @pl.when(at >= middle)
        def _():
            out_ref[down, across] = second[at - middle].astype(F32)


def unpack_attn_kernel(n_rep, idx, first, second, q_ref, kv_ref, o_ref, gain_ref, a_all):
    unpack_down_kernel(n_rep, idx, first, second, a_all)
    width = q_ref.shape[0]
    q_ref[...] = a_all[:width, :]
    o_ref[...] = a_all[width : 2 * width, :]
    kv_ref[...] = a_all[2 * width : 3 * width, : kv_ref.shape[1]]
    gain_ref[...] = a_all[3 * width : 3 * width + 8, :]


def call(body, operands, outs, scratch=(), flops=0, moved=0, exps=0):
    vmem = pl.BlockSpec(memory_space=pltpu.VMEM)
    return pl.pallas_call(
        body,
        out_shape=outs,
        in_specs=[pl.BlockSpec(memory_space=pltpu.SMEM)] + [vmem] * (len(operands) - 1),
        out_specs=jax.tree.map(lambda _: vmem, outs),
        scratch_shapes=list(scratch),
        compiler_params=pltpu.CompilerParams(vmem_limit_bytes=56 * 2**20),
        cost_estimate=pl.CostEstimate(flops=flops, bytes_accessed=moved, transcendentals=exps),
    )(*operands)


def shape(dims, dtype):
    return jax.ShapeDtypeStruct(dims, dtype)


def exchange(value, axis, total, mask):
    return lax.ppermute(value, axis, [(member, member ^ mask) for member in range(total)])


def gather_group(value, total):
    held = [value]
    pieces = {0: value}
    bit = total // 2
    while bit:
        for known in sorted(pieces):
            pieces[known | bit] = exchange(pieces[known], "fsdp", total, bit)
        bit //= 2
    return [pieces[part] for part in range(total)]


def sum_over_replicas(low, high, total):
    mask = 1
    while True:
        arrived = exchange(high, "rep", total, mask)
        summed = (low.astype(F32) + arrived.astype(F32)).astype(BF16)
        mask *= 2
        count = summed.shape[0]
        if count == 1:
            break
        low, high = summed[: count // 2], summed[count // 2 :]
    held = summed
    mask = total // 2
    while True:
        arrived = exchange(held, "rep", total, mask)
        mask //= 2
        if mask == 0:
            return held, arrived
        held = jnp.concatenate([held, arrived], axis=0)


def on_device(n_rep, n_shard, tokens, positions, seq_count, w_query, w_keyval, w_out, w_gateup, w_down, gain_attn,
              gain_mlp, out_grad):
    row_count, model = tokens.shape
    width = w_query.shape[1]
    ff = w_gateup.shape[2] // 2
    kv_width = w_keyval.shape[2]
    group_rows = n_shard * row_count
    shard = lax.axis_index("fsdp").astype(jnp.int32)
    member = lax.axis_index("rep").astype(jnp.int32)
    idx = jnp.stack([shard, member])
    live = (jnp.arange(row_count, dtype=jnp.int32) // LEN < seq_count[0]).astype(F32)[:, None]
    cotangent = (out_grad.astype(F32) * live).astype(BF16)
    codes = jnp.stack([positions // 64, positions % 64]).astype(BF16)
    small = jnp.concatenate(
        [
            jnp.pad(codes, ((0, 0), (0, 256 - row_count))),
            jnp.pad(jnp.concatenate([gain_attn, gain_mlp], axis=0), ((0, 0), (0, 256 - width))),
            jnp.zeros((12, 256), BF16),
        ],
        axis=0,
    )
    tok = gather_group(tokens, n_shard)
    small = gather_group(small, n_shard)
    wq = gather_group(w_query[0], n_shard)
    wkv = gather_group(w_keyval[0], n_shard)
    wo = gather_group(w_out[0], n_shard)
    wgu = gather_group(w_gateup[0], n_shard)
    cot = gather_group(cotangent, n_shard)
    wd = gather_group(w_down[0], n_shard)
    (x_all, normed, query, keyval, mixed, mid, normed_mid, cosine, sine, gains, wq_full, wkv_full, wo_full) = call(
        functools.partial(attn_forward_kernel, n_shard),
        [idx] + tok + small + wq + wkv + wo,
        (
            shape((group_rows, model), BF16),
            shape((group_rows, model), BF16),
            shape((group_rows, QW), BF16),
            shape((group_rows, kv_width), BF16),
            shape((group_rows, QW), BF16),
            shape((group_rows, model), F32),
            shape((group_rows, model), BF16),
            shape((group_rows, 128), F32),
            shape((group_rows, 128), F32),
            shape((16, model), F32),
            shape((model, QW), BF16),
            shape((model, kv_width), BF16),
            shape((QW, model), BF16),
        ),
        flops=2 * group_rows * model * (2 * model + kv_width + 2 * 256),
        moved=8 * 2**20,
        exps=group_rows * 128 * HEADS,
    )
    middle = n_rep // 2
    groups = max(1, n_rep // (2 * n_shard))
    gu_slab = (width // groups, ff // n_shard)
    down_slab = (w_down.shape[1] // n_rep, model)
    a_rows = 3 * width + 16
    a_slab = (a_rows // n_rep, model)
    out_act, d_normed_mid, down_lo, down_hi, gu_lo, gu_hi, dcot = call(
        functools.partial(mlp_kernel, n_shard, n_rep),
        [idx, normed_mid, mid[:row_count], live] + cot + wgu + wd,
        (
            shape((row_count, model), F32),
            shape((group_rows, model), F32),
            shape((middle,) + down_slab, BF16),
            shape((middle,) + down_slab, BF16),
            shape((middle,) + gu_slab, BF16),
            shape((middle,) + gu_slab, BF16),
            shape((group_rows, model), BF16),
        ),
        [
            pltpu.VMEM((model, 2 * ff), BF16),
            pltpu.VMEM((n_rep,) + down_slab, BF16),
            pltpu.VMEM((n_rep,) + gu_slab, BF16),
        ],
        flops=2 * group_rows * model * 10 * ff // 2,
        moved=12 * 2**20,
        exps=group_rows * ff,
    )
    down = sum_over_replicas(down_lo, down_hi, n_rep)
    gateup = sum_over_replicas(gu_lo, gu_hi, n_rep)
    in_grad, a_lo, a_hi = call(
        functools.partial(attn_backward_kernel, n_shard, n_rep),
        [idx, x_all, normed, query, keyval, mixed, mid, cosine, sine, gains, wq_full, wkv_full, wo_full,
         d_normed_mid, dcot],
        (
            shape((row_count, model), F32),
            shape((middle,) + a_slab, BF16),
            shape((middle,) + a_slab, BF16),
        ),
        [
            pltpu.VMEM((group_rows, model), BF16),
            pltpu.VMEM((group_rows, QW), BF16),
            pltpu.VMEM((group_rows, kv_width), BF16),
            pltpu.VMEM((a_rows, model), F32),
        ],
        flops=2 * group_rows * model * (3 * model + 2 * kv_width),
        moved=8 * 2**20,
        exps=group_rows * 128 * HEADS,
    )
    attn = sum_over_replicas(a_lo, a_hi, n_rep)
    grad_down = call(
        functools.partial(unpack_down_kernel, n_rep),
        [idx] + list(down),
        shape((w_down.shape[1], model), F32),
        moved=2 * 2**20,
    )
    grad_gateup = call(
        functools.partial(unpack_gateup_kernel, n_rep),
        [idx] + list(gateup),
        shape((width, 2 * ff), F32),
        moved=3 * 2**20,
    )
    grad_query, grad_keyval, grad_out, gain_rows = call(
        functools.partial(unpack_attn_kernel, n_rep),
        [idx] + list(attn),
        (
            shape((width, model), F32),
            shape((width, kv_width), F32),
            shape((width, model), F32),
            shape((8, model), F32),
        ),
        [pltpu.VMEM((a_rows, model), F32)],
        moved=2 * 2**20,
    )
    own_gains = lax.dynamic_slice(gain_rows, (0, shard * width), (2, width))
    return (
        out_act,
        in_grad,
        grad_query[None],
        grad_keyval[None],
        grad_out[None],
        grad_gateup[None],
        grad_down[None],
        own_gains[:1],
        own_gains[1:],
    )


def solution(mesh):
    placed = (
        P(("rep", "fsdp"), None),
        P(("rep", "fsdp")),
        P(("rep", "fsdp")),
        P(None, "fsdp", None),
        P(None, "fsdp", None),
        P(None, "fsdp", None),
        P(None, "fsdp", None),
        P(None, "fsdp", None),
        P(None, "fsdp"),
        P(None, "fsdp"),
        P(("rep", "fsdp"), None),
    )
    return jax.shard_map(
        functools.partial(on_device, mesh.shape["rep"], mesh.shape["fsdp"]),
        mesh=mesh,
        in_specs=placed,
        out_specs=(
            P(("rep", "fsdp"), None),
            P(("rep", "fsdp"), None),
            P(None, "fsdp", None),
            P(None, "fsdp", None),
            P(None, "fsdp", None),
            P(None, "fsdp", None),
            P(None, "fsdp", None),
            P(None, "fsdp"),
            P(None, "fsdp"),
        ),
        check_vma=False,
    )
```

time: 434 us -> 198 us (0.46)
  blocking collectives: 187 us -> 0 us
  waiting for transfers between devices: 172 us -> 81.1 us
  Pallas kernels: 0 us -> 53.8 us
  starting transfers between devices: 0.55 us -> 40.2 us
  matrix products: 24.8 us -> 0 us
  between operations: 15.8 us -> 1.75 us
  local copies, waits for them, and re-layouts: 25.4 us -> 15 us
    psum x1 -> x0, blocking collectives: 147 us -> none  [on_device(): stacked = lax.psum(shared, 'rep')]
    reduce_scatter x4 -> x0, waiting for transfers between devices: 116 us -> none  [on_device(): lax.psum_scatter(shortened(stacked), 'fsdp', scatter_dimension=1, tiled=T...]
    ppermute x0 -> x42, waiting for transfers between devices: none -> 81.1 us  [exchange(): lax.ppermute(value, axis, [(member, member ^ mask) for member in range(to...]
    pallas_call x0 -> x6, Pallas kernels: none -> 53.8 us  [call(): pl.pallas_call(body, out_shape=outs, in_specs=[pl.BlockSpec(memory_space=...]
    unnamed x12 -> x0, waiting for transfers between devices: 51.2 us -> none
    ppermute x0 -> x42, starting transfers between devices: none -> 40.2 us  [exchange(): lax.ppermute(value, axis, [(member, member ^ mask) for member in range(to...]
    all_gather x3 -> x0, blocking collectives: 30.8 us -> none  [the longest x1 12.8 us: on_device(): lax.all_gather(w_query, 'fsdp', axis=1, tiled=True)]
    dot_general x21 -> x0, matrix products: 24.8 us -> none  [the longest x1 4.11 us: forward_layer(): gateup = jnp.dot(normed_mid, w_gateup, preferred_element_type=jnp.float32)]
  transfers between devices with their start and end apart: 9 -> 42, of which waited for: 7 -> 20; matrix products, arithmetic and copies ran while one was open for 10% -> 8% of each run, Pallas kernels for 0% -> 19%
where the time goes in v1:
time: 198 us; the launch traced here: 197 us
  waiting for transfers between devices  81.1 us (41%)
  Pallas kernels  53.8 us (27%)
  starting transfers between devices  40.2 us (20%)
  local copies, waits for them, and re-layouts  15 us (8%)
  other arithmetic  5.43 us (3%)
    ppermute x42, waiting for transfers between devices, exchange(): lax.ppermute(value, axis, [(member, member ^ mask) for member in range(to...  81.1 us
    pallas_call x6, Pallas kernels, call(): pl.pallas_call(body, out_shape=outs, in_specs=[pl.BlockSpec(memory_space=...  53.8 us
    ppermute x42, starting transfers between devices, exchange(): lax.ppermute(value, axis, [(member, member ^ mask) for member in range(to...  40.2 us
    unnamed x66, local copies, waits for them, and re-layouts  11.7 us
  transfers between devices with their start and end apart: 42, of which 20 were waited for; matrix products, arithmetic and copies ran while one was open for 8% of the time, Pallas kernels for 19%

profile of v1, /device:TPU:0, one launch (start us, length us, event | category | flops | bytes accessed | tf_op | source)
XLA Modules:
  0.0 197.2 jit_solution(16494990771173716562)
XLA Ops:
  0.7 3.0 %collective-permute-start.19 = (bf16[144,3072]{1,0:T(8,128)(2,1)}, bf16[144,3072]{1,0:T(8,128)(2,1)S(1)}, u32[]{:S(2)}, u32[]{:S(2)}) collective-permute-start(bf16[144,3072]{1,0:T(8,128)(2,1)} %bitcast.24), channel_id=1, source_target_pairs={{0,2},{1,3},{2,0},{3,1},{4,6},{5,7},{6,4},{7,5},{8,10},{9,11},{10,... | collective-permute-start | bytes 2654216 | tf_op jit(solution)/shard_map/ppermute | solution.py:430
  6.4 2.0 %collective-permute-start.1 = (bf16[128,576]{1,0:T(8,128)(2,1)S(1)}, bf16[128,576]{1,0:T(8,128)(2,1)S(1)}, u32[]{:S(2)}, u32[]{:S(2)}) collective-permute-start(bf16[128,576]{1,0:T(8,128)(2,1)S(1)} %copy.22.refs_0_), channel_id=1, source_target_pairs={{0,2},{1,3},{2,0},{3,1},{4,6},{5,7},{6,4},{7,5},{8,10},{9,11},{10,... | collective-permute-start | bytes 442376 | tf_op jit(solution)/shard_map/ppermute | solution.py:430
  9.3 15.3 %collective-permute-done.4.refs_6_ = bf16[16,256]{1,0:T(8,128)(2,1)S(1)} collective-permute-done((bf16[16,256]{1,0:T(8,128)(2,1)S(1)}, bf16[16,256]{1,0:T(8,128)(2,1)S(1)}, u32[]{:S(2)}, u32[]{:S(2)}) %collective-permute-start.4) | collective-permute-done | bytes 8224 | tf_op jit(solution)/shard_map/ppermute | solution.py:430
  25.6 2.1 %collective-permute-start.10 = (bf16[144,384]{1,0:T(8,128)(2,1)}, bf16[144,384]{1,0:T(8,128)(2,1)S(1)}, u32[]{:S(2)}, u32[]{:S(2)}) collective-permute-start(bf16[144,384]{1,0:T(8,128)(2,1)} %bitcast.36), channel_id=1, source_target_pairs={{0,2},{1,3},{2,0},{3,1},{4,6},{5,7},{6,4},{7,5},{8,10},{9,11},{10,... | collective-permute-start | bytes 331784 | tf_op jit(solution)/shard_map/ppermute | solution.py:430
  28.1 3.6 %collective-permute-done.10.refs_14_ = bf16[144,384]{1,0:T(8,128)(2,1)S(1)} collective-permute-done((bf16[144,384]{1,0:T(8,128)(2,1)}, bf16[144,384]{1,0:T(8,128)(2,1)S(1)}, u32[]{:S(2)}, u32[]{:S(2)}) %collective-permute-start.10) | collective-permute-done | bytes 110624 | tf_op jit(solution)/shard_map/ppermute | solution.py:430
  31.7 1.7 collective-permute-start.16
  36.9 1.7 collective-permute-done.16.refs_5_
  38.6 1.9 collective-permute-start.22
  42.6 3.9 %collective-permute-done.7.refs_10_ = bf16[144,576]{1,0:T(8,128)(2,1)} collective-permute-done((bf16[144,576]{1,0:T(8,128)(2,1)}, bf16[144,576]{1,0:T(8,128)(2,1)}, u32[]{:S(2)}, u32[]{:S(2)}) %collective-permute-start.7) | collective-permute-done | bytes 165920 | tf_op jit(solution)/shard_map/ppermute | solution.py:430
  50.0 6.3 %collective-permute-done.22.refs_13_ = bf16[384,576]{1,0:T(8,128)(2,1)} collective-permute-done((bf16[384,576]{1,0:T(8,128)(2,1)S(1)}, bf16[384,576]{1,0:T(8,128)(2,1)}, u32[]{:S(2)}, u32[]{:S(2)}) %collective-permute-start.22) | collective-permute-done | bytes 442400 | tf_op jit(solution)/shard_map/ppermute | solution.py:430
  59.9 12.4 %shard_map.178 = (bf16[512,576]{1,0:T(8,128)(2,1)}, bf16[512,576]{1,0:T(8,128)(2,1)}, bf16[512,640]{1,0:T(8,128)(2,1)}, bf16[512,384]{1,0:T(8,128)(2,1)}, bf16[5...) custom-call(s32[2]{0:T(128)} %pad_add_fusion.idx, ...), custom_call_target="tpu_custom_call" | custom-call | flops 1207959552 | bytes 8388608 | tf_op jit(solution)/shard_map/pallas_call | solution.py:414
  72.3 1.7 slice.45.refs_1_
  75.0 14.6 %shard_map.179 = (f32[128,576]{1,0:T(8,128)}, f32[512,576]{1,0:T(8,128)}, bf16[4,48,576]{2,1,0:T(8,128)(2,1)}, bf16[4,48,576]{2,1,0:T(8,128)(2,1)}, bf16[4,144,3...) custom-call(s32[2]{0:T(128)} %pad_add_fusion.idx, ...), custom_call_target="tpu_custom_call" | custom-call | flops 4529848320 | bytes 12582912 | tf_op jit(solution)/shard_map/pallas_call | solution.py:414
  91.2 6.6 %collective-permute-done.36 = bf16[4,48,576]{2,1,0:T(8,128)(2,1)S(1)} collective-permute-done((bf16[4,48,576]{2,1,0:T(8,128)(2,1)}, bf16[4,48,576]{2,1,0:T(8,128)(2,1)S(1)}, u32[]{:S(2)}, u32[]{:S(2)}) %collective-permute-start.36) | collective-permute-done | bytes 221216 | tf_op jit(solution)/shard_map/ppermute | solution.py:430
  100.6 19.8 %shard_map.180 = (f32[128,576]{1,0:T(8,128)}, bf16[4,56,576]{2,1,0:T(8,128)(2,1)}, bf16[4,56,576]{2,1,0:T(8,128)(2,1)}) custom-call(s32[2]{0:T(128)} %pad_add_fusion.idx, bf16[512,576]{1,0:T(8,128)(2,1)} %get-tuple-element.39.x_ref, bf16[512,576]{1,0:T(8,128)(2,1)} %get-tuple-element.40.nrm_ref, bf16[512,640]{1,0:T(8,128)(2,1)} %get-tuple-element.41.q_ref, ...), custom_call_target="tpu_custom_call" | custom-call | flops 1472200704 | bytes 8388608 | tf_op jit(solution)/shard_map/pallas_call | solution.py:414
  122.5 2.7 %collective-permute-start.38 = (bf16[1,48,576]{2,1,0:T(8,128)(2,1)S(1)}, bf16[1,48,576]{2,1,0:T(8,128)(2,1)S(1)}, u32[]{:S(2)}, u32[]{:S(2)}) collective-permute-start(bf16[1,48,576]{2,1,0:T(8,128)(2,1)S(1)} %slice.71), channel_id=1, source_target_pairs={{0,16},{4,20},{8,24},{12,28},{16,0},{20,4},{24,8},{28,12},{1,17},{... | collective-permute-start | bytes 165896 | tf_op jit(solution)/shard_map/ppermute | solution.py:430
  125.2 5.2 %collective-permute-done.24 = bf16[4,56,576]{2,1,0:T(8,128)(2,1)S(1)} collective-permute-done((bf16[4,56,576]{2,1,0:T(8,128)(2,1)}, bf16[4,56,576]{2,1,0:T(8,128)(2,1)S(1)}, u32[]{:S(2)}, u32[]{:S(2)}) %collective-permute-start.24) | collective-permute-done | bytes 258080 | tf_op jit(solution)/shard_map/ppermute | solution.py:430
  132.0 2.7 %collective-permute-start.39 = (bf16[1,48,576]{2,1,0:T(8,128)(2,1)S(1)}, bf16[1,48,576]{2,1,0:T(8,128)(2,1)S(1)}, u32[]{:S(2)}, u32[]{:S(2)}) collective-permute-start(bf16[1,48,576]{2,1,0:T(8,128)(2,1)S(1)} %add_convert_fusion.8), channel_id=1, source_target_pairs={{0,16},{4,20},{8,24},{12,28},{16,0},{20,4},{24,8},{28,12},{1,17},{... | collective-permute-start | bytes 165896 | tf_op jit(solution)/shard_map/ppermute | solution.py:430
  134.7 3.2 %collective-permute-done.30 = bf16[4,144,384]{2,1,0:T(8,128)(2,1)S(1)} collective-permute-done((bf16[4,144,384]{2,1,0:T(8,128)(2,1)S(1)}, bf16[4,144,384]{2,1,0:T(8,128)(2,1)S(1)}, u32[]{:S(2)}, u32[]{:S(2)}) %collective-permute-start.30) | collective-permute-done | bytes 442400 | tf_op jit(solution)/shard_map/ppermute | solution.py:430
  138.6 2.7 %collective-permute-start.26 = (bf16[1,56,576]{2,1,0:T(8,128)(2,1)S(1)}, bf16[1,56,576]{2,1,0:T(8,128)(2,1)S(1)}, u32[]{:S(2)}, u32[]{:S(2)}) collective-permute-start(bf16[1,56,576]{2,1,0:T(8,128)(2,1)S(1)} %slice.63), channel_id=1, source_target_pairs={{0,16},{4,20},{8,24},{12,28},{16,0},{20,4},{24,8},{28,12},{1,17},{... | collective-permute-start | bytes 193544 | tf_op jit(solution)/shard_map/ppermute | solution.py:430
  141.3 3.8 %collective-permute-done.31 = bf16[2,144,384]{2,1,0:T(8,128)(2,1)S(1)} collective-permute-done((bf16[2,144,384]{2,1,0:T(8,128)(2,1)S(1)}, bf16[2,144,384]{2,1,0:T(8,128)(2,1)S(1)}, u32[]{:S(2)}, u32[]{:S(2)}) %collective-permute-start.31) | collective-permute-done | bytes 221216 | tf_op jit(solution)/shard_map/ppermute | solution.py:430
  145.2 3.1 %collective-permute-start.32 = (bf16[1,144,384]{2,1,0:T(8,128)(2,1)S(1)}, bf16[1,144,384]{2,1,0:T(8,128)(2,1)S(1)}, u32[]{:S(2)}, u32[]{:S(2)}) collective-permute-start(bf16[1,144,384]{2,1,0:T(8,128)(2,1)S(1)} %slice.67), channel_id=1, source_target_pairs={{0,16},{4,20},{8,24},{12,28},{16,0},{20,4},{24,8},{28,12},{1,17},{... | collective-permute-start | bytes 331784 | tf_op jit(solution)/shard_map/ppermute | solution.py:430
  148.4 5.2 %collective-permute-done.32 = bf16[1,144,384]{2,1,0:T(8,128)(2,1)S(1)} collective-permute-done((bf16[1,144,384]{2,1,0:T(8,128)(2,1)S(1)}, bf16[1,144,384]{2,1,0:T(8,128)(2,1)S(1)}, u32[]{:S(2)}, u32[]{:S(2)}) %collective-permute-start.32) | collective-permute-done | bytes 110624 | tf_op jit(solution)/shard_map/ppermute | solution.py:430
  154.0 1.9 collective-permute-done.27
  156.1 3.2 %collective-permute-done.33 = bf16[1,144,384]{2,1,0:T(8,128)(2,1)S(1)} collective-permute-done((bf16[1,144,384]{2,1,0:T(8,128)(2,1)S(1)}, bf16[1,144,384]{2,1,0:T(8,128)(2,1)S(1)}, u32[]{:S(2)}, u32[]{:S(2)}) %collective-permute-start.33) | collective-permute-done | bytes 110624 | tf_op jit(solution)/shard_map/ppermute | solution.py:430
  159.4 2.1 %collective-permute-start.40 = (bf16[2,48,576]{2,1,0:T(8,128)(2,1)S(1)}, bf16[2,48,576]{2,1,0:T(8,128)(2,1)S(1)}, u32[]{:S(2)}, u32[]{:S(2)}) collective-permute-start(bf16[2,48,576]{2,1,0:T(8,128)(2,1)S(1)} %pad_maximum_fusion.5), channel_id=1, source_target_pairs={{0,8},{4,12},{8,0},{12,4},{16,24},{20,28},{24,16},{28,20},{1,9},{5... | collective-permute-start | bytes 331784 | tf_op jit(solution)/shard_map/ppermute | solution.py:430
  164.3 2.9 %collective-permute-done.34 = bf16[2,144,384]{2,1,0:T(8,128)(2,1)S(1)} collective-permute-done((bf16[2,144,384]{2,1,0:T(8,128)(2,1)S(1)}, bf16[2,144,384]{2,1,0:T(8,128)(2,1)S(1)}, u32[]{:S(2)}, u32[]{:S(2)}) %collective-permute-start.34) | collective-permute-done | bytes 221216 | tf_op jit(solution)/shard_map/ppermute | solution.py:430
  171.8 12.4 %collective-permute-done.41.second = bf16[4,48,576]{2,1,0:T(8,128)(2,1)S(1)} collective-permute-done((bf16[4,48,576]{2,1,0:T(8,128)(2,1)S(1)}, bf16[4,48,576]{2,1,0:T(8,128)(2,1)S(1)}, u32[]{:S(2)}, u32[]{:S(2)}) %collective-permute-start.41) | collective-permute-done | bytes 221216 | tf_op jit(solution)/shard_map/ppermute | solution.py:430
  184.9 2.2 %shard_map.183 = f32[384,576]{1,0:T(8,128)} custom-call(s32[2]{0:T(128)} %pad_add_fusion.idx, bf16[4,48,576]{2,1,0:T(8,128)(2,1)} %copy-done.2, bf16[4,48,576]{2,1,0:T(8,128)(2,1)} %copy-done.9), custom_call_target="tpu_custom_call" | custom-call | bytes 2097152 | tf_op jit(solution)/shard_map/pallas_call | solution.py:414
  187.1 2.4 %copy.27 = f32[1,384,576]{1,2,0:T(8,128)} copy(f32[1,384,576]{2,1,0:T(8,128)} %bitcast.19) | data formatting | bytes 1769472
  190.2 2.2 %shard_map.181 = (f32[144,576]{1,0:T(8,128)}, f32[144,384]{1,0:T(8,128)}, f32[144,576]{1,0:T(8,128)}, f32[8,576]{1,0:T(8,128)}) custom-call(s32[2]{0:T(128)} %pad_add_fusion.idx, bf16[4,56,576]{2,1,0:T(8,128)(2,1)} %copy-done.1, bf16[4,56,576]{2,1,0:T(8,128)(2,1)} %copy-done.8), custom_call_target="tpu_custom_call" | custom-call | bytes 2097152 | tf_op jit(solution)/shard_map/pallas_call | solution.py:414
  194.6 2.6 %shard_map.182 = f32[144,3072]{1,0:T(8,128)} custom-call(s32[2]{0:T(128)} %pad_add_fusion.idx, bf16[4,144,384]{2,1,0:T(8,128)(2,1)} %copy-done, bf16[4,144,384]{2,1,0:T(8,128)(2,1)} %copy-done.5), custom_call_target="tpu_custom_call" | custom-call | bytes 3145728 | tf_op jit(solution)/shard_map/pallas_call | solution.py:414
  (156 shorter events, 38.2 us)
Async XLA Ops:
  0.7 40.0 %collective-permute-start.19 = (bf16[144,3072]{1,0:T(8,128)(2,1)}, bf16[144,3072]{1,0:T(8,128)(2,1)S(1)}, u32[]{:S(2)}, u32[]{:S(2)}) collective-permute-start(bf16[144,3072]{1,0:T(8,128)(2,1)} %bitcast.24), channel_id=1, source_target_pairs={{0,2},{1,3},{2,0},{3,1},{4,6},{5,7},{6,4},{7,5},{8,10},{9,11},{10,... | collective-permute-start | bytes 2654216 | tf_op jit(solution)/shard_map/ppermute | solution.py:430
  5.2 19.3 %collective-permute-start.4 = (bf16[16,256]{1,0:T(8,128)(2,1)S(1)}, bf16[16,256]{1,0:T(8,128)(2,1)S(1)}, u32[]{:S(2)}, u32[]{:S(2)}) collective-permute-start(bf16[16,256]{1,0:T(8,128)(2,1)S(1)} %maximum_maximum_fusion.refs_4_), channel_id=1, source_target_pairs={{0,2},{1,3},{2,0},{3,1},{4,6},{5,7},{6,4},{7,5},{8,10},{9,11},{10,... | collective-permute-start | bytes 24584 | tf_op jit(solution)/shard_map/ppermute | solution.py:430
  5.3 20.3 %collective-permute-start.3 = (bf16[16,256]{1,0:T(8,128)(2,1)S(1)}, bf16[16,256]{1,0:T(8,128)(2,1)S(1)}, u32[]{:S(2)}, u32[]{:S(2)}) collective-permute-start(bf16[16,256]{1,0:T(8,128)(2,1)S(1)} %maximum_maximum_fusion.refs_4_), channel_id=1, source_target_pairs={{0,1},{1,0},{2,3},{3,2},{4,5},{5,4},{6,7},{7,6},{8,9},{9,8},{10,11... | collective-permute-start | bytes 24584 | tf_op jit(solution)/shard_map/ppermute | solution.py:430
  6.4 27.1 %collective-permute-start.1 = (bf16[128,576]{1,0:T(8,128)(2,1)S(1)}, bf16[128,576]{1,0:T(8,128)(2,1)S(1)}, u32[]{:S(2)}, u32[]{:S(2)}) collective-permute-start(bf16[128,576]{1,0:T(8,128)(2,1)S(1)} %copy.22.refs_0_), channel_id=1, source_target_pairs={{0,2},{1,3},{2,0},{3,1},{4,6},{5,7},{6,4},{7,5},{8,10},{9,11},{10,... | collective-permute-start | bytes 442376 | tf_op jit(solution)/shard_map/ppermute | solution.py:430
  8.4 25.4 %collective-permute-start = (bf16[128,576]{1,0:T(8,128)(2,1)S(1)}, bf16[128,576]{1,0:T(8,128)(2,1)S(1)}, u32[]{:S(2)}, u32[]{:S(2)}) collective-permute-start(bf16[128,576]{1,0:T(8,128)(2,1)S(1)} %copy.22.refs_0_), channel_id=1, source_target_pairs={{0,1},{1,0},{2,3},{3,2},{4,5},{5,4},{6,7},{7,6},{8,9},{9,8},{10,11... | collective-permute-start | bytes 442376 | tf_op jit(solution)/shard_map/ppermute | solution.py:430
  31.7 6.9 %collective-permute-start.16 = (bf16[128,576]{1,0:T(8,128)(2,1)S(1)}, bf16[128,576]{1,0:T(8,128)(2,1)S(1)}, u32[]{:S(2)}, u32[]{:S(2)}) collective-permute-start(bf16[128,576]{1,0:T(8,128)(2,1)S(1)} %multiply_convert_fusion.refs_3_), channel_id=1, source_target_pairs={{0,2},{1,3},{2,0},{3,1},{4,6},{5,7},{6,4},{7,5},{8,10},{9,11},{10,... | collective-permute-start | bytes 442376 | tf_op jit(solution)/shard_map/ppermute | solution.py:430
  33.4 7.1 %collective-permute-start.15 = (bf16[128,576]{1,0:T(8,128)(2,1)S(1)}, bf16[128,576]{1,0:T(8,128)(2,1)}, u32[]{:S(2)}, u32[]{:S(2)}) collective-permute-start(bf16[128,576]{1,0:T(8,128)(2,1)S(1)} %multiply_convert_fusion.refs_3_), channel_id=1, source_target_pairs={{0,1},{1,0},{2,3},{3,2},{4,5},{5,4},{6,7},{7,6},{8,9},{9,8},{10,11... | collective-permute-start | bytes 442376 | tf_op jit(solution)/shard_map/ppermute | solution.py:430
  33.5 9.2 %collective-permute-start.13 = (bf16[144,576]{1,0:T(8,128)(2,1)}, bf16[144,576]{1,0:T(8,128)(2,1)}, u32[]{:S(2)}, u32[]{:S(2)}) collective-permute-start(bf16[144,576]{1,0:T(8,128)(2,1)} %bitcast.33), channel_id=1, source_target_pairs={{0,2},{1,3},{2,0},{3,1},{4,6},{5,7},{6,4},{7,5},{8,10},{9,11},{10,... | collective-permute-start | bytes 497672 | tf_op jit(solution)/shard_map/ppermute | solution.py:430
  34.1 12.5 %collective-permute-start.7 = (bf16[144,576]{1,0:T(8,128)(2,1)}, bf16[144,576]{1,0:T(8,128)(2,1)}, u32[]{:S(2)}, u32[]{:S(2)}) collective-permute-start(bf16[144,576]{1,0:T(8,128)(2,1)} %bitcast.30), channel_id=1, source_target_pairs={{0,2},{1,3},{2,0},{3,1},{4,6},{5,7},{6,4},{7,5},{8,10},{9,11},{10,... | collective-permute-start | bytes 497672 | tf_op jit(solution)/shard_map/ppermute | solution.py:430
  38.6 17.7 %collective-permute-start.22 = (bf16[384,576]{1,0:T(8,128)(2,1)S(1)}, bf16[384,576]{1,0:T(8,128)(2,1)}, u32[]{:S(2)}, u32[]{:S(2)}) collective-permute-start(bf16[384,576]{1,0:T(8,128)(2,1)S(1)} %bitcast.21), channel_id=1, source_target_pairs={{0,2},{1,3},{2,0},{3,1},{4,6},{5,7},{6,4},{7,5},{8,10},{9,11},{10,... | collective-permute-start | bytes 1327112 | tf_op jit(solution)/shard_map/ppermute | solution.py:430
  40.5 33.5 %collective-permute-start.18 = (bf16[144,3072]{1,0:T(8,128)(2,1)S(1)}, bf16[144,3072]{1,0:T(8,128)(2,1)S(1)}, u32[]{:S(2)}, u32[]{:S(2)}) collective-permute-start(bf16[144,3072]{1,0:T(8,128)(2,1)S(1)} %bitcast.26), channel_id=1, source_target_pairs={{0,1},{1,0},{2,3},{3,2},{4,5},{5,4},{6,7},{7,6},{8,9},{9,8},{10,11... | collective-permute-start | bytes 2654216 | tf_op jit(solution)/shard_map/ppermute | solution.py:430
  40.6 33.5 %collective-permute-start.20 = (bf16[144,3072]{1,0:T(8,128)(2,1)S(1)}, bf16[144,3072]{1,0:T(8,128)(2,1)}, u32[]{:S(2)}, u32[]{:S(2)}) collective-permute-start(bf16[144,3072]{1,0:T(8,128)(2,1)S(1)} %collective-permute-done.19.refs_9_), channel_id=1, source_target_pairs={{0,1},{1,0},{2,3},{3,2},{4,5},{5,4},{6,7},{7,6},{8,9},{9,8},{10,11... | collective-permute-start | bytes 2654216 | tf_op jit(solution)/shard_map/ppermute | solution.py:430
  48.5 7.7 %collective-permute-start.14 = (bf16[144,576]{1,0:T(8,128)(2,1)}, bf16[144,576]{1,0:T(8,128)(2,1)S(1)}, u32[]{:S(2)}, u32[]{:S(2)}) collective-permute-start(bf16[144,576]{1,0:T(8,128)(2,1)} %collective-permute-done.13.refs_18_), channel_id=1, source_target_pairs={{0,1},{1,0},{2,3},{3,2},{4,5},{5,4},{6,7},{7,6},{8,9},{9,8},{10,11... | collective-permute-start | bytes 497672 | tf_op jit(solution)/shard_map/ppermute | solution.py:430
  49.8 24.2 %collective-permute-start.21 = (bf16[384,576]{1,0:T(8,128)(2,1)S(1)}, bf16[384,576]{1,0:T(8,128)(2,1)}, u32[]{:S(2)}, u32[]{:S(2)}) collective-permute-start(bf16[384,576]{1,0:T(8,128)(2,1)S(1)} %bitcast.22), channel_id=1, source_target_pairs={{0,1},{1,0},{2,3},{3,2},{4,5},{5,4},{6,7},{7,6},{8,9},{9,8},{10,11... | collective-permute-start | bytes 1327112 | tf_op jit(solution)/shard_map/ppermute | solution.py:430
  56.2 17.8 %collective-permute-start.23 = (bf16[384,576]{1,0:T(8,128)(2,1)}, bf16[384,576]{1,0:T(8,128)(2,1)}, u32[]{:S(2)}, u32[]{:S(2)}) collective-permute-start(bf16[384,576]{1,0:T(8,128)(2,1)} %collective-permute-done.22.refs_13_), channel_id=1, source_target_pairs={{0,1},{1,0},{2,3},{3,2},{4,5},{5,4},{6,7},{7,6},{8,9},{9,8},{10,11... | collective-permute-start | bytes 1327112 | tf_op jit(solution)/shard_map/ppermute | solution.py:430
  58.8 15.2 %collective-permute-start.17 = (bf16[128,576]{1,0:T(8,128)(2,1)}, bf16[128,576]{1,0:T(8,128)(2,1)S(1)}, u32[]{:S(2)}, u32[]{:S(2)}) collective-permute-start(bf16[128,576]{1,0:T(8,128)(2,1)} %copy-done.20), channel_id=1, source_target_pairs={{0,1},{1,0},{2,3},{3,2},{4,5},{5,4},{6,7},{7,6},{8,9},{9,8},{10,11... | collective-permute-start | bytes 442376 | tf_op jit(solution)/shard_map/ppermute | solution.py:430
  89.6 8.2 %collective-permute-start.36 = (bf16[4,48,576]{2,1,0:T(8,128)(2,1)}, bf16[4,48,576]{2,1,0:T(8,128)(2,1)S(1)}, u32[]{:S(2)}, u32[]{:S(2)}) collective-permute-start(bf16[4,48,576]{2,1,0:T(8,128)(2,1)} %get-tuple-element.61), channel_id=1, source_target_pairs={{0,4},{4,0},{8,12},{12,8},{16,20},{20,16},{24,28},{28,24},{1,5},{5... | collective-permute-start | bytes 663560 | tf_op jit(solution)/shard_map/ppermute | solution.py:430
  98.9 23.6 %collective-permute-start.37 = (bf16[2,48,576]{2,1,0:T(8,128)(2,1)S(1)}, bf16[2,48,576]{2,1,0:T(8,128)(2,1)S(1)}, u32[]{:S(2)}, u32[]{:S(2)}) collective-permute-start(bf16[2,48,576]{2,1,0:T(8,128)(2,1)S(1)} %slice.69), channel_id=1, source_target_pairs={{0,8},{4,12},{8,0},{12,4},{16,24},{20,28},{24,16},{28,20},{1,9},{5... | collective-permute-start | bytes 331784 | tf_op jit(solution)/shard_map/ppermute | solution.py:430
  120.4 10.0 %collective-permute-start.24 = (bf16[4,56,576]{2,1,0:T(8,128)(2,1)}, bf16[4,56,576]{2,1,0:T(8,128)(2,1)S(1)}, u32[]{:S(2)}, u32[]{:S(2)}) collective-permute-start(bf16[4,56,576]{2,1,0:T(8,128)(2,1)} %get-tuple-element.54), channel_id=1, source_target_pairs={{0,4},{4,0},{8,12},{12,8},{16,20},{20,16},{24,28},{28,24},{1,5},{5... | collective-permute-start | bytes 774152 | tf_op jit(solution)/shard_map/ppermute | solution.py:430
  122.0 15.9 %collective-permute-start.30 = (bf16[4,144,384]{2,1,0:T(8,128)(2,1)S(1)}, bf16[4,144,384]{2,1,0:T(8,128)(2,1)S(1)}, u32[]{:S(2)}, u32[]{:S(2)}) collective-permute-start(bf16[4,144,384]{2,1,0:T(8,128)(2,1)S(1)} %copy-done.16), channel_id=1, source_target_pairs={{0,4},{4,0},{8,12},{12,8},{16,20},{20,16},{24,28},{28,24},{1,5},{5... | collective-permute-start | bytes 1327112 | tf_op jit(solution)/shard_map/ppermute | solution.py:430
  122.5 9.4 %collective-permute-start.38 = (bf16[1,48,576]{2,1,0:T(8,128)(2,1)S(1)}, bf16[1,48,576]{2,1,0:T(8,128)(2,1)S(1)}, u32[]{:S(2)}, u32[]{:S(2)}) collective-permute-start(bf16[1,48,576]{2,1,0:T(8,128)(2,1)S(1)} %slice.71), channel_id=1, source_target_pairs={{0,16},{4,20},{8,24},{12,28},{16,0},{20,4},{24,8},{28,12},{1,17},{... | collective-permute-start | bytes 165896 | tf_op jit(solution)/shard_map/ppermute | solution.py:430
  131.5 7.0 %collective-permute-start.25 = (bf16[2,56,576]{2,1,0:T(8,128)(2,1)S(1)}, bf16[2,56,576]{2,1,0:T(8,128)(2,1)S(1)}, u32[]{:S(2)}, u32[]{:S(2)}) collective-permute-start(bf16[2,56,576]{2,1,0:T(8,128)(2,1)S(1)} %slice.61), channel_id=1, source_target_pairs={{0,8},{4,12},{8,0},{12,4},{16,24},{20,28},{24,16},{28,20},{1,9},{5... | collective-permute-start | bytes 387080 | tf_op jit(solution)/shard_map/ppermute | solution.py:430
  132.0 27.4 %collective-permute-start.39 = (bf16[1,48,576]{2,1,0:T(8,128)(2,1)S(1)}, bf16[1,48,576]{2,1,0:T(8,128)(2,1)S(1)}, u32[]{:S(2)}, u32[]{:S(2)}) collective-permute-start(bf16[1,48,576]{2,1,0:T(8,128)(2,1)S(1)} %add_convert_fusion.8), channel_id=1, source_target_pairs={{0,16},{4,20},{8,24},{12,28},{16,0},{20,4},{24,8},{28,12},{1,17},{... | collective-permute-start | bytes 165896 | tf_op jit(solution)/shard_map/ppermute | solution.py:430
  138.1 7.0 %collective-permute-start.31 = (bf16[2,144,384]{2,1,0:T(8,128)(2,1)S(1)}, bf16[2,144,384]{2,1,0:T(8,128)(2,1)S(1)}, u32[]{:S(2)}, u32[]{:S(2)}) collective-permute-start(bf16[2,144,384]{2,1,0:T(8,128)(2,1)S(1)} %slice.65), channel_id=1, source_target_pairs={{0,8},{4,12},{8,0},{12,4},{16,24},{20,28},{24,16},{28,20},{1,9},{5... | collective-permute-start | bytes 663560 | tf_op jit(solution)/shard_map/ppermute | solution.py:430
  138.6 9.6 %collective-permute-start.26 = (bf16[1,56,576]{2,1,0:T(8,128)(2,1)S(1)}, bf16[1,56,576]{2,1,0:T(8,128)(2,1)S(1)}, u32[]{:S(2)}, u32[]{:S(2)}) collective-permute-start(bf16[1,56,576]{2,1,0:T(8,128)(2,1)S(1)} %slice.63), channel_id=1, source_target_pairs={{0,16},{4,20},{8,24},{12,28},{16,0},{20,4},{24,8},{28,12},{1,17},{... | collective-permute-start | bytes 193544 | tf_op jit(solution)/shard_map/ppermute | solution.py:430
  145.2 8.4 %collective-permute-start.32 = (bf16[1,144,384]{2,1,0:T(8,128)(2,1)S(1)}, bf16[1,144,384]{2,1,0:T(8,128)(2,1)S(1)}, u32[]{:S(2)}, u32[]{:S(2)}) collective-permute-start(bf16[1,144,384]{2,1,0:T(8,128)(2,1)S(1)} %slice.67), channel_id=1, source_target_pairs={{0,16},{4,20},{8,24},{12,28},{16,0},{20,4},{24,8},{28,12},{1,17},{... | collective-permute-start | bytes 331784 | tf_op jit(solution)/shard_map/ppermute | solution.py:430
  148.3 7.7 %collective-permute-start.27 = (bf16[1,56,576]{2,1,0:T(8,128)(2,1)S(1)}, bf16[1,56,576]{2,1,0:T(8,128)(2,1)S(1)}, u32[]{:S(2)}, u32[]{:S(2)}) collective-permute-start(bf16[1,56,576]{2,1,0:T(8,128)(2,1)S(1)} %add_convert_fusion.7), channel_id=1, source_target_pairs={{0,16},{4,20},{8,24},{12,28},{16,0},{20,4},{24,8},{28,12},{1,17},{... | collective-permute-start | bytes 193544 | tf_op jit(solution)/shard_map/ppermute | solution.py:430
  159.3 7.8 %collective-permute-start.34 = (bf16[2,144,384]{2,1,0:T(8,128)(2,1)S(1)}, bf16[2,144,384]{2,1,0:T(8,128)(2,1)S(1)}, u32[]{:S(2)}, u32[]{:S(2)}) collective-permute-start(bf16[2,144,384]{2,1,0:T(8,128)(2,1)S(1)} %pad_maximum_fusion.3), channel_id=1, source_target_pairs={{0,8},{4,12},{8,0},{12,4},{16,24},{20,28},{24,16},{28,20},{1,9},{5... | collective-permute-start | bytes 663560 | tf_op jit(solution)/shard_map/ppermute | solution.py:430
  159.4 9.3 %collective-permute-start.40 = (bf16[2,48,576]{2,1,0:T(8,128)(2,1)S(1)}, bf16[2,48,576]{2,1,0:T(8,128)(2,1)S(1)}, u32[]{:S(2)}, u32[]{:S(2)}) collective-permute-start(bf16[2,48,576]{2,1,0:T(8,128)(2,1)S(1)} %pad_maximum_fusion.5), channel_id=1, source_target_pairs={{0,8},{4,12},{8,0},{12,4},{16,24},{20,28},{24,16},{28,20},{1,9},{5... | collective-permute-start | bytes 331784 | tf_op jit(solution)/shard_map/ppermute | solution.py:430
  162.7 26.8 %collective-permute-start.29 = (bf16[4,56,576]{2,1,0:T(8,128)(2,1)S(1)}, bf16[4,56,576]{2,1,0:T(8,128)(2,1)S(1)}, u32[]{:S(2)}, u32[]{:S(2)}) collective-permute-start(bf16[4,56,576]{2,1,0:T(8,128)(2,1)S(1)} %pad_maximum_fusion.1.first), channel_id=1, source_target_pairs={{0,4},{4,0},{8,12},{12,8},{16,20},{20,16},{24,28},{28,24},{1,5},{5... | collective-permute-start | bytes 774152 | tf_op jit(solution)/shard_map/ppermute | solution.py:430
  167.2 26.6 %collective-permute-start.35 = (bf16[4,144,384]{2,1,0:T(8,128)(2,1)S(1)}, bf16[4,144,384]{2,1,0:T(8,128)(2,1)S(1)}, u32[]{:S(2)}, u32[]{:S(2)}) collective-permute-start(bf16[4,144,384]{2,1,0:T(8,128)(2,1)S(1)} %pad_maximum_fusion.first), channel_id=1, source_target_pairs={{0,4},{4,0},{8,12},{12,8},{16,20},{20,16},{24,28},{28,24},{1,5},{5... | collective-permute-start | bytes 1327112 | tf_op jit(solution)/shard_map/ppermute | solution.py:430
  168.8 15.4 %collective-permute-start.41 = (bf16[4,48,576]{2,1,0:T(8,128)(2,1)S(1)}, bf16[4,48,576]{2,1,0:T(8,128)(2,1)S(1)}, u32[]{:S(2)}, u32[]{:S(2)}) collective-permute-start(bf16[4,48,576]{2,1,0:T(8,128)(2,1)S(1)} %pad_maximum_fusion.2.first), channel_id=1, source_target_pairs={{0,4},{4,0},{8,12},{12,8},{16,20},{20,16},{24,28},{28,24},{1,5},{5... | collective-permute-start | bytes 663560 | tf_op jit(solution)/shard_map/ppermute | solution.py:430
  (40 other events, 556.6 us)

commit v2 on v1

--- a/solution.py
+++ b/solution.py
@@ -17,6 +17,8 @@
 BLOCK = 128
 PAIRS = 5
 QW = PAIRS * 128
+UNROLL = 4
+MICROS = (7, 6, 6, 13)
 F32 = jnp.float32
 BF16 = jnp.bfloat16
 
@@ -82,9 +84,9 @@
 def soft_rows(scores, allowed):
     halves = []
     for start in range(0, scores.shape[1], BLOCK):
-        part = jnp.where(allowed, scores[:, start : start + BLOCK] * HD ** (-0.5), -1e30)
+        part = jnp.where(allowed, scores[:, start : start + BLOCK], -1e30)
         part = jnp.exp(part - jnp.max(part, axis=-1, keepdims=True))
-        halves.append(part / jnp.sum(part, axis=-1, keepdims=True))
+        halves.append(part * (1.0 / jnp.sum(part, axis=-1, keepdims=True)))
     return halves
 
 
@@ -99,7 +101,7 @@
     wkv = refs[3 * n_shard : 4 * n_shard]
     wo = refs[4 * n_shard : 5 * n_shard]
     (x_ref, nrm_ref, q_ref, kv_ref, mix_ref, mid_ref, nmid_ref, cos_ref, sin_ref, gain_ref,
-     wq_full, wkv_full, wo_full) = refs[5 * n_shard :]
+     wq_full, wkv_full, wo_full, query_all, keyval_all) = refs[5 * n_shard :]
     shard = idx[0]
     width = wq[0].shape[0]
     model = x_ref.shape[1]
@@ -133,16 +135,20 @@
     gain_attn = gains[2:3, :]
     gain_mlp = gains[3:4, :]
 
+    for part in range(n_shard):
+        stream = tok[part][...].astype(F32)
+        rows = pl.ds(part * BLOCK, BLOCK)
+        nrm_ref[rows, :] = (stream * inverse_rms(stream) * gain_attn).astype(BF16)
+    query_all[...] = mm(nrm_ref[...], wq_full[...])
+    keyval_all[...] = mm(nrm_ref[...], wkv_full[...])
+
     def body(block, carry):
         rows = pl.ds(pl.multiple_of(block * BLOCK, BLOCK), BLOCK)
-        stream = x_ref[rows, :].astype(F32)
-        normed = (stream * inverse_rms(stream) * gain_attn).astype(BF16)
-        nrm_ref[rows, :] = normed
         cosine = cos_ref[rows, :]
         sine = sin_ref[rows, :]
         sine = jnp.where(first_half, -sine, sine)
-        query_raw = mm(normed, wq_full[...])
-        keyval = mm(normed, wkv_full[...])
+        query_raw = query_all[rows, :]
+        keyval = keyval_all[rows, :]
 
         def rope(values):
             return values * cosine + swapped(values, first_half) * sine
@@ -154,18 +160,18 @@
         keys, values = split_heads(keyval)
         mixed = []
         for pair in range(PAIRS):
-            query = rope(query_raw[:, 128 * pair : 128 * pair + 128]).astype(BF16)
+            query = (rope(query_raw[:, 128 * pair : 128 * pair + 128]) * HD ** (-0.5)).astype(BF16)
             q_ref[rows, 128 * pair : 128 * pair + 128] = query
             soft = soft_rows(mm_nt(query, pair_operand(keys, pair)), allowed)
             mixed.append(mm(joined(soft).astype(BF16), pair_operand(values, pair)).astype(BF16))
         mixed = jnp.concatenate(mixed, axis=1)
         mix_ref[rows, :] = mixed
-        stream_mid = stream + mm(mixed, wo_full[...])
-        mid_ref[rows, :] = stream_mid
-        nmid_ref[rows, :] = (stream_mid * inverse_rms(stream_mid) * gain_mlp).astype(BF16)
         return carry
 
-    lax.fori_loop(0, n_shard, body, 0)
+    lax.fori_loop(0, n_shard, body, 0, unroll=UNROLL)
+    stream_mid = x_ref[...].astype(F32) + mm(mix_ref[...], wo_full[...])
+    mid_ref[...] = stream_mid
+    nmid_ref[...] = (stream_mid * inverse_rms(stream_mid) * gain_mlp).astype(BF16)
 
 
 def bit_reverse(value, total):
@@ -178,66 +184,100 @@
     return result
 
 
-def mlp_kernel(n_shard, n_rep, idx, *refs):
-    nmid_ref, mid_ref, live_ref = refs[:3]
-    cot = refs[3 : 3 + n_shard]
-    wgu = refs[3 + n_shard : 3 + 2 * n_shard]
-    wd = refs[3 + 2 * n_shard : 3 + 3 * n_shard]
-    (act_ref, dn_ref, down_lo, down_hi, gu_lo, gu_hi, dcot_ref, w_full, down_all, gu_all) = refs[3 + 3 * n_shard :]
+def spread(target, member, n_rep, first_row, slab, value):
+    to = bit_reverse(member ^ slab, n_rep)
+    target[to, first_row : first_row + value.shape[0], :] = value.astype(BF16)
+
+
+def mlp_kernel(n_shard, n_rep, first_call, idx, *refs):
+    if first_call:
+        (nmid_ref, mid_ref, wd_own, wd_other), cot, wgu = refs[:4], refs[4 : 4 + n_shard], refs[4 + n_shard : -13]
+        (act_ref, dn_ref, lo_ref, hi_ref, dcot_ref, w_full, own_ref, all_ref, wd_pair, wide_ref, sem, wd_sem,
+         cot_sem) = refs[-13:]
+    else:
+        (nmid_ref, act_in, live_ref, wd_own, wd_other, dcot_ref, w_full, own_ref, dn_in, act_ref, dn_ref, lo_ref,
+         hi_ref, all_ref, wd_pair, wd_sem) = refs
     shard = idx[0]
     member = idx[1]
-    width = wgu[0].shape[0]
-    ff = wgu[0].shape[1] // 2
+    first = 0 if first_call else 2
+    model = nmid_ref.shape[1]
+    ff = w_full.shape[1] // 2
     chunk = ff // n_shard
-    for part in range(n_shard):
-        at = pl.multiple_of((shard ^ part) * width, 16)
-        w_full[pl.ds(at, width), :] = wgu[part][...]
-        dcot_ref[pl.ds(part * BLOCK, BLOCK), :] = cot[part][...]
+    waits = []
+    for part, source in ((first, wd_own), (first + 1, wd_other)):
+        at = pl.multiple_of(((shard ^ part) & 1) * chunk, 128)
+        waits.append(pltpu.make_async_copy(source, wd_pair.at[pl.ds(at, chunk)], wd_sem.at[part - first]))
+    if first_call:
+        width = model // n_shard
+        side = member & 1
+        pieces = [(0, wgu[0], None), (1, wgu[1], None), (2, wgu[2], side), (2, wgu[3], 1 - side),
+                  (3, wgu[4], side), (3, wgu[5], 1 - side)]
+        for number, (part, source, which) in enumerate(pieces):
+            down = pl.ds(pl.multiple_of((shard ^ part) * width, 16), width)
+            if which is None:
+                target = w_full.at[down]
+            else:
+                target = w_full.at[down, pl.ds(pl.multiple_of(which * ff, 128), ff)]
+            waits.append(pltpu.make_async_copy(source, target, sem.at[number]))
+        for part in range(n_shard):
+            waits.append(
+                pltpu.make_async_copy(cot[part], dcot_ref.at[pl.ds(part * BLOCK, BLOCK)], cot_sem.at[part])
+            )
+    for wait in waits:
+        wait.start()
+    if first_call:
+        own_ref[...] = mm(nmid_ref[...], own_columns(shard, model, width)).astype(BF16)
+    for wait in waits:
+        wait.wait()
     normed_mid = nmid_ref[...]
-    own_mid = mm(normed_mid, own_columns(shard, normed_mid.shape[1], width)).astype(BF16)
     d_branch = dcot_ref[...]
-    result = mid_ref[...]
-    gu_rows = gu_all.shape[1]
-    groups = width // gu_rows
-    down_rows = down_all.shape[1]
-    for part in range(n_shard):
-        place = shard ^ part
-        gate_at = pl.ds(pl.multiple_of(place * chunk, 128), chunk)
-        up_at = pl.ds(pl.multiple_of(place * chunk + ff, 128), chunk)
-        gate = mm(normed_mid, w_full[:, gate_at])
-        up = mm(normed_mid, w_full[:, up_at])
-        d_hidden = mm_nt(d_branch, wd[part][...])
-        sigmoid = 1.0 / (1.0 + jnp.exp(-gate))
-        silu = gate * sigmoid
-        hidden = (silu * up).astype(BF16)
-        d_gate = (d_hidden * up * sigmoid * (1.0 + gate * (1.0 - sigmoid))).astype(BF16)
-        d_up = (d_hidden * silu).astype(BF16)
-        d_normed = mm_nt(d_gate, w_full[:, gate_at]) + mm_nt(d_up, w_full[:, up_at])
-        if part == 0:
-            dn_ref[...] = d_normed
-            grad_down = mm_tn(hidden, d_branch)
-            for slab in range(n_rep):
-                to = bit_reverse(member ^ slab, n_rep)
-                down_all[to] = grad_down[slab * down_rows : (slab + 1) * down_rows].astype(BF16)
-        else:
-            dn_ref[...] += d_normed
-        result = result + mm(hidden[:BLOCK], wd[part][...])
-        for offset, piece in ((0, d_gate), (n_shard, d_up)):
-            grad = mm_tn(own_mid, piece)
-            for group in range(groups):
-                to = bit_reverse(member ^ ((place + offset) * groups + group), n_rep)
-                gu_all[to] = grad[group * gu_rows : (group + 1) * gu_rows].astype(BF16)
-    act_ref[...] = result * live_ref[...]
+    base = ((shard ^ first) >> 1) * 2 * chunk
+    gate_at = pl.ds(pl.multiple_of(base, 256), 2 * chunk)
+    up_at = pl.ds(pl.multiple_of(base + ff, 256), 2 * chunk)
+    gate = mm(normed_mid, w_full[:, gate_at])
+    up = mm(normed_mid, w_full[:, up_at])
+    d_hidden = mm_nt(d_branch, wd_pair[...])
+    sigmoid = 0.5 * jnp.tanh(0.5 * gate) + 0.5
+    silu = gate * sigmoid
+    hidden = (silu * up).astype(BF16)
+    d_gate = (d_hidden * up * sigmoid * (1.0 + gate * (1.0 - sigmoid))).astype(BF16)
+    d_up = (d_hidden * silu).astype(BF16)
+    rows = all_ref.shape[1]
+    if first_call:
+        wide_ref[...] = hidden
+        own_hidden = wide_ref[:, pl.ds(pl.multiple_of((shard & 1) * chunk, 128), chunk)]
+        rows = rows // 2
+        grad_down = mm_tn(own_hidden, d_branch)
+        tail = grad_down[:, chunk:]
+        half = chunk // 2
+        grad_down = jnp.concatenate(
+            [grad_down[:, :chunk], jnp.concatenate([tail[:half], tail[half:]], axis=1)], axis=0
+        )
+        for slab in range(n_rep):
+            spread(all_ref, member, n_rep, rows, slab, grad_down[slab * rows : (slab + 1) * rows])
+    slab = 0
+    for piece in (d_gate, d_up):
+        grad = mm_tn(own_ref[...], piece)
+        for column in range(0, 2 * chunk, chunk):
+            for row in range(0, grad.shape[0], rows):
+                spread(all_ref, member, n_rep, 0, slab, grad[row : row + rows, column : column + chunk])
+                slab += 1
     middle = n_rep // 2
-    down_lo[...] = down_all[:middle]
-    down_hi[...] = down_all[middle:]
-    gu_lo[...] = gu_all[:middle]
-    gu_hi[...] = gu_all[middle:]
+    lo_ref[...] = all_ref[:middle]
+    hi_ref[...] = all_ref[middle:]
+    d_normed = mm_nt(d_gate, w_full[:, gate_at]) + mm_nt(d_up, w_full[:, up_at])
+    added = mm(hidden[:BLOCK], wd_pair[...])
+    if first_call:
+        dn_ref[...] = d_normed
+        act_ref[...] = mid_ref[:BLOCK, :] + added
+    else:
+        dn_ref[...] = dn_in[...] + d_normed
+        act_ref[...] = (act_in[...] + added) * live_ref[...]
 
 
 def attn_backward_kernel(n_shard, n_rep, idx, x_ref, nrm_ref, q_ref, kv_ref, mix_ref, mid_ref, cos_ref, sin_ref,
                          gain_ref, wq_full, wkv_full, wo_full, dn_ref, dcot_ref,
-                         din_ref, a_lo, a_hi, dattn_all, dq_all, dkv_all, a_all):
+                         din_ref, a_lo, a_hi, dattn_all, dmix_all, dq_all, dkv_all, a_all):
     shard = idx[0]
     member = idx[1]
     model = x_ref.shape[1]
@@ -250,23 +290,23 @@
     gain_attn = gain_ref[2:3, :]
     gain_mlp = gain_ref[3:4, :]
 
+    stream_mid = mid_ref[...]
+    inv_mlp = inverse_rms(stream_mid)
+    d_normed_mid = dn_ref[...]
+    sum_mlp = jnp.sum(d_normed_mid * stream_mid * inv_mlp, axis=0, keepdims=True)
+    scaled = d_normed_mid * gain_mlp
+    d_mid = (
+        dcot_ref[...].astype(F32)
+        + inv_mlp * scaled
+        - inv_mlp**3 * stream_mid * jnp.mean(scaled * stream_mid, axis=-1, keepdims=True)
+    )
+    din_ref[...] = d_mid[:BLOCK, :]
+    dattn_all[...] = d_mid.astype(BF16)
+    dmix_all[...] = mm_nt(dattn_all[...], wo_full[...]).astype(BF16)
+
     def body(block, carry):
-        sum_attn, sum_mlp = carry
         rows = pl.ds(pl.multiple_of(block * BLOCK, BLOCK), BLOCK)
-        stream = x_ref[rows, :].astype(F32)
-        stream_mid = mid_ref[rows, :]
-        inv_mlp = inverse_rms(stream_mid)
-        d_normed_mid = dn_ref[rows, :]
-        sum_mlp = sum_mlp + jnp.sum(d_normed_mid * stream_mid * inv_mlp, axis=0, keepdims=True)
-        scaled = d_normed_mid * gain_mlp
-        d_mid = (
-            dcot_ref[rows, :].astype(F32)
-            + inv_mlp * scaled
-            - inv_mlp**3 * stream_mid * jnp.mean(scaled * stream_mid, axis=-1, keepdims=True)
-        )
-        d_attn = d_mid.astype(BF16)
-        dattn_all[rows, :] = d_attn
-        d_mixed = mm_nt(d_attn, wo_full[...]).astype(BF16)
+        d_mixed = dmix_all[rows, :]
         cosine = cos_ref[rows, :]
         sine = sin_ref[rows, :]
         sine = jnp.where(first_half, sine, -sine)
@@ -314,30 +354,23 @@
             total = jnp.where(low, 0.0, pltpu.roll(low_piece, HD, 1))
             return total if high_piece is None else total + jnp.where(low, 0.0, high_piece)
 
-        scale = HD ** (-0.5)
-        first = rope_back((placed(d_keys[0], True) + placed(d_keys[1], False)) * scale)
-        second = rope_back(placed(d_keys[2], True) * scale) + placed(d_values[0], False)
+        first = rope_back(placed(d_keys[0], True) + placed(d_keys[1], False))
+        second = rope_back(placed(d_keys[2], True)) + placed(d_values[0], False)
         third = placed(d_values[1], True) + placed(d_values[2], False)
         d_keyval = jnp.concatenate([first, second, third], axis=1).astype(BF16)
         dq_all[rows, :] = d_query
         dkv_all[rows, :] = d_keyval
-        d_normed = mm_nt(d_query, wq_full[...]) + mm_nt(d_keyval, wkv_full[...])
-        inv_attn = inverse_rms(stream)
-        sum_attn = sum_attn + jnp.sum(d_normed * stream * inv_attn, axis=0, keepdims=True)
-
-        @pl.when(block == 0)
-        def _():
-            scaled_in = d_normed * gain_attn
-            din_ref[...] = (
-                d_mid
-                + inv_attn * scaled_in
-                - inv_attn**3 * stream * jnp.mean(scaled_in * stream, axis=-1, keepdims=True)
-            )
-
-        return (sum_attn, sum_mlp)
-
-    zero = jnp.zeros((1, model), F32)
-    sum_attn, sum_mlp = lax.fori_loop(0, n_shard, body, (zero, zero))
+        return carry
+
+    lax.fori_loop(0, n_shard, body, 0, unroll=UNROLL)
+    d_normed = mm_nt(dq_all[...], wq_full[...]) + mm_nt(dkv_all[...], wkv_full[...])
+    stream = x_ref[...].astype(F32)
+    inv_attn = inverse_rms(stream)
+    sum_attn = jnp.sum(d_normed * stream * inv_attn, axis=0, keepdims=True)
+    own_in = d_normed[:BLOCK, :] * gain_attn
+    own_stream = stream[:BLOCK, :]
+    own_inv = inv_attn[:BLOCK, :]
+    din_ref[...] += own_inv * own_in - own_inv**3 * own_stream * jnp.mean(own_in * own_stream, axis=-1, keepdims=True)
     chosen = own_columns(shard, model, width)
     own_normed = mm(nrm_ref[...], chosen).astype(BF16)
     own_mixed = mm(mix_ref[:, :model], chosen).astype(BF16)
@@ -364,44 +397,68 @@
             a_hi[to - middle] = piece
 
 
-def unpack_down_kernel(n_rep, idx, first, second, out_ref):
+def fetch(first, second, member, slab, n_rep, target, rows):
+    at = bit_reverse(member ^ slab, n_rep)
+    middle = n_rep // 2
+
+    @pl.when(at < middle)
+    def _():
+        target[pl.ds(slab * rows, rows), :] = first[at].astype(F32)
+
+    @pl.when(at >= middle)
+    def _():
+        target[pl.ds(slab * rows, rows), :] = second[at - middle].astype(F32)
+
+
+def unpack_mlp_kernel(n_rep, n_shard, idx, one_lo, one_hi, two_lo, two_hi, down_ref, gu_ref):
+    shard = idx[0]
     member = idx[1]
     middle = n_rep // 2
+    rows, chunk = two_lo.shape[1:]
+    ff = gu_ref.shape[1] // 2
+    half = chunk // 2
+    groups = gu_ref.shape[0] // rows
+
+    def place_down(slab, piece):
+        row = slab * rows
+        if row < chunk:
+            count = min(rows, chunk - row)
+            down_ref[row : row + count, :chunk] = piece[:count]
+            piece = piece[count:]
+            row += count
+        if piece.shape[0]:
+            row -= chunk
+            down_ref[row : row + piece.shape[0], chunk:] = piece[:, :half]
+            down_ref[half + row : half + row + piece.shape[0], chunk:] = piece[:, half:]
+
+    def place_gateup(slab, pair, piece):
+        up, rest = divmod(slab, 2 * groups)
+        column, group = divmod(rest, groups)
+        base = ((shard ^ (2 * pair)) >> 1) * 2 * chunk + column * chunk + up * ff
+        gu_ref[group * rows : (group + 1) * rows, pl.ds(pl.multiple_of(base, 128), chunk)] = piece
+
+    for slab in range(n_rep):
+        at = bit_reverse(member ^ slab, n_rep)
+
+        def place(one, two, where):
+            piece = one[where].astype(F32)
+            place_gateup(slab, 0, piece[:rows])
+            place_down(slab, piece[rows:])
+            place_gateup(slab, 1, two[where].astype(F32))
+
+        @pl.when(at < middle)
+        def _():
+            place(one_lo, two_lo, at)
+
+        @pl.when(at >= middle)
+        def _():
+            place(one_hi, two_hi, at - middle)
+
+
+def unpack_attn_kernel(n_rep, idx, first, second, q_ref, kv_ref, o_ref, gain_ref, a_all):
     rows = first.shape[1]
     for slab in range(n_rep):
-        at = bit_reverse(member ^ slab, n_rep)
-        here = pl.ds(slab * rows, rows)
-
-        @pl.when(at < middle)
-        def _():
-            out_ref[here, :] = first[at].astype(F32)
-
-        @pl.when(at >= middle)
-        def _():
-            out_ref[here, :] = second[at - middle].astype(F32)
-
-
-def unpack_gateup_kernel(n_rep, idx, first, second, out_ref):
-    member = idx[1]
-    middle = n_rep // 2
-    rows, columns = first.shape[1:]
-    groups = out_ref.shape[0] // rows
-    for slab in range(n_rep):
-        at = bit_reverse(member ^ slab, n_rep)
-        down = pl.ds((slab % groups) * rows, rows)
-        across = pl.ds((slab // groups) * columns, columns)
-
-        @pl.when(at < middle)
-        def _():
-            out_ref[down, across] = first[at].astype(F32)
-
-        @pl.when(at >= middle)
-        def _():
-            out_ref[down, across] = second[at - middle].astype(F32)
-
-
-def unpack_attn_kernel(n_rep, idx, first, second, q_ref, kv_ref, o_ref, gain_ref, a_all):
-    unpack_down_kernel(n_rep, idx, first, second, a_all)
+        fetch(first, second, idx[1], slab, n_rep, a_all, rows)
     width = q_ref.shape[0]
     q_ref[...] = a_all[:width, :]
     o_ref[...] = a_all[width : 2 * width, :]
@@ -409,16 +466,18 @@
     gain_ref[...] = a_all[3 * width : 3 * width + 8, :]
 
 
-def call(body, operands, outs, scratch=(), flops=0, moved=0, exps=0):
-    vmem = pl.BlockSpec(memory_space=pltpu.VMEM)
+def call(body, operands, outs, scratch=(), micros=1, vmem=24, raw=()):
+    in_vmem = pl.BlockSpec(memory_space=pltpu.VMEM)
+    in_hbm = pl.BlockSpec(memory_space=pltpu.HBM)
+    specs = [in_hbm if number in raw else in_vmem for number in range(1, len(operands))]
     return pl.pallas_call(
         body,
         out_shape=outs,
-        in_specs=[pl.BlockSpec(memory_space=pltpu.SMEM)] + [vmem] * (len(operands) - 1),
-        out_specs=jax.tree.map(lambda _: vmem, outs),
+        in_specs=[pl.BlockSpec(memory_space=pltpu.SMEM)] + specs,
+        out_specs=jax.tree.map(lambda _: in_vmem, outs),
         scratch_shapes=list(scratch),
-        compiler_params=pltpu.CompilerParams(vmem_limit_bytes=56 * 2**20),
-        cost_estimate=pl.CostEstimate(flops=flops, bytes_accessed=moved, transcendentals=exps),
+        compiler_params=pltpu.CompilerParams(vmem_limit_bytes=vmem * 2**20),
+        cost_estimate=pl.CostEstimate(flops=int(micros * 1e9), bytes_accessed=2**20, transcendentals=0),
     )(*operands)
 
 
@@ -487,9 +546,11 @@
     wq = gather_group(w_query[0], n_shard)
     wkv = gather_group(w_keyval[0], n_shard)
     wo = gather_group(w_out[0], n_shard)
-    wgu = gather_group(w_gateup[0], n_shard)
-    cot = gather_group(cotangent, n_shard)
-    wd = gather_group(w_down[0], n_shard)
+    side = member & 1
+    gu_direct = exchange(lax.dynamic_slice(w_gateup[0], (0, side * ff), (width, ff)), "fsdp", n_shard, 2)
+    gu_around = exchange(gu_direct, "rep", n_rep, 1)
+    cot_across = exchange(cotangent, "fsdp", n_shard, 2)
+    down_across = exchange(w_down[0], "fsdp", n_shard, 2)
     (x_all, normed, query, keyval, mixed, mid, normed_mid, cosine, sine, gains, wq_full, wkv_full, wo_full) = call(
         functools.partial(attn_forward_kernel, n_shard),
         [idx] + tok + small + wq + wkv + wo,
@@ -508,39 +569,65 @@
             shape((model, kv_width), BF16),
             shape((QW, model), BF16),
         ),
-        flops=2 * group_rows * model * (2 * model + kv_width + 2 * 256),
-        moved=8 * 2**20,
-        exps=group_rows * 128 * HEADS,
+        [pltpu.VMEM((group_rows, QW), F32), pltpu.VMEM((group_rows, kv_width), F32)],
+        micros=MICROS[0],
     )
     middle = n_rep // 2
-    groups = max(1, n_rep // (2 * n_shard))
-    gu_slab = (width // groups, ff // n_shard)
-    down_slab = (w_down.shape[1] // n_rep, model)
+    chunk = ff // n_shard
+    slab_rows = width * 4 // n_rep
     a_rows = 3 * width + 16
     a_slab = (a_rows // n_rep, model)
-    out_act, d_normed_mid, down_lo, down_hi, gu_lo, gu_hi, dcot = call(
-        functools.partial(mlp_kernel, n_shard, n_rep),
-        [idx, normed_mid, mid[:row_count], live] + cot + wgu + wd,
+    gu_own, cot_own, down_own, gu_direct, gu_around, cot_across, down_across, _ = lax.optimization_barrier(
+        (w_gateup[0], cotangent, w_down[0], gu_direct, gu_around, cot_across, down_across, gains)
+    )
+    gu = [gu_own, exchange(gu_own, "fsdp", n_shard, 1), gu_direct, gu_around,
+          exchange(gu_direct, "fsdp", n_shard, 1), exchange(gu_around, "fsdp", n_shard, 1)]
+    cot = [cot_own, exchange(cot_own, "fsdp", n_shard, 1), cot_across, exchange(cot_across, "fsdp", n_shard, 1)]
+    down_beside = exchange(down_own, "fsdp", n_shard, 1)
+    half_act, half_dn, one_lo, one_hi, dcot, gu_full, own_mid = call(
+        functools.partial(mlp_kernel, n_shard, n_rep, True),
+        [idx, normed_mid, mid, down_own, down_beside] + cot + gu,
         (
             shape((row_count, model), F32),
             shape((group_rows, model), F32),
-            shape((middle,) + down_slab, BF16),
-            shape((middle,) + down_slab, BF16),
-            shape((middle,) + gu_slab, BF16),
-            shape((middle,) + gu_slab, BF16),
+            shape((middle, 2 * slab_rows, chunk), BF16),
+            shape((middle, 2 * slab_rows, chunk), BF16),
             shape((group_rows, model), BF16),
+            shape((model, 2 * ff), BF16),
+            shape((group_rows, width), BF16),
         ),
         [
-            pltpu.VMEM((model, 2 * ff), BF16),
-            pltpu.VMEM((n_rep,) + down_slab, BF16),
-            pltpu.VMEM((n_rep,) + gu_slab, BF16),
+            pltpu.VMEM((n_rep, 2 * slab_rows, chunk), BF16),
+            pltpu.VMEM((2 * chunk, model), BF16),
+            pltpu.VMEM((group_rows, 2 * chunk), BF16),
+            pltpu.SemaphoreType.DMA((6,)),
+            pltpu.SemaphoreType.DMA((2,)),
+            pltpu.SemaphoreType.DMA((n_shard,)),
         ],
-        flops=2 * group_rows * model * 10 * ff // 2,
-        moved=12 * 2**20,
-        exps=group_rows * ff,
-    )
-    down = sum_over_replicas(down_lo, down_hi, n_rep)
-    gateup = sum_over_replicas(gu_lo, gu_hi, n_rep)
+        micros=MICROS[1],
+        raw=range(3, 5 + 2 * n_shard + 2),
+    )
+    down_across, _ = lax.optimization_barrier((down_across, half_act))
+    down_corner = exchange(down_across, "fsdp", n_shard, 1)
+    out_act, d_normed_mid, two_lo, two_hi = call(
+        functools.partial(mlp_kernel, n_shard, n_rep, False),
+        [idx, normed_mid, half_act, live, down_across, down_corner, dcot, gu_full, own_mid, half_dn],
+        (
+            shape((row_count, model), F32),
+            shape((group_rows, model), F32),
+            shape((middle, slab_rows, chunk), BF16),
+            shape((middle, slab_rows, chunk), BF16),
+        ),
+        [
+            pltpu.VMEM((n_rep, slab_rows, chunk), BF16),
+            pltpu.VMEM((2 * chunk, model), BF16),
+            pltpu.SemaphoreType.DMA((2,)),
+        ],
+        micros=MICROS[2],
+        raw=(4, 5),
+    )
+    one = sum_over_replicas(one_lo, one_hi, n_rep)
+    two = sum_over_replicas(two_lo, two_hi, n_rep)
     in_grad, a_lo, a_hi = call(
         functools.partial(attn_backward_kernel, n_shard, n_rep),
         [idx, x_all, normed, query, keyval, mixed, mid, cosine, sine, gains, wq_full, wkv_full, wo_full,
@@ -553,25 +640,18 @@
         [
             pltpu.VMEM((group_rows, model), BF16),
             pltpu.VMEM((group_rows, QW), BF16),
+            pltpu.VMEM((group_rows, QW), BF16),
             pltpu.VMEM((group_rows, kv_width), BF16),
             pltpu.VMEM((a_rows, model), F32),
         ],
-        flops=2 * group_rows * model * (3 * model + 2 * kv_width),
-        moved=8 * 2**20,
-        exps=group_rows * 128 * HEADS,
+        micros=MICROS[3],
     )
     attn = sum_over_replicas(a_lo, a_hi, n_rep)
-    grad_down = call(
-        functools.partial(unpack_down_kernel, n_rep),
-        [idx] + list(down),
-        shape((w_down.shape[1], model), F32),
-        moved=2 * 2**20,
-    )
-    grad_gateup = call(
-        functools.partial(unpack_gateup_kernel, n_rep),
-        [idx] + list(gateup),
-        shape((width, 2 * ff), F32),
-        moved=3 * 2**20,
+    grad_down, grad_gateup = call(
+        functools.partial(unpack_mlp_kernel, n_rep, n_shard),
+        [idx] + list(one) + list(two),
+        (shape((w_down.shape[1], model), F32), shape((width, 2 * ff), F32)),
+        micros=3,
     )
     grad_query, grad_keyval, grad_out, gain_rows = call(
         functools.partial(unpack_attn_kernel, n_rep),
@@ -583,7 +663,7 @@
             shape((8, model), F32),
         ),
         [pltpu.VMEM((a_rows, model), F32)],
-        moved=2 * 2**20,
+        micros=2,
     )
     own_gains = lax.dynamic_slice(gain_rows, (0, shard * width), (2, width))
     return (

time: 198 us -> 147 us (0.74)
  waiting for transfers between devices: 81.1 us -> 59.2 us
  Pallas kernels: 53.8 us -> 37.6 us
  local copies, waits for them, and re-layouts: 15 us -> 8.97 us
  starting transfers between devices: 40.2 us -> 36.9 us
  other arithmetic: 5.43 us -> 2.29 us
    ppermute x42 -> x44, waiting for transfers between devices: 81.1 us -> 59.2 us  [exchange(): lax.ppermute(value, axis, [(member, member ^ mask) for member in range(to...]
    pallas_call x6, Pallas kernels: 53.8 us -> 37.6 us  [call(): pl.pallas_call(body, out_shape=outs, in_specs=[pl.BlockSpec(memory_space=...]
    unnamed x66 -> x20, local copies, waits for them, and re-layouts: 11.7 us -> 6.37 us
    ppermute x42 -> x44, starting transfers between devices: 40.2 us -> 36.9 us  [exchange(): lax.ppermute(value, axis, [(member, member ^ mask) for member in range(to...]
  transfers between devices with their start and end apart: 42 -> 44, of which waited for: 20 -> 19; matrix products, arithmetic and copies ran while one was open for 8% -> 6% of each run, Pallas kernels for 19% -> 18%
where the time goes in v2:
time: 147 us
  waiting for transfers between devices  59.2 us (40%)
  Pallas kernels  37.6 us (26%)
  starting transfers between devices  36.9 us (25%)
  local copies, waits for them, and re-layouts  8.97 us (6%)
  other arithmetic  2.29 us (2%)
  between operations  1.65 us (1%)
    ppermute x44, waiting for transfers between devices, exchange(): lax.ppermute(value, axis, [(member, member ^ mask) for member in range(to...  59.2 us
    pallas_call x6, Pallas kernels, call(): pl.pallas_call(body, out_shape=outs, in_specs=[pl.BlockSpec(memory_space=...  37.6 us
    ppermute x44, starting transfers between devices, exchange(): lax.ppermute(value, axis, [(member, member ^ mask) for member in range(to...  36.9 us
    unnamed x20, local copies, waits for them, and re-layouts  6.37 us
  transfers between devices with their start and end apart: 44, of which 19 were waited for; matrix products, arithmetic and copies ran while one was open for 6% of the time, Pallas kernels for 18%

profile of v2, /device:TPU:0, one launch (start us, length us, event | category | flops | bytes accessed | tf_op | source)
XLA Modules:
  0.0 146.5 jit_solution(15301903187083165515)
XLA Ops:
  0.7 3.0 %collective-permute-start.10 = (bf16[144,384]{1,0:T(8,128)(2,1)}, bf16[144,384]{1,0:T(8,128)(2,1)S(1)}, u32[]{:S(2)}, u32[]{:S(2)}) collective-permute-start(bf16[144,384]{1,0:T(8,128)(2,1)} %bitcast.33), channel_id=1, source_target_pairs={{0,2},{1,3},{2,0},{3,1},{4,6},{5,7},{6,4},{7,5},{8,10},{9,11},{10,... | collective-permute-start | bytes 331784 | tf_op jit(solution)/shard_map/ppermute | solution.py:489
  5.8 3.1 %collective-permute-done.4.refs_6_ = bf16[16,256]{1,0:T(8,128)(2,1)S(1)} collective-permute-done((bf16[16,256]{1,0:T(8,128)(2,1)S(1)}, bf16[16,256]{1,0:T(8,128)(2,1)S(1)}, u32[]{:S(2)}, u32[]{:S(2)}) %collective-permute-start.4) | collective-permute-done | bytes 8224 | tf_op jit(solution)/shard_map/ppermute | solution.py:489
  10.6 1.7 %collective-permute-start.13 = (bf16[144,576]{1,0:T(8,128)(2,1)}, bf16[144,576]{1,0:T(8,128)(2,1)S(1)}, u32[]{:S(2)}, u32[]{:S(2)}) collective-permute-start(bf16[144,576]{1,0:T(8,128)(2,1)} %bitcast.30), channel_id=1, source_target_pairs={{0,2},{1,3},{2,0},{3,1},{4,6},{5,7},{6,4},{7,5},{8,10},{9,11},{10,... | collective-permute-start | bytes 497672 | tf_op jit(solution)/shard_map/ppermute | solution.py:489
  12.7 1.8 %dynamic-slice_bitcast_fusion = bf16[144,1536]{1,0:T(8,128)(2,1)} fusion(bf16[1,144,3072]{2,1,0:T(8,128)(2,1)} %param.17, s32[]{:T(128)S(6)} %select_n.34), kind=kLoop, calls=%fused_computation.5 | loop fusion | bytes 884740 | tf_op jit(solution)/shard_map/dynamic_slice | solution.py:550
  15.4 1.6 %collective-permute-done.1.refs_2_ = bf16[128,576]{1,0:T(8,128)(2,1)S(1)} collective-permute-done((bf16[128,576]{1,0:T(8,128)(2,1)S(1)}, bf16[128,576]{1,0:T(8,128)(2,1)S(1)}, u32[]{:S(2)}, u32[]{:S(2)}) %collective-permute-start.1) | collective-permute-done | bytes 147488 | tf_op jit(solution)/shard_map/ppermute | solution.py:489
  17.3 3.7 %collective-permute-done.13.refs_18_ = bf16[144,576]{1,0:T(8,128)(2,1)S(1)} collective-permute-done((bf16[144,576]{1,0:T(8,128)(2,1)}, bf16[144,576]{1,0:T(8,128)(2,1)S(1)}, u32[]{:S(2)}, u32[]{:S(2)}) %collective-permute-start.13) | collective-permute-done | bytes 165920 | tf_op jit(solution)/shard_map/ppermute | solution.py:489
  21.0 3.9 %collective-permute-done.7.refs_10_ = bf16[144,576]{1,0:T(8,128)(2,1)S(1)} collective-permute-done((bf16[144,576]{1,0:T(8,128)(2,1)}, bf16[144,576]{1,0:T(8,128)(2,1)S(1)}, u32[]{:S(2)}, u32[]{:S(2)}) %collective-permute-start.7) | collective-permute-done | bytes 165920 | tf_op jit(solution)/shard_map/ppermute | solution.py:489
  28.4 1.9 %collective-permute-start.18 = (bf16[384,576]{1,0:T(8,128)(2,1)S(1)}, bf16[384,576]{1,0:T(8,128)(2,1)S(1)}, u32[]{:S(2)}, u32[]{:S(2)}) collective-permute-start(bf16[384,576]{1,0:T(8,128)(2,1)S(1)} %bitcast.22), channel_id=1, source_target_pairs={{0,2},{1,3},{2,0},{3,1},{4,6},{5,7},{6,4},{7,5},{8,10},{9,11},{10,... | collective-permute-start | bytes 1327112 | tf_op jit(solution)/shard_map/ppermute | solution.py:489
  30.2 4.2 %collective-permute-done.15.refs_10_ = bf16[144,1536]{1,0:T(8,128)(2,1)S(1)} collective-permute-done((bf16[144,1536]{1,0:T(8,128)(2,1)}, bf16[144,1536]{1,0:T(8,128)(2,1)S(1)}, u32[]{:S(2)}, u32[]{:S(2)}) %collective-permute-start.15) | collective-permute-done | bytes 442400 | tf_op jit(solution)/shard_map/ppermute | solution.py:489
  36.8 6.3 %shard_map.178 = (bf16[512,576]{1,0:T(8,128)(2,1)S(1)}, bf16[512,576]{1,0:T(8,128)(2,1)S(1)}, bf16[512,640]{1,0:T(8,128)(2,1)S(1)}, bf16[512,384]{1,0:T(8,128)(2...) custom-call(s32[2]{0:T(128)S(1)} %pad_add_fusion.idx, ...), custom_call_target="tpu_custom_call" | custom-call | flops 7000000000 | bytes 1048576 | tf_op jit(solution)/shard_map/pallas_call | solution.py:473
  43.2 4.9 %collective-permute-done.18.refs_3_ = bf16[384,576]{1,0:T(8,128)(2,1)S(1)} collective-permute-done((bf16[384,576]{1,0:T(8,128)(2,1)S(1)}, bf16[384,576]{1,0:T(8,128)(2,1)S(1)}, u32[]{:S(2)}, u32[]{:S(2)}) %collective-permute-start.18) | collective-permute-done | bytes 442400 | tf_op jit(solution)/shard_map/ppermute | solution.py:489
  49.2 3.5 %collective-permute-done.20.refs_5_ = bf16[128,576]{1,0:T(8,128)(2,1)S(1)} collective-permute-done((bf16[128,576]{1,0:T(8,128)(2,1)S(1)}, bf16[128,576]{1,0:T(8,128)(2,1)S(1)}, u32[]{:S(2)}, u32[]{:S(2)}) %collective-permute-start.20) | collective-permute-done | bytes 147488 | tf_op jit(solution)/shard_map/ppermute | solution.py:489
  54.1 8.5 %shard_map.179 = (f32[128,576]{1,0:T(8,128)S(1)}, f32[512,576]{1,0:T(8,128)S(1)}, bf16[4,144,384]{2,1,0:T(8,128)(2,1)S(1)}, bf16[4,144,384]{2,1,0:T(8,128)(2,1)S...) custom-call(s32[2]{0:T(128)S(1)} %pad_add_fusion.idx, ...), custom_call_target="tpu_custom_call" | custom-call | flops 6000000000 | bytes 1048576 | tf_op jit(solution)/shard_map/pallas_call | solution.py:473
  64.5 5.5 %shard_map.180 = (f32[128,576]{1,0:T(8,128)S(1)}, f32[512,576]{1,0:T(8,128)S(1)}, bf16[4,72,384]{2,1,0:T(8,128)(2,1)S(1)}, bf16[4,72,384]{2,1,0:T(8,128)(2,1)S(1)}) custom-call(s32[2]{0:T(128)S(1)} %pad_add_fusion.idx, bf16[512,576]{1,0:T(8,128)(2,1)S(1)} %get-tuple-element.50.refs_0_, f32[128,576]{1,0:T(8,128)S(1)} %get-tuple-element.59.refs_1_, ...), custom_call_target="tpu_custom_call" | custom-call | flops 6000000000 | bytes 1048576 | tf_op jit(solution)/shard_map/pallas_call | solution.py:473
  71.6 4.3 %collective-permute-done.32 = bf16[4,144,384]{2,1,0:T(8,128)(2,1)S(1)} collective-permute-done((bf16[4,144,384]{2,1,0:T(8,128)(2,1)S(1)}, bf16[4,144,384]{2,1,0:T(8,128)(2,1)S(1)}, u32[]{:S(2)}, u32[]{:S(2)}) %collective-permute-start.32) | collective-permute-done | bytes 442400 | tf_op jit(solution)/shard_map/ppermute | solution.py:489
  76.0 1.6 %collective-permute-start.33 = (bf16[2,144,384]{2,1,0:T(8,128)(2,1)S(1)}, bf16[2,144,384]{2,1,0:T(8,128)(2,1)S(1)}, u32[]{:S(2)}, u32[]{:S(2)}) collective-permute-start(bf16[2,144,384]{2,1,0:T(8,128)(2,1)S(1)} %slice.61), channel_id=1, source_target_pairs={{0,8},{4,12},{8,0},{12,4},{16,24},{20,28},{24,16},{28,20},{1,9},{5... | collective-permute-start | bytes 663560 | tf_op jit(solution)/shard_map/ppermute | solution.py:489
  77.7 13.3 %shard_map.181 = (f32[128,576]{1,0:T(8,128)S(1)}, bf16[4,56,576]{2,1,0:T(8,128)(2,1)S(1)}, bf16[4,56,576]{2,1,0:T(8,128)(2,1)S(1)}) custom-call(s32[2]{0:T(128)S(1)} %pad_add_fusion.idx, bf16[512,576]{1,0:T(8,128)(2,1)S(1)} %get-tuple-element.67.x_ref, bf16[512,576]{1,0:T(8,128)(2,1)S(1)} %get-tuple-element.68.nrm_ref, ...), custom_call_target="tpu_custom_call" | custom-call | flops 12999999488 | bytes 1048576 | tf_op jit(solution)/shard_map/pallas_call | solution.py:473
  93.3 2.7 %collective-permute-start.34 = (bf16[1,144,384]{2,1,0:T(8,128)(2,1)S(1)}, bf16[1,144,384]{2,1,0:T(8,128)(2,1)S(1)}, u32[]{:S(2)}, u32[]{:S(2)}) collective-permute-start(bf16[1,144,384]{2,1,0:T(8,128)(2,1)S(1)} %slice.63), channel_id=1, source_target_pairs={{0,16},{4,20},{8,24},{12,28},{16,0},{20,4},{24,8},{28,12},{1,17},{... | collective-permute-start | bytes 331784 | tf_op jit(solution)/shard_map/ppermute | solution.py:489
  95.9 2.6 %collective-permute-done.26 = bf16[4,56,576]{2,1,0:T(8,128)(2,1)S(1)} collective-permute-done((bf16[4,56,576]{2,1,0:T(8,128)(2,1)S(1)}, bf16[4,56,576]{2,1,0:T(8,128)(2,1)S(1)}, u32[]{:S(2)}, u32[]{:S(2)}) %collective-permute-start.26) | collective-permute-done | bytes 258080 | tf_op jit(solution)/shard_map/ppermute | solution.py:489
  99.2 2.7 %collective-permute-start.40 = (bf16[1,72,384]{2,1,0:T(8,128)(2,1)S(1)}, bf16[1,72,384]{2,1,0:T(8,128)(2,1)S(1)}, u32[]{:S(2)}, u32[]{:S(2)}) collective-permute-start(bf16[1,72,384]{2,1,0:T(8,128)(2,1)S(1)} %slice.67), channel_id=1, source_target_pairs={{0,16},{4,20},{8,24},{12,28},{16,0},{20,4},{24,8},{28,12},{1,17},{... | collective-permute-start | bytes 165896 | tf_op jit(solution)/shard_map/ppermute | solution.py:489
  101.9 2.0 %collective-permute-done.27 = bf16[2,56,576]{2,1,0:T(8,128)(2,1)S(1)} collective-permute-done((bf16[2,56,576]{2,1,0:T(8,128)(2,1)S(1)}, bf16[2,56,576]{2,1,0:T(8,128)(2,1)S(1)}, u32[]{:S(2)}, u32[]{:S(2)}) %collective-permute-start.27) | collective-permute-done | bytes 129056 | tf_op jit(solution)/shard_map/ppermute | solution.py:489
  103.9 3.2 %collective-permute-start.28 = (bf16[1,56,576]{2,1,0:T(8,128)(2,1)S(1)}, bf16[1,56,576]{2,1,0:T(8,128)(2,1)S(1)}, u32[]{:S(2)}, u32[]{:S(2)}) collective-permute-start(bf16[1,56,576]{2,1,0:T(8,128)(2,1)S(1)} %slice.59), channel_id=1, source_target_pairs={{0,16},{4,20},{8,24},{12,28},{16,0},{20,4},{24,8},{28,12},{1,17},{... | collective-permute-start | bytes 193544 | tf_op jit(solution)/shard_map/ppermute | solution.py:489
  107.2 6.2 %collective-permute-done.28 = bf16[1,56,576]{2,1,0:T(8,128)(2,1)S(1)} collective-permute-done((bf16[1,56,576]{2,1,0:T(8,128)(2,1)S(1)}, bf16[1,56,576]{2,1,0:T(8,128)(2,1)S(1)}, u32[]{:S(2)}, u32[]{:S(2)}) %collective-permute-start.28) | collective-permute-done | bytes 64544 | tf_op jit(solution)/shard_map/ppermute | solution.py:489
  113.5 3.0 %collective-permute-start.41 = (bf16[1,72,384]{2,1,0:T(8,128)(2,1)S(1)}, bf16[1,72,384]{2,1,0:T(8,128)(2,1)S(1)}, u32[]{:S(2)}, u32[]{:S(2)}) collective-permute-start(bf16[1,72,384]{2,1,0:T(8,128)(2,1)S(1)} %add_convert_fusion.8), channel_id=1, source_target_pairs={{0,16},{4,20},{8,24},{12,28},{16,0},{20,4},{24,8},{28,12},{1,17},{... | collective-permute-start | bytes 165896 | tf_op jit(solution)/shard_map/ppermute | solution.py:489
  116.4 2.9 %collective-permute-done.29 = bf16[1,56,576]{2,1,0:T(8,128)(2,1)S(1)} collective-permute-done((bf16[1,56,576]{2,1,0:T(8,128)(2,1)S(1)}, bf16[1,56,576]{2,1,0:T(8,128)(2,1)S(1)}, u32[]{:S(2)}, u32[]{:S(2)}) %collective-permute-start.29) | collective-permute-done | bytes 64544 | tf_op jit(solution)/shard_map/ppermute | solution.py:489
  119.5 2.1 %collective-permute-start.36 = (bf16[2,144,384]{2,1,0:T(8,128)(2,1)S(1)}, bf16[2,144,384]{2,1,0:T(8,128)(2,1)S(1)}, u32[]{:S(2)}, u32[]{:S(2)}) collective-permute-start(bf16[2,144,384]{2,1,0:T(8,128)(2,1)S(1)} %pad_maximum_fusion.2), channel_id=1, source_target_pairs={{0,8},{4,12},{8,0},{12,4},{16,24},{20,28},{24,16},{28,20},{1,9},{5... | collective-permute-start | bytes 663560 | tf_op jit(solution)/shard_map/ppermute | solution.py:489
  122.6 2.4 %collective-permute-done.30 = bf16[2,56,576]{2,1,0:T(8,128)(2,1)S(1)} collective-permute-done((bf16[2,56,576]{2,1,0:T(8,128)(2,1)S(1)}, bf16[2,56,576]{2,1,0:T(8,128)(2,1)S(1)}, u32[]{:S(2)}, u32[]{:S(2)}) %collective-permute-start.30) | collective-permute-done | bytes 129056 | tf_op jit(solution)/shard_map/ppermute | solution.py:489
  125.4 2.0 %collective-permute-done.36 = bf16[2,144,384]{2,1,0:T(8,128)(2,1)S(1)} collective-permute-done((bf16[2,144,384]{2,1,0:T(8,128)(2,1)S(1)}, bf16[2,144,384]{2,1,0:T(8,128)(2,1)S(1)}, u32[]{:S(2)}, u32[]{:S(2)}) %collective-permute-start.36) | collective-permute-done | bytes 221216 | tf_op jit(solution)/shard_map/ppermute | solution.py:489
  131.4 3.5 %collective-permute-done.31.second = bf16[4,56,576]{2,1,0:T(8,128)(2,1)S(1)} collective-permute-done((bf16[4,56,576]{2,1,0:T(8,128)(2,1)S(1)}, bf16[4,56,576]{2,1,0:T(8,128)(2,1)S(1)}, u32[]{:S(2)}, u32[]{:S(2)}) %collective-permute-start.31) | collective-permute-done | bytes 258080 | tf_op jit(solution)/shard_map/ppermute | solution.py:489
  134.9 1.7 %shard_map.182 = (f32[144,576]{1,0:T(8,128)}, f32[144,384]{1,0:T(8,128)}, f32[144,576]{1,0:T(8,128)}, f32[8,576]{1,0:T(8,128)S(1)}) custom-call(s32[2]{0:T(128)S(1)} %pad_add_fusion.idx, bf16[4,56,576]{2,1,0:T(8,128)(2,1)S(1)} %pad_maximum_fusion.1.first, bf16[4,56,576]{2,1,0:T(8,128)(2,1)S(1)} %collective-permute-done.31.second), custom_call_target="tpu_custom_call" | custom-call | flops 2000000000 | bytes 1048576 | tf_op jit(solution)/shard_map/pallas_call | solution.py:473
  137.3 5.8 %collective-permute-done.43.two_hi = bf16[4,72,384]{2,1,0:T(8,128)(2,1)S(1)} collective-permute-done((bf16[4,72,384]{2,1,0:T(8,128)(2,1)S(1)}, bf16[4,72,384]{2,1,0:T(8,128)(2,1)S(1)}, u32[]{:S(2)}, u32[]{:S(2)}) %collective-permute-start.43) | collective-permute-done | bytes 221216 | tf_op jit(solution)/shard_map/ppermute | solution.py:489
  143.1 2.2 %shard_map.183 = (f32[384,576]{1,0:T(8,128)S(1)}, f32[144,3072]{1,0:T(8,128)}) custom-call(s32[2]{0:T(128)S(1)} %pad_add_fusion.idx, bf16[4,144,384]{2,1,0:T(8,128)(2,1)S(1)} %pad_maximum_fusion.one_lo, bf16[4,144,384]{2,1,0:T(8,128)(2,1)S(1)} %collective-permute-done.37.one_hi, bf16[4,72,384]{2,1,0:T(8,128)(2,1)S(1)} %pad_maximum_fusion.3.two_lo, ...), custom_call_target="tpu_custom_call" | custom-call | flops 3000000000 | bytes 1048576 | tf_op jit(solution)/shard_map/pallas_call | solution.py:473
  (114 shorter events, 27.2 us)
Async XLA Ops:
  0.7 11.6 %collective-permute-start.10 = (bf16[144,384]{1,0:T(8,128)(2,1)}, bf16[144,384]{1,0:T(8,128)(2,1)S(1)}, u32[]{:S(2)}, u32[]{:S(2)}) collective-permute-start(bf16[144,384]{1,0:T(8,128)(2,1)} %bitcast.33), channel_id=1, source_target_pairs={{0,2},{1,3},{2,0},{3,1},{4,6},{5,7},{6,4},{7,5},{8,10},{9,11},{10,... | collective-permute-start | bytes 331784 | tf_op jit(solution)/shard_map/ppermute | solution.py:489
  3.7 8.6 %collective-permute-start.9 = (bf16[144,384]{1,0:T(8,128)(2,1)}, bf16[144,384]{1,0:T(8,128)(2,1)S(1)}, u32[]{:S(2)}, u32[]{:S(2)}) collective-permute-start(bf16[144,384]{1,0:T(8,128)(2,1)} %bitcast.34), channel_id=1, source_target_pairs={{0,1},{1,0},{2,3},{3,2},{4,5},{5,4},{6,7},{7,6},{8,9},{9,8},{10,11... | collective-permute-start | bytes 331784 | tf_op jit(solution)/shard_map/ppermute | solution.py:489
  10.0 7.1 %collective-permute-start.1 = (bf16[128,576]{1,0:T(8,128)(2,1)S(1)}, bf16[128,576]{1,0:T(8,128)(2,1)S(1)}, u32[]{:S(2)}, u32[]{:S(2)}) collective-permute-start(bf16[128,576]{1,0:T(8,128)(2,1)S(1)} %copy.22.refs_0_), channel_id=1, source_target_pairs={{0,2},{1,3},{2,0},{3,1},{4,6},{5,7},{6,4},{7,5},{8,10},{9,11},{10,... | collective-permute-start | bytes 442376 | tf_op jit(solution)/shard_map/ppermute | solution.py:489
  10.1 7.1 %collective-permute-start = (bf16[128,576]{1,0:T(8,128)(2,1)S(1)}, bf16[128,576]{1,0:T(8,128)(2,1)S(1)}, u32[]{:S(2)}, u32[]{:S(2)}) collective-permute-start(bf16[128,576]{1,0:T(8,128)(2,1)S(1)} %copy.22.refs_0_), channel_id=1, source_target_pairs={{0,1},{1,0},{2,3},{3,2},{4,5},{5,4},{6,7},{7,6},{8,9},{9,8},{10,11... | collective-permute-start | bytes 442376 | tf_op jit(solution)/shard_map/ppermute | solution.py:489
  10.6 10.3 %collective-permute-start.13 = (bf16[144,576]{1,0:T(8,128)(2,1)}, bf16[144,576]{1,0:T(8,128)(2,1)S(1)}, u32[]{:S(2)}, u32[]{:S(2)}) collective-permute-start(bf16[144,576]{1,0:T(8,128)(2,1)} %bitcast.30), channel_id=1, source_target_pairs={{0,2},{1,3},{2,0},{3,1},{4,6},{5,7},{6,4},{7,5},{8,10},{9,11},{10,... | collective-permute-start | bytes 497672 | tf_op jit(solution)/shard_map/ppermute | solution.py:489
  12.3 12.6 %collective-permute-start.12 = (bf16[144,576]{1,0:T(8,128)(2,1)}, bf16[144,576]{1,0:T(8,128)(2,1)S(1)}, u32[]{:S(2)}, u32[]{:S(2)}) collective-permute-start(bf16[144,576]{1,0:T(8,128)(2,1)} %bitcast.31), channel_id=1, source_target_pairs={{0,1},{1,0},{2,3},{3,2},{4,5},{5,4},{6,7},{7,6},{8,9},{9,8},{10,11... | collective-permute-start | bytes 497672 | tf_op jit(solution)/shard_map/ppermute | solution.py:489
  12.3 12.6 %collective-permute-start.7 = (bf16[144,576]{1,0:T(8,128)(2,1)}, bf16[144,576]{1,0:T(8,128)(2,1)S(1)}, u32[]{:S(2)}, u32[]{:S(2)}) collective-permute-start(bf16[144,576]{1,0:T(8,128)(2,1)} %bitcast.27), channel_id=1, source_target_pairs={{0,2},{1,3},{2,0},{3,1},{4,6},{5,7},{6,4},{7,5},{8,10},{9,11},{10,... | collective-permute-start | bytes 497672 | tf_op jit(solution)/shard_map/ppermute | solution.py:489
  17.0 17.4 %collective-permute-start.15 = (bf16[144,1536]{1,0:T(8,128)(2,1)}, bf16[144,1536]{1,0:T(8,128)(2,1)S(1)}, u32[]{:S(2)}, u32[]{:S(2)}) collective-permute-start(bf16[144,1536]{1,0:T(8,128)(2,1)} %dynamic-slice_bitcast_fusion), channel_id=1, source_target_pairs={{0,2},{1,3},{2,0},{3,1},{4,6},{5,7},{6,4},{7,5},{8,10},{9,11},{10,... | collective-permute-start | bytes 1327112 | tf_op jit(solution)/shard_map/ppermute | solution.py:489
  17.2 9.6 %collective-permute-start.6 = (bf16[144,576]{1,0:T(8,128)(2,1)S(1)}, bf16[144,576]{1,0:T(8,128)(2,1)S(1)}, u32[]{:S(2)}, u32[]{:S(2)}) collective-permute-start(bf16[144,576]{1,0:T(8,128)(2,1)S(1)} %bitcast.28), channel_id=1, source_target_pairs={{0,1},{1,0},{2,3},{3,2},{4,5},{5,4},{6,7},{7,6},{8,9},{9,8},{10,11... | collective-permute-start | bytes 497672 | tf_op jit(solution)/shard_map/ppermute | solution.py:489
  21.0 7.4 %collective-permute-start.2 = (bf16[128,576]{1,0:T(8,128)(2,1)S(1)}, bf16[128,576]{1,0:T(8,128)(2,1)S(1)}, u32[]{:S(2)}, u32[]{:S(2)}) collective-permute-start(bf16[128,576]{1,0:T(8,128)(2,1)S(1)} %collective-permute-done.1.refs_2_), channel_id=1, source_target_pairs={{0,1},{1,0},{2,3},{3,2},{4,5},{5,4},{6,7},{7,6},{8,9},{9,8},{10,11... | collective-permute-start | bytes 442376 | tf_op jit(solution)/shard_map/ppermute | solution.py:489
  24.9 11.0 %collective-permute-start.14 = (bf16[144,576]{1,0:T(8,128)(2,1)S(1)}, bf16[144,576]{1,0:T(8,128)(2,1)S(1)}, u32[]{:S(2)}, u32[]{:S(2)}) collective-permute-start(bf16[144,576]{1,0:T(8,128)(2,1)S(1)} %collective-permute-done.13.refs_18_), channel_id=1, source_target_pairs={{0,1},{1,0},{2,3},{3,2},{4,5},{5,4},{6,7},{7,6},{8,9},{9,8},{10,11... | collective-permute-start | bytes 497672 | tf_op jit(solution)/shard_map/ppermute | solution.py:489
  24.9 11.0 %collective-permute-start.8 = (bf16[144,576]{1,0:T(8,128)(2,1)S(1)}, bf16[144,576]{1,0:T(8,128)(2,1)S(1)}, u32[]{:S(2)}, u32[]{:S(2)}) collective-permute-start(bf16[144,576]{1,0:T(8,128)(2,1)S(1)} %collective-permute-done.7.refs_10_), channel_id=1, source_target_pairs={{0,1},{1,0},{2,3},{3,2},{4,5},{5,4},{6,7},{7,6},{8,9},{9,8},{10,11... | collective-permute-start | bytes 497672 | tf_op jit(solution)/shard_map/ppermute | solution.py:489
  28.2 15.0 %collective-permute-start.17 = (bf16[128,576]{1,0:T(8,128)(2,1)S(1)}, bf16[128,576]{1,0:T(8,128)(2,1)S(1)}, u32[]{:S(2)}, u32[]{:S(2)}) collective-permute-start(bf16[128,576]{1,0:T(8,128)(2,1)S(1)} %multiply_convert_fusion.refs_4_), channel_id=1, source_target_pairs={{0,2},{1,3},{2,0},{3,1},{4,6},{5,7},{6,4},{7,5},{8,10},{9,11},{10,... | collective-permute-start | bytes 442376 | tf_op jit(solution)/shard_map/ppermute | solution.py:489
  28.4 19.7 %collective-permute-start.18 = (bf16[384,576]{1,0:T(8,128)(2,1)S(1)}, bf16[384,576]{1,0:T(8,128)(2,1)S(1)}, u32[]{:S(2)}, u32[]{:S(2)}) collective-permute-start(bf16[384,576]{1,0:T(8,128)(2,1)S(1)} %bitcast.22), channel_id=1, source_target_pairs={{0,2},{1,3},{2,0},{3,1},{4,6},{5,7},{6,4},{7,5},{8,10},{9,11},{10,... | collective-permute-start | bytes 1327112 | tf_op jit(solution)/shard_map/ppermute | solution.py:489
  34.4 13.7 %collective-permute-start.16 = (bf16[144,1536]{1,0:T(8,128)(2,1)S(1)}, bf16[144,1536]{1,0:T(8,128)(2,1)S(1)}, u32[]{:S(2)}, u32[]{:S(2)}) collective-permute-start(bf16[144,1536]{1,0:T(8,128)(2,1)S(1)} %collective-permute-done.15.refs_10_), channel_id=1, source_target_pairs={{0,4},{4,0},{8,12},{12,8},{16,20},{20,16},{24,28},{28,24},{1,5},{5... | collective-permute-start | bytes 1327112 | tf_op jit(solution)/shard_map/ppermute | solution.py:489
  48.1 6.0 %collective-permute-start.22 = (bf16[144,3072]{1,0:T(8,128)(2,1)S(1)}, bf16[144,3072]{1,0:T(8,128)(2,1)S(1)}, u32[]{:S(2)}, u32[]{:S(2)}) collective-permute-start(bf16[144,3072]{1,0:T(8,128)(2,1)S(1)} %bitcast.25), channel_id=1, source_target_pairs={{0,1},{1,0},{2,3},{3,2},{4,5},{5,4},{6,7},{7,6},{8,9},{9,8},{10,11... | collective-permute-start | bytes 2654216 | tf_op jit(solution)/shard_map/ppermute | solution.py:489
  48.1 6.0 %collective-permute-start.19 = (bf16[384,576]{1,0:T(8,128)(2,1)S(1)}, bf16[384,576]{1,0:T(8,128)(2,1)S(1)}, u32[]{:S(2)}, u32[]{:S(2)}) collective-permute-start(bf16[384,576]{1,0:T(8,128)(2,1)S(1)} %bitcast.23), channel_id=1, source_target_pairs={{0,1},{1,0},{2,3},{3,2},{4,5},{5,4},{6,7},{7,6},{8,9},{9,8},{10,11... | collective-permute-start | bytes 1327112 | tf_op jit(solution)/shard_map/ppermute | solution.py:489
  62.8 13.1 %collective-permute-start.32 = (bf16[4,144,384]{2,1,0:T(8,128)(2,1)S(1)}, bf16[4,144,384]{2,1,0:T(8,128)(2,1)S(1)}, u32[]{:S(2)}, u32[]{:S(2)}) collective-permute-start(bf16[4,144,384]{2,1,0:T(8,128)(2,1)S(1)} %get-tuple-element.85), channel_id=1, source_target_pairs={{0,4},{4,0},{8,12},{12,8},{16,20},{20,16},{24,28},{28,24},{1,5},{5... | collective-permute-start | bytes 1327112 | tf_op jit(solution)/shard_map/ppermute | solution.py:489
  70.0 22.6 %collective-permute-start.38 = (bf16[4,72,384]{2,1,0:T(8,128)(2,1)S(1)}, bf16[4,72,384]{2,1,0:T(8,128)(2,1)S(1)}, u32[]{:S(2)}, u32[]{:S(2)}) collective-permute-start(bf16[4,72,384]{2,1,0:T(8,128)(2,1)S(1)} %get-tuple-element.87), channel_id=1, source_target_pairs={{0,4},{4,0},{8,12},{12,8},{16,20},{20,16},{24,28},{28,24},{1,5},{5... | collective-permute-start | bytes 663560 | tf_op jit(solution)/shard_map/ppermute | solution.py:489
  76.0 17.2 %collective-permute-start.33 = (bf16[2,144,384]{2,1,0:T(8,128)(2,1)S(1)}, bf16[2,144,384]{2,1,0:T(8,128)(2,1)S(1)}, u32[]{:S(2)}, u32[]{:S(2)}) collective-permute-start(bf16[2,144,384]{2,1,0:T(8,128)(2,1)S(1)} %slice.61), channel_id=1, source_target_pairs={{0,8},{4,12},{8,0},{12,4},{16,24},{20,28},{24,16},{28,20},{1,9},{5... | collective-permute-start | bytes 663560 | tf_op jit(solution)/shard_map/ppermute | solution.py:489
  91.0 7.5 %collective-permute-start.26 = (bf16[4,56,576]{2,1,0:T(8,128)(2,1)S(1)}, bf16[4,56,576]{2,1,0:T(8,128)(2,1)S(1)}, u32[]{:S(2)}, u32[]{:S(2)}) collective-permute-start(bf16[4,56,576]{2,1,0:T(8,128)(2,1)S(1)} %get-tuple-element.80), channel_id=1, source_target_pairs={{0,4},{4,0},{8,12},{12,8},{16,20},{20,16},{24,28},{28,24},{1,5},{5... | collective-permute-start | bytes 774152 | tf_op jit(solution)/shard_map/ppermute | solution.py:489
  92.7 6.5 %collective-permute-start.39 = (bf16[2,72,384]{2,1,0:T(8,128)(2,1)S(1)}, bf16[2,72,384]{2,1,0:T(8,128)(2,1)S(1)}, u32[]{:S(2)}, u32[]{:S(2)}) collective-permute-start(bf16[2,72,384]{2,1,0:T(8,128)(2,1)S(1)} %slice.65), channel_id=1, source_target_pairs={{0,8},{4,12},{8,0},{12,4},{16,24},{20,28},{24,16},{28,20},{1,9},{5... | collective-permute-start | bytes 331784 | tf_op jit(solution)/shard_map/ppermute | solution.py:489
  93.3 13.7 %collective-permute-start.34 = (bf16[1,144,384]{2,1,0:T(8,128)(2,1)S(1)}, bf16[1,144,384]{2,1,0:T(8,128)(2,1)S(1)}, u32[]{:S(2)}, u32[]{:S(2)}) collective-permute-start(bf16[1,144,384]{2,1,0:T(8,128)(2,1)S(1)} %slice.63), channel_id=1, source_target_pairs={{0,16},{4,20},{8,24},{12,28},{16,0},{20,4},{24,8},{28,12},{1,17},{... | collective-permute-start | bytes 331784 | tf_op jit(solution)/shard_map/ppermute | solution.py:489
  99.2 14.3 %collective-permute-start.40 = (bf16[1,72,384]{2,1,0:T(8,128)(2,1)S(1)}, bf16[1,72,384]{2,1,0:T(8,128)(2,1)S(1)}, u32[]{:S(2)}, u32[]{:S(2)}) collective-permute-start(bf16[1,72,384]{2,1,0:T(8,128)(2,1)S(1)} %slice.67), channel_id=1, source_target_pairs={{0,16},{4,20},{8,24},{12,28},{16,0},{20,4},{24,8},{28,12},{1,17},{... | collective-permute-start | bytes 165896 | tf_op jit(solution)/shard_map/ppermute | solution.py:489
  103.9 9.5 %collective-permute-start.28 = (bf16[1,56,576]{2,1,0:T(8,128)(2,1)S(1)}, bf16[1,56,576]{2,1,0:T(8,128)(2,1)S(1)}, u32[]{:S(2)}, u32[]{:S(2)}) collective-permute-start(bf16[1,56,576]{2,1,0:T(8,128)(2,1)S(1)} %slice.59), channel_id=1, source_target_pairs={{0,16},{4,20},{8,24},{12,28},{16,0},{20,4},{24,8},{28,12},{1,17},{... | collective-permute-start | bytes 193544 | tf_op jit(solution)/shard_map/ppermute | solution.py:489
  107.1 12.4 %collective-permute-start.35 = (bf16[1,144,384]{2,1,0:T(8,128)(2,1)S(1)}, bf16[1,144,384]{2,1,0:T(8,128)(2,1)S(1)}, u32[]{:S(2)}, u32[]{:S(2)}) collective-permute-start(bf16[1,144,384]{2,1,0:T(8,128)(2,1)S(1)} %add_convert_fusion.6), channel_id=1, source_target_pairs={{0,16},{4,20},{8,24},{12,28},{16,0},{20,4},{24,8},{28,12},{1,17},{... | collective-permute-start | bytes 331784 | tf_op jit(solution)/shard_map/ppermute | solution.py:489
  113.5 8.1 %collective-permute-start.41 = (bf16[1,72,384]{2,1,0:T(8,128)(2,1)S(1)}, bf16[1,72,384]{2,1,0:T(8,128)(2,1)S(1)}, u32[]{:S(2)}, u32[]{:S(2)}) collective-permute-start(bf16[1,72,384]{2,1,0:T(8,128)(2,1)S(1)} %add_convert_fusion.8), channel_id=1, source_target_pairs={{0,16},{4,20},{8,24},{12,28},{16,0},{20,4},{24,8},{28,12},{1,17},{... | collective-permute-start | bytes 165896 | tf_op jit(solution)/shard_map/ppermute | solution.py:489
  119.5 7.9 %collective-permute-start.36 = (bf16[2,144,384]{2,1,0:T(8,128)(2,1)S(1)}, bf16[2,144,384]{2,1,0:T(8,128)(2,1)S(1)}, u32[]{:S(2)}, u32[]{:S(2)}) collective-permute-start(bf16[2,144,384]{2,1,0:T(8,128)(2,1)S(1)} %pad_maximum_fusion.2), channel_id=1, source_target_pairs={{0,8},{4,12},{8,0},{12,4},{16,24},{20,28},{24,16},{28,20},{1,9},{5... | collective-permute-start | bytes 663560 | tf_op jit(solution)/shard_map/ppermute | solution.py:489
  121.6 8.3 %collective-permute-start.42 = (bf16[2,72,384]{2,1,0:T(8,128)(2,1)S(1)}, bf16[2,72,384]{2,1,0:T(8,128)(2,1)S(1)}, u32[]{:S(2)}, u32[]{:S(2)}) collective-permute-start(bf16[2,72,384]{2,1,0:T(8,128)(2,1)S(1)} %pad_maximum_fusion.5), channel_id=1, source_target_pairs={{0,8},{4,12},{8,0},{12,4},{16,24},{20,28},{24,16},{28,20},{1,9},{5... | collective-permute-start | bytes 331784 | tf_op jit(solution)/shard_map/ppermute | solution.py:489
  125.1 9.8 %collective-permute-start.31 = (bf16[4,56,576]{2,1,0:T(8,128)(2,1)S(1)}, bf16[4,56,576]{2,1,0:T(8,128)(2,1)S(1)}, u32[]{:S(2)}, u32[]{:S(2)}) collective-permute-start(bf16[4,56,576]{2,1,0:T(8,128)(2,1)S(1)} %pad_maximum_fusion.1.first), channel_id=1, source_target_pairs={{0,4},{4,0},{8,12},{12,8},{16,20},{20,16},{24,28},{28,24},{1,5},{5... | collective-permute-start | bytes 774152 | tf_op jit(solution)/shard_map/ppermute | solution.py:489
  127.5 15.6 %collective-permute-start.37 = (bf16[4,144,384]{2,1,0:T(8,128)(2,1)S(1)}, bf16[4,144,384]{2,1,0:T(8,128)(2,1)S(1)}, u32[]{:S(2)}, u32[]{:S(2)}) collective-permute-start(bf16[4,144,384]{2,1,0:T(8,128)(2,1)S(1)} %pad_maximum_fusion.one_lo), channel_id=1, source_target_pairs={{0,4},{4,0},{8,12},{12,8},{16,20},{20,16},{24,28},{28,24},{1,5},{5... | collective-permute-start | bytes 1327112 | tf_op jit(solution)/shard_map/ppermute | solution.py:489
  129.9 13.2 %collective-permute-start.43 = (bf16[4,72,384]{2,1,0:T(8,128)(2,1)S(1)}, bf16[4,72,384]{2,1,0:T(8,128)(2,1)S(1)}, u32[]{:S(2)}, u32[]{:S(2)}) collective-permute-start(bf16[4,72,384]{2,1,0:T(8,128)(2,1)S(1)} %pad_maximum_fusion.3.two_lo), channel_id=1, source_target_pairs={{0,4},{4,0},{8,12},{12,8},{16,20},{20,16},{24,28},{28,24},{1,5},{5... | collective-permute-start | bytes 663560 | tf_op jit(solution)/shard_map/ppermute | solution.py:489
  (19 other events, 162.6 us)

commit v3 on v2

v3 whole, which is shorter than its diff:
```python
import functools

import jax
import jax.numpy as jnp
from jax import lax
from jax.experimental import pallas as pl
from jax.experimental.pallas import tpu as pltpu
from jax.sharding import PartitionSpec as P

HEADS = 9
KVH = 3
HD = 64
LEN = 64
norm_eps = 1e-05
rope_base = 100000.0

BLOCK = 128
PAIRS = 5
QW = PAIRS * 128
GROUP = 4
PREPARE_VMEM = 60
MICROS = (7, 6, 6, 3, 4, 4)
F32 = jnp.float32
BF16 = jnp.bfloat16


def mm(left, right):
    return jnp.dot(left, right, preferred_element_type=F32)


def mm_nt(left, right):
    return lax.dot_general(left, right, (((1,), (1,)), ((), ())), preferred_element_type=F32)


def mm_tn(left, right):
    return lax.dot_general(left, right, (((0,), (0,)), ((), ())), preferred_element_type=F32)


def inverse_rms(stream):
    return lax.rsqrt(jnp.mean(stream * stream, axis=-1, keepdims=True) + norm_eps)


def lane_index(shape):
    return lax.broadcasted_iota(jnp.int32, shape, 1)


def own_columns(shard, rows, width):
    row = lax.broadcasted_iota(jnp.int32, (rows, width), 0)
    column = lax.broadcasted_iota(jnp.int32, (rows, width), 1)
    return (row == column + shard * width).astype(BF16)


def swapped(values, first_half):
    return jnp.where(first_half, pltpu.roll(values, 96, 1), pltpu.roll(values, 32, 1))


def split_heads(keyval):
    low = lane_index((BLOCK, 128)) < HD
    slices = [keyval[:, 128 * part : 128 * part + 128].astype(F32) for part in range(3)]

    def pair(piece, is_low):
        kept = jnp.where(low, piece, 0.0) if is_low else jnp.where(low, 0.0, piece)
        moved = pltpu.roll(kept, HD, 1)
        kept, moved = kept.astype(BF16), moved.astype(BF16)
        return (kept, moved) if is_low else (moved, kept)

    keys = [pair(slices[0], True), pair(slices[0], False), pair(slices[1], True)]
    values = [pair(slices[1], False), pair(slices[2], True), pair(slices[2], False)]
    return keys, values


def pair_operand(parts, pair):
    first = parts[(2 * pair) * KVH // HEADS][0]
    if 2 * pair + 1 >= HEADS:
        return first
    return jnp.concatenate([first, parts[(2 * pair + 1) * KVH // HEADS][1]], axis=0)


def attention_mask():
    query = lax.broadcasted_iota(jnp.int32, (BLOCK, BLOCK), 0)
    key = lax.broadcasted_iota(jnp.int32, (BLOCK, BLOCK), 1)
    return (query // LEN == key // LEN) & (query >= key)


def soft_rows(scores, allowed):
    halves = []
    for start in range(0, scores.shape[1], BLOCK):
        part = jnp.where(allowed, scores[:, start : start + BLOCK], -1e30)
        part = jnp.exp(part - jnp.max(part, axis=-1, keepdims=True))
        halves.append(part * (1.0 / jnp.sum(part, axis=-1, keepdims=True)))
    return halves


def joined(halves):
    return halves[0] if len(halves) == 1 else jnp.concatenate(halves, axis=1)


def prepare_kernel(idx, wq, wkv, wo, wgu, tokens, grad, positions, gain_attn, gain_mlp,
                   own_ref, send_ref, gu_ref, cot_ref, kv_all, tok_all, grad_all, codes, sem):
    width, kv_width = wkv.shape
    model = own_ref.shape[1]
    side = idx[1] & 1
    ff = gu_ref.shape[1]
    across = pl.ds(pl.multiple_of(side * ff, 128), ff)
    waits = [
        pltpu.make_async_copy(wkv, kv_all, sem.at[0]),
        pltpu.make_async_copy(wq, own_ref.at[pl.ds(0, width)], sem.at[1]),
        pltpu.make_async_copy(wo, own_ref.at[pl.ds(width, width)], sem.at[2]),
        pltpu.make_async_copy(tokens, tok_all, sem.at[3]),
        pltpu.make_async_copy(grad, grad_all, sem.at[4]),
        pltpu.make_async_copy(wgu.at[:, across], gu_ref, sem.at[5]),
    ]
    for wait in waits:
        wait.start()
    count = send_ref.shape[0] - BLOCK - 16
    codes[...] = jnp.zeros_like(codes)
    codes[0:1, :BLOCK] = (positions[...] >> 6).astype(F32)
    codes[1:2, :BLOCK] = (positions[...] & 63).astype(F32)
    codes[2:3, :width] = gain_attn[...].astype(F32)
    codes[3:4, :width] = gain_mlp[...].astype(F32)
    small = codes[...].astype(BF16)
    own_ref[2 * count + BLOCK :, :] = small
    send_ref[count + BLOCK :, :] = small
    rest = model - kv_width
    top = width - width * rest // model
    waits[0].wait()
    own_ref[2 * width : 2 * count, :kv_width] = kv_all[:top, :]
    own_ref[2 * width : 3 * width - top, kv_width:] = kv_all[top:, :rest]
    own_ref[3 * width - top : 2 * count, kv_width:] = kv_all[top:, rest:]
    waits[3].wait()
    rows = tok_all[...].T
    own_ref[2 * count : 2 * count + BLOCK, :] = rows
    send_ref[count : count + BLOCK, :] = rows
    waits[1].wait()
    waits[2].wait()
    send_ref[:count, :] = own_ref[pl.ds(pl.multiple_of(side * count, 16), count), :]
    waits[4].wait()
    cot_ref[...] = (grad_all[...].T.astype(F32) * live_rows(idx)).astype(BF16)
    waits[5].wait()


def live_rows(idx):
    slot = lax.broadcasted_iota(jnp.int32, (BLOCK, 1), 0) // LEN
    return (slot < idx[2]).astype(F32)


def attn_forward_kernel(n_shard, idx, *refs):
    packs = refs[:6]
    (x_ref, nrm_ref, q_ref, kv_ref, mix_ref, mid_ref, nmid_ref, cos_ref, sin_ref, gain_ref,
     wq_full, wkv_full, wo_full, query_all, keyval_all, pack_all, small, sem, tok_sem, small_sem) = refs[6:]
    shard = idx[0]
    side = idx[1] & 1
    model = x_ref.shape[1]
    width = model // n_shard
    count = pack_all.shape[1] // 2
    waits = []
    pieces = [(0, packs[0], None), (1, packs[1], None), (2, packs[2], side), (2, packs[3], 1 - side),
              (3, packs[4], side), (3, packs[5], 1 - side)]
    for number, (part, source, which) in enumerate(pieces):
        target = pack_all.at[part]
        size = 2 * count
        if which is not None:
            target = pack_all.at[part, pl.ds(pl.multiple_of(which * count, 16), count)]
            size = count
        waits.append(pltpu.make_async_copy(source.at[pl.ds(0, size)], target, sem.at[number]))
        if number not in (3, 5):
            tokens_to = x_ref.at[pl.ds(part * BLOCK, BLOCK)]
            waits.append(pltpu.make_async_copy(source.at[pl.ds(size, BLOCK)], tokens_to, tok_sem.at[part]))
            rest = source.at[pl.ds(size + BLOCK, 16)]
            waits.append(pltpu.make_async_copy(rest, small.at[part], small_sem.at[part]))
    for wait in waits:
        wait.start()
    wq_full[:, model:] = jnp.zeros((model, QW - model), BF16)
    wo_full[model:, :] = jnp.zeros((QW - model, model), BF16)
    for wait in waits:
        wait.wait()
    gains = jnp.zeros((16, model), F32)
    kv_width = wkv_full.shape[1]
    rest = model - kv_width
    top = width - width * rest // model
    for part in range(n_shard):
        at = pl.multiple_of((shard ^ part) * width, 16)
        wq_full[pl.ds(at, width), :model] = pack_all[part, :width, :]
        wo_full[pl.ds(at, width), :] = pack_all[part, width : 2 * width, :]
        wkv_full[pl.ds(at, top), :] = pack_all[part, 2 * width :, :kv_width]
        low = pl.ds(pl.multiple_of(at + top, 16), width - top)
        wkv_full[low, :rest] = pack_all[part, 2 * width : 3 * width - top, model - rest :]
        wkv_full[low, rest:] = pack_all[part, 3 * width - top :, model - rest :]
        row = lax.broadcasted_iota(jnp.int32, (256, model), 0)
        column = lax.broadcasted_iota(jnp.int32, (256, model), 1)
        place = ((column == row + at) & (row < width)).astype(BF16)
        gains = gains + mm(small[part, :, :256], place)
    gain_ref[...] = gains
    half = HD // 2
    step = lax.broadcasted_iota(jnp.int32, (half, 1), 0).astype(F32)
    frequency = jnp.exp(step * (-2.0 / HD * jnp.log(F32(rope_base))))
    for part in range(n_shard):
        codes = small[part].astype(F32)
        position = codes[0:1, :BLOCK] * 64.0 + codes[1:2, :BLOCK]
        angle = frequency * position
        rows = pl.ds(part * BLOCK, BLOCK)
        cos_ref[rows, :] = jnp.concatenate([jnp.cos(angle)] * 4, axis=0).T
        sin_ref[rows, :] = jnp.concatenate([jnp.sin(angle)] * 4, axis=0).T
    allowed = attention_mask()
    lane = lane_index((BLOCK, 128))
    first_half = lane % HD < half
    gain_attn = gains[2:3, :]
    gain_mlp = gains[3:4, :]

    for part in range(n_shard):
        rows = pl.ds(part * BLOCK, BLOCK)
        stream = x_ref[rows, :].astype(F32)
        nrm_ref[rows, :] = (stream * inverse_rms(stream) * gain_attn).astype(BF16)
    query_all[...] = mm(nrm_ref[...], wq_full[...])
    keyval_all[...] = mm(nrm_ref[...], wkv_full[...])

    heads = []
    for number in range(n_shard):
        rows = pl.ds(number * BLOCK, BLOCK)
        cosine = cos_ref[rows, :]
        sine = sin_ref[rows, :]
        sine = jnp.where(first_half, -sine, sine)

        def rope(values):
            return values * cosine + swapped(values, first_half) * sine

        kv_ref[rows, :128] = rope(keyval_all[rows, :128]).astype(BF16)
        second = keyval_all[rows, 128:256]
        kv_ref[rows, 128:256] = jnp.where(lane < HD, rope(second), second).astype(BF16)
        kv_ref[rows, 256:] = keyval_all[rows, 256:].astype(BF16)
        for pair in range(PAIRS):
            columns = slice(128 * pair, 128 * pair + 128)
            q_ref[rows, columns] = (rope(query_all[rows, columns]) * HD ** (-0.5)).astype(BF16)
        heads.append(split_heads(kv_ref[rows, :]))
    for start in range(0, n_shard, GROUP):
        units = [(number, pair) for number in range(start, start + GROUP) for pair in range(PAIRS)]
        scores, probs = {}, {}
        for number, pair in units:
            query = q_ref[number * BLOCK : (number + 1) * BLOCK, 128 * pair : 128 * pair + 128]
            scores[number, pair] = mm_nt(query, pair_operand(heads[number][0], pair))
        for unit in units:
            probs[unit] = joined(soft_rows(scores[unit], allowed)).astype(BF16)
        for number, pair in units:
            mixed = mm(probs[number, pair], pair_operand(heads[number][1], pair))
            mix_ref[number * BLOCK : (number + 1) * BLOCK, 128 * pair : 128 * pair + 128] = mixed.astype(BF16)
    stream_mid = x_ref[...].astype(F32) + mm(mix_ref[...], wo_full[...])
    mid_ref[...] = stream_mid
    nmid_ref[...] = (stream_mid * inverse_rms(stream_mid) * gain_mlp).astype(BF16)


def bit_reverse(value, total):
    result = jnp.zeros_like(value)
    bit = 1
    while bit < total:
        result = result * 2 + (value & 1)
        value = value >> 1
        bit *= 2
    return result


def spread(target, member, n_rep, first_row, slab, value):
    to = bit_reverse(member ^ slab, n_rep)
    target[to, first_row : first_row + value.shape[0], :] = value.astype(BF16)


def mlp_kernel(n_shard, n_rep, first_call, idx, *refs):
    if first_call:
        (nmid_ref, mid_ref, wd_own, wd_other), cot, wgu = refs[:4], refs[4 : 4 + n_shard], refs[4 + n_shard : -13]
        (act_ref, dn_ref, lo_ref, hi_ref, dcot_ref, w_full, own_ref, all_ref, wd_pair, wide_ref, sem, wd_sem,
         cot_sem) = refs[-13:]
    else:
        (nmid_ref, act_in, wd_own, wd_other, dcot_ref, w_full, own_ref, dn_in, act_ref, dn_ref, lo_ref,
         hi_ref, all_ref, wd_pair, wd_sem) = refs
    shard = idx[0]
    member = idx[1]
    first = 0 if first_call else 2
    model = nmid_ref.shape[1]
    ff = w_full.shape[1] // 2
    chunk = ff // n_shard
    waits = []
    for part, source in ((first, wd_own), (first + 1, wd_other)):
        at = pl.multiple_of(((shard ^ part) & 1) * chunk, 128)
        waits.append(pltpu.make_async_copy(source, wd_pair.at[:, pl.ds(at, chunk)], wd_sem.at[part - first]))
    if first_call:
        width = model // n_shard
        side = member & 1
        pieces = [(0, wgu[0], None), (1, wgu[1], None), (2, wgu[2], side), (2, wgu[3], 1 - side),
                  (3, wgu[4], side), (3, wgu[5], 1 - side)]
        for number, (part, source, which) in enumerate(pieces):
            down = pl.ds(pl.multiple_of((shard ^ part) * width, 16), width)
            if which is None:
                target = w_full.at[down]
            else:
                target = w_full.at[down, pl.ds(pl.multiple_of(which * ff, 128), ff)]
            waits.append(pltpu.make_async_copy(source, target, sem.at[number]))
        for part in range(n_shard):
            waits.append(
                pltpu.make_async_copy(cot[part], dcot_ref.at[pl.ds(part * BLOCK, BLOCK)], cot_sem.at[part])
            )
    for wait in waits:
        wait.start()
    if first_call:
        own_ref[...] = mm(nmid_ref[...], own_columns(shard, model, width)).astype(BF16)
    for wait in waits:
        wait.wait()
    normed_mid = nmid_ref[...]
    d_branch = dcot_ref[...]
    base = ((shard ^ first) >> 1) * 2 * chunk
    gate_at = pl.ds(pl.multiple_of(base, 256), 2 * chunk)
    up_at = pl.ds(pl.multiple_of(base + ff, 256), 2 * chunk)
    gate = mm(normed_mid, w_full[:, gate_at])
    up = mm(normed_mid, w_full[:, up_at])
    d_hidden = mm(d_branch, wd_pair[...])
    sigmoid = 0.5 * jnp.tanh(0.5 * gate) + 0.5
    silu = gate * sigmoid
    hidden = (silu * up).astype(BF16)
    d_gate = (d_hidden * up * sigmoid * (1.0 + gate * (1.0 - sigmoid))).astype(BF16)
    d_up = (d_hidden * silu).astype(BF16)
    rows = all_ref.shape[1]
    if first_call:
        wide_ref[...] = hidden
        own_hidden = wide_ref[:, pl.ds(pl.multiple_of((shard & 1) * chunk, 128), chunk)]
        rows = rows // 2
        grad_down = mm_tn(d_branch, own_hidden)
        for slab in range(n_rep):
            spread(all_ref, member, n_rep, rows, slab, grad_down[slab * rows : (slab + 1) * rows])
    slab = 0
    for piece in (d_gate, d_up):
        grad = mm_tn(own_ref[...], piece)
        for column in range(0, 2 * chunk, chunk):
            for row in range(0, grad.shape[0], rows):
                spread(all_ref, member, n_rep, 0, slab, grad[row : row + rows, column : column + chunk])
                slab += 1
    middle = n_rep // 2
    lo_ref[...] = all_ref[:middle]
    hi_ref[...] = all_ref[middle:]
    d_normed = mm_nt(d_gate, w_full[:, gate_at]) + mm_nt(d_up, w_full[:, up_at])
    added = mm_nt(hidden[:BLOCK], wd_pair[...])
    if first_call:
        dn_ref[...] = d_normed
        act_ref[...] = mid_ref[:BLOCK, :] + added
    else:
        dn_ref[...] = dn_in[...] + d_normed
        act_ref[...] = ((act_in[...] + added) * live_rows(idx)).T


def residual_backward_kernel(n_shard, idx, mid_ref, dn_ref, dcot_ref, mix_ref, gain_ref, wo_full,
                             dattn_ref, dmix_ref, dmid_ref, gout_ref, gain_out):
    model = mid_ref.shape[1]
    stream_mid = mid_ref[...]
    inv_mlp = inverse_rms(stream_mid)
    d_normed_mid = dn_ref[...]
    sum_mlp = jnp.sum(d_normed_mid * stream_mid * inv_mlp, axis=0, keepdims=True)
    scaled = d_normed_mid * gain_ref[3:4, :]
    d_mid = (
        dcot_ref[...].astype(F32)
        + inv_mlp * scaled
        - inv_mlp**3 * stream_mid * jnp.mean(scaled * stream_mid, axis=-1, keepdims=True)
    )
    dmid_ref[...] = d_mid[:BLOCK, :]
    dattn_ref[...] = d_mid.astype(BF16)
    dmix_ref[...] = mm_nt(dattn_ref[...], wo_full[...]).astype(BF16)
    own_mixed = mm(mix_ref[:, :model], own_columns(idx[0], model, gout_ref.shape[0])).astype(BF16)
    gout_ref[...] = mm_tn(own_mixed, dattn_ref[...])
    gain_out[...] = jnp.broadcast_to(sum_mlp, gain_out.shape)


def heads_backward_kernel(first_row, idx, q_ref, kv_ref, dmix_ref, cos_ref, sin_ref, dq_ref, dkv_ref):
    half = HD // 2
    allowed = attention_mask()
    lane = lane_index((BLOCK, 128))
    first_half = lane % HD < half
    low = lane < HD
    blocks = range(dq_ref.shape[0] // BLOCK)
    units = [(number, pair) for number in blocks for pair in range(PAIRS)]
    rows = [pl.ds(first_row + number * BLOCK, BLOCK) for number in blocks]
    columns = [slice(128 * pair, 128 * pair + 128) for pair in range(PAIRS)]
    heads = [split_heads(kv_ref[rows[number], :]) for number in blocks]
    scores, d_probs = {}, {}
    for number, pair in units:
        keys, values = heads[number]
        scores[number, pair] = mm_nt(q_ref[rows[number], columns[pair]], pair_operand(keys, pair))
        d_probs[number, pair] = mm_nt(dmix_ref[rows[number], columns[pair]], pair_operand(values, pair))
    probs, d_scores = {}, {}
    for unit in units:
        soft = soft_rows(scores[unit], allowed)
        probs[unit] = joined(soft).astype(BF16)
        d_soft = []
        for side, part in enumerate(soft):
            d_part = d_probs[unit][:, side * BLOCK : (side + 1) * BLOCK]
            d_soft.append(part * (d_part - jnp.sum(d_part * part, axis=-1, keepdims=True)))
        d_scores[unit] = joined(d_soft).astype(BF16)
    d_query, d_key_pair, d_value_pair = {}, {}, {}
    for number, pair in units:
        keys, _ = heads[number]
        d_query[number, pair] = mm(d_scores[number, pair], pair_operand(keys, pair))
        d_key_pair[number, pair] = mm_tn(d_scores[number, pair], q_ref[rows[number], columns[pair]])
        d_value_pair[number, pair] = mm_tn(probs[number, pair], dmix_ref[rows[number], columns[pair]])

    def collected(pieces, number, head, to_low):
        sides = [None, None]
        for query_head in range(HEADS):
            if query_head * KVH // HEADS == head:
                pair, side = divmod(query_head, 2)
                piece = pieces[number, pair][side * BLOCK : (side + 1) * BLOCK]
                sides[side] = piece if sides[side] is None else sides[side] + piece
        keep, move = (sides[0], sides[1]) if to_low else (sides[1], sides[0])
        total = keep if move is None else keep + pltpu.roll(move, HD, 1)
        return total

    for number in blocks:
        cosine = cos_ref[rows[number], :]
        sine = sin_ref[rows[number], :]
        sine = jnp.where(first_half, sine, -sine)

        def rope_back(grad):
            return grad * cosine + swapped(grad, first_half) * sine

        to = pl.ds(number * BLOCK, BLOCK)
        for pair in range(PAIRS):
            dq_ref[to, columns[pair]] = rope_back(d_query[number, pair] * HD ** (-0.5)).astype(BF16)
        key = [collected(d_key_pair, number, head, head % 2 == 0) for head in range(KVH)]
        value = [collected(d_value_pair, number, head, head % 2 == 1) for head in range(KVH)]
        dkv_ref[to, :128] = rope_back(jnp.where(low, key[0], key[1])).astype(BF16)
        dkv_ref[to, 128:256] = jnp.where(low, rope_back(key[2]), value[0]).astype(BF16)
        dkv_ref[to, 256:] = jnp.where(low, value[1], value[2]).astype(BF16)


def input_backward_kernel(n_shard, n_rep, idx, x_ref, nrm_ref, gain_ref, wq_full, wkv_full, dmid_ref, gout_ref,
                          gain_mlp_ref, dq_one, dq_two, dkv_one, dkv_two, din_ref, a_lo, a_hi, a_all, dq_all, dkv_all):
    model = x_ref.shape[1]
    width = gout_ref.shape[0]
    half_rows = dq_one.shape[0]
    dq_all[:half_rows, :] = dq_one[...]
    dq_all[half_rows:, :] = dq_two[...]
    dkv_all[:half_rows, :] = dkv_one[...]
    dkv_all[half_rows:, :] = dkv_two[...]
    own_normed = mm(nrm_ref[...], own_columns(idx[0], model, width)).astype(BF16)
    kv_width = dkv_all.shape[1]
    a_all[:width, :] = mm_tn(own_normed, dq_all[:, :model])
    a_all[width : 2 * width, :] = gout_ref[...]
    a_all[2 * width : 3 * width, :kv_width] = mm_tn(own_normed, dkv_all[...])
    a_all[2 * width : 3 * width, kv_width:] = jnp.zeros((width, model - kv_width), F32)
    d_normed = mm_nt(dq_all[...], wq_full[...]) + mm_nt(dkv_all[...], wkv_full[...])
    stream = x_ref[...].astype(F32)
    inv_attn = inverse_rms(stream)
    sum_attn = jnp.sum(d_normed * stream * inv_attn, axis=0, keepdims=True)
    tail = a_all.shape[0] - 3 * width
    row = lax.broadcasted_iota(jnp.int32, (tail, model), 0)
    a_all[3 * width :, :] = jnp.where(row == 0, sum_attn, jnp.where(row == 1, gain_mlp_ref[:1, :], 0.0))
    rows = a_all.shape[0] // n_rep
    middle = n_rep // 2
    for slab in range(n_rep):
        to = bit_reverse(idx[1] ^ slab, n_rep)
        piece = a_all[slab * rows : (slab + 1) * rows, :].astype(BF16)

        @pl.when(to < middle)
        def _():
            a_lo[to] = piece

        @pl.when(to >= middle)
        def _():
            a_hi[to - middle] = piece

    own_in = d_normed[:BLOCK, :] * gain_ref[2:3, :]
    own_stream = stream[:BLOCK, :]
    own_inv = inv_attn[:BLOCK, :]
    din_ref[...] = (
        dmid_ref[...]
        + own_inv * own_in
        - own_inv**3 * own_stream * jnp.mean(own_in * own_stream, axis=-1, keepdims=True)
    ).T


def fetch(first, second, member, slab, n_rep, target, rows):
    at = bit_reverse(member ^ slab, n_rep)
    middle = n_rep // 2

    @pl.when(at < middle)
    def _():
        target[pl.ds(slab * rows, rows), :] = first[at].astype(F32)

    @pl.when(at >= middle)
    def _():
        target[pl.ds(slab * rows, rows), :] = second[at - middle].astype(F32)


def unpack_mlp_kernel(n_rep, n_shard, idx, one_lo, one_hi, two_lo, two_hi, down_ref, gu_ref):
    shard = idx[0]
    member = idx[1]
    middle = n_rep // 2
    rows, chunk = two_lo.shape[1:]
    ff = gu_ref.shape[1] // 2
    groups = gu_ref.shape[0] // rows

    def place_gateup(slab, pair, piece):
        up, rest = divmod(slab, 2 * groups)
        column, group = divmod(rest, groups)
        base = ((shard ^ (2 * pair)) >> 1) * 2 * chunk + column * chunk + up * ff
        gu_ref[group * rows : (group + 1) * rows, pl.ds(pl.multiple_of(base, 128), chunk)] = piece

    for slab in range(n_rep):
        at = bit_reverse(member ^ slab, n_rep)

        def place(one, two, where):
            piece = one[where].astype(F32)
            place_gateup(slab, 0, piece[:rows])
            down_ref[slab * rows : (slab + 1) * rows, :] = piece[rows:]
            place_gateup(slab, 1, two[where].astype(F32))

        @pl.when(at < middle)
        def _():
            place(one_lo, two_lo, at)

        @pl.when(at >= middle)
        def _():
            place(one_hi, two_hi, at - middle)


def unpack_attn_kernel(n_rep, idx, first, second, q_ref, kv_ref, o_ref, gain_ref, a_all):
    rows = first.shape[1]
    for slab in range(n_rep):
        fetch(first, second, idx[1], slab, n_rep, a_all, rows)
    width = q_ref.shape[0]
    q_ref[...] = a_all[:width, :]
    o_ref[...] = a_all[width : 2 * width, :]
    kv_ref[...] = a_all[2 * width : 3 * width, : kv_ref.shape[1]]
    gain_ref[...] = a_all[3 * width : 3 * width + 8, :]


def call(body, operands, outs, scratch=(), micros=1, vmem=24, raw=()):
    in_vmem = pl.BlockSpec(memory_space=pltpu.VMEM)
    in_hbm = pl.BlockSpec(memory_space=pltpu.HBM)
    specs = [in_hbm if number in raw else in_vmem for number in range(1, len(operands))]
    return pl.pallas_call(
        body,
        out_shape=outs,
        in_specs=[pl.BlockSpec(memory_space=pltpu.SMEM)] + specs,
        out_specs=jax.tree.map(lambda _: in_vmem, outs),
        scratch_shapes=list(scratch),
        compiler_params=pltpu.CompilerParams(vmem_limit_bytes=vmem * 2**20),
        cost_estimate=pl.CostEstimate(flops=int(micros * 1e9), bytes_accessed=2**20, transcendentals=0),
    )(*operands)


def shape(dims, dtype):
    return jax.ShapeDtypeStruct(dims, dtype)


def exchange(value, axis, total, mask):
    return lax.ppermute(value, axis, [(member, member ^ mask) for member in range(total)])


def replica_steps(low, high, total):
    mask = 1
    while True:
        arrived = exchange(high, "rep", total, mask)
        held = (low.astype(F32) + arrived.astype(F32)).astype(BF16)
        yield held
        mask *= 2
        if mask == total:
            break
        low, high = held[: held.shape[0] // 2], held[held.shape[0] // 2 :]
    mask = total // 2
    while True:
        arrived = exchange(held, "rep", total, mask)
        mask //= 2
        if mask == 0:
            yield held, arrived
            return
        held = jnp.concatenate([held, arrived], axis=0)
        yield held


def last_of(steps):
    for result in steps:
        pass
    return result


def after(value, *earlier):
    return lax.optimization_barrier((value,) + earlier)[0]


def on_device(n_rep, n_shard, tokens, positions, seq_count, w_query, w_keyval, w_out, w_gateup, w_down, gain_attn,
              gain_mlp, out_grad):
    row_count, model = tokens.shape
    width = w_query.shape[1]
    ff = w_gateup.shape[2] // 2
    kv_width = w_keyval.shape[2]
    group_rows = n_shard * row_count
    shard = lax.axis_index("fsdp").astype(jnp.int32)
    member = lax.axis_index("rep").astype(jnp.int32)
    idx = jnp.stack([shard, member, seq_count[0]])
    pack_rows = 2 * width + width * kv_width // model
    own_full, half_full, gu_half, cotangent = call(
        prepare_kernel,
        [idx, w_query[0], w_keyval[0], w_out[0], w_gateup[0], tokens.T, out_grad.T, positions[None], gain_attn,
         gain_mlp],
        (
            shape((pack_rows + row_count + 16, model), BF16),
            shape((pack_rows // 2 + row_count + 16, model), BF16),
            shape((width, ff), BF16),
            shape((row_count, model), BF16),
        ),
        [
            pltpu.VMEM((width, kv_width), BF16),
            pltpu.VMEM((model, row_count), BF16),
            pltpu.VMEM((model, row_count), BF16),
            pltpu.VMEM((16, model), F32),
            pltpu.SemaphoreType.DMA((6,)),
        ],
        micros=1,
        vmem=PREPARE_VMEM,
        raw=range(1, 7),
    )
    direct = exchange(half_full, "fsdp", n_shard, 2)
    around = exchange(direct[: pack_rows // 2], "rep", n_rep, 1)
    packs = [own_full, exchange(own_full, "fsdp", n_shard, 1), direct, around,
             exchange(direct, "fsdp", n_shard, 1), exchange(around, "fsdp", n_shard, 1)]
    gu_direct = exchange(gu_half, "fsdp", n_shard, 2)
    idx_late, gu_direct = lax.optimization_barrier((idx, gu_direct))
    gu_around = exchange(gu_direct, "rep", n_rep, 1)
    cot_across = exchange(cotangent, "fsdp", n_shard, 2)
    down_across = exchange(w_down[0].T, "fsdp", n_shard, 2)
    (x_all, normed, query, keyval, mixed, mid, normed_mid, cosine, sine, gains, wq_full, wkv_full, wo_full) = call(
        functools.partial(attn_forward_kernel, n_shard),
        [idx_late] + packs,
        (
            shape((group_rows, model), BF16),
            shape((group_rows, model), BF16),
            shape((group_rows, QW), BF16),
            shape((group_rows, kv_width), BF16),
            shape((group_rows, QW), BF16),
            shape((group_rows, model), F32),
            shape((group_rows, model), BF16),
            shape((group_rows, 128), F32),
            shape((group_rows, 128), F32),
            shape((16, model), F32),
            shape((model, QW), BF16),
            shape((model, kv_width), BF16),
            shape((QW, model), BF16),
        ),
        [
            pltpu.VMEM((group_rows, QW), F32),
            pltpu.VMEM((group_rows, kv_width), F32),
            pltpu.VMEM((n_shard, pack_rows, model), BF16),
            pltpu.VMEM((n_shard, 16, model), BF16),
            pltpu.SemaphoreType.DMA((6,)),
            pltpu.SemaphoreType.DMA((n_shard,)),
            pltpu.SemaphoreType.DMA((n_shard,)),
        ],
        micros=MICROS[0],
        raw=range(1, 7),
    )
    middle = n_rep // 2
    chunk = ff // n_shard
    slab_rows = width * 4 // n_rep
    a_rows = 3 * width + 16
    a_slab = (a_rows // n_rep, model)
    gu_own, cot_own, down_own, gu_direct, gu_around, cot_across, down_across, _ = lax.optimization_barrier(
        (w_gateup[0], cotangent, w_down[0].T, gu_direct, gu_around, cot_across, down_across, gains)
    )
    gu = [gu_own, exchange(gu_own, "fsdp", n_shard, 1), gu_direct, gu_around,
          exchange(gu_direct, "fsdp", n_shard, 1), exchange(gu_around, "fsdp", n_shard, 1)]
    cot = [cot_own, exchange(cot_own, "fsdp", n_shard, 1), cot_across, exchange(cot_across, "fsdp", n_shard, 1)]
    down_beside = exchange(down_own, "fsdp", n_shard, 1)
    half_act, half_dn, one_lo, one_hi, dcot, gu_full, own_mid = call(
        functools.partial(mlp_kernel, n_shard, n_rep, True),
        [idx, normed_mid, mid, down_own, down_beside] + cot + gu,
        (
            shape((row_count, model), F32),
            shape((group_rows, model), F32),
            shape((middle, 2 * slab_rows, chunk), BF16),
            shape((middle, 2 * slab_rows, chunk), BF16),
            shape((group_rows, model), BF16),
            shape((model, 2 * ff), BF16),
            shape((group_rows, width), BF16),
        ),
        [
            pltpu.VMEM((n_rep, 2 * slab_rows, chunk), BF16),
            pltpu.VMEM((model, 2 * chunk), BF16),
            pltpu.VMEM((group_rows, 2 * chunk), BF16),
            pltpu.SemaphoreType.DMA((6,)),
            pltpu.SemaphoreType.DMA((2,)),
            pltpu.SemaphoreType.DMA((n_shard,)),
        ],
        micros=MICROS[1],
        raw=range(3, 5 + 2 * n_shard + 2),
    )
    down_across, _ = lax.optimization_barrier((down_across, half_act))
    down_corner = exchange(down_across, "fsdp", n_shard, 1)
    out_act, d_normed_mid, two_lo, two_hi = call(
        functools.partial(mlp_kernel, n_shard, n_rep, False),
        [idx, normed_mid, half_act, down_across, down_corner, dcot, gu_full, own_mid, half_dn],
        (
            shape((model, row_count), F32),
            shape((group_rows, model), F32),
            shape((middle, slab_rows, chunk), BF16),
            shape((middle, slab_rows, chunk), BF16),
        ),
        [
            pltpu.VMEM((n_rep, slab_rows, chunk), BF16),
            pltpu.VMEM((model, 2 * chunk), BF16),
            pltpu.SemaphoreType.DMA((2,)),
        ],
        micros=MICROS[2],
        raw=(3, 4),
    )
    one = replica_steps(one_lo, one_hi, n_rep)
    two = replica_steps(two_lo, two_hi, n_rep)
    d_attn, d_mixed, d_mid, part_out, part_gain = call(
        functools.partial(residual_backward_kernel, n_shard),
        [idx, mid, d_normed_mid, dcot, mixed, gains, wo_full],
        (
            shape((group_rows, model), BF16),
            shape((group_rows, QW), BF16),
            shape((row_count, model), F32),
            shape((width, model), F32),
            shape((8, model), F32),
        ),
        micros=MICROS[3],
    )
    halves = []
    for first_row in (0, group_rows // 2):
        d_mixed = after(d_mixed, *([next(one)] if first_row == 0 else [next(one), next(two), halves[0][0]]))
        halves.append(
            call(
                functools.partial(heads_backward_kernel, first_row),
                [idx, query, keyval, d_mixed, cosine, sine],
                (shape((group_rows // 2, QW), BF16), shape((group_rows // 2, kv_width), BF16)),
                micros=MICROS[4],
            )
        )
    d_mid = after(d_mid, next(one), next(two))
    in_grad, a_lo, a_hi = call(
        functools.partial(input_backward_kernel, n_shard, n_rep),
        [idx, x_all, normed, gains, wq_full, wkv_full, d_mid, part_out, part_gain,
         halves[0][0], halves[1][0], halves[0][1], halves[1][1]],
        (
            shape((model, row_count), F32),
            shape((middle,) + a_slab, BF16),
            shape((middle,) + a_slab, BF16),
        ),
        [
            pltpu.VMEM((a_rows, model), F32),
            pltpu.VMEM((group_rows, QW), BF16),
            pltpu.VMEM((group_rows, kv_width), BF16),
        ],
        micros=MICROS[5],
    )
    one, two = last_of(one), last_of(two)
    attn = last_of(replica_steps(a_lo, a_hi, n_rep))
    grad_down, grad_gateup = call(
        functools.partial(unpack_mlp_kernel, n_rep, n_shard),
        [idx] + list(one) + list(two),
        (shape((model, chunk), F32), shape((width, 2 * ff), F32)),
        micros=3,
    )
    grad_query, grad_keyval, grad_out, gain_rows = call(
        functools.partial(unpack_attn_kernel, n_rep),
        [idx] + list(attn),
        (
            shape((width, model), F32),
            shape((width, kv_width), F32),
            shape((width, model), F32),
            shape((8, model), F32),
        ),
        [pltpu.VMEM((a_rows, model), F32)],
        micros=2,
    )
    own_gains = lax.dynamic_slice(gain_rows, (0, shard * width), (2, width))
    return (
        out_act.T,
        in_grad.T,
        grad_query[None],
        grad_keyval[None],
        grad_out[None],
        grad_gateup[None],
        grad_down.T[None],
        own_gains[:1],
        own_gains[1:],
    )


def solution(mesh):
    placed = (
        P(("rep", "fsdp"), None),
        P(("rep", "fsdp")),
        P(("rep", "fsdp")),
        P(None, "fsdp", None),
        P(None, "fsdp", None),
        P(None, "fsdp", None),
        P(None, "fsdp", None),
        P(None, "fsdp", None),
        P(None, "fsdp"),
        P(None, "fsdp"),
        P(("rep", "fsdp"), None),
    )
    return jax.shard_map(
        functools.partial(on_device, mesh.shape["rep"], mesh.shape["fsdp"]),
        mesh=mesh,
        in_specs=placed,
        out_specs=(
            P(("rep", "fsdp"), None),
            P(("rep", "fsdp"), None),
            P(None, "fsdp", None),
            P(None, "fsdp", None),
            P(None, "fsdp", None),
            P(None, "fsdp", None),
            P(None, "fsdp", None),
            P(None, "fsdp"),
            P(None, "fsdp"),
        ),
        check_vma=False,
    )
```

time: 147 us -> 135 us (0.918)
  waiting for transfers between devices: 59.2 us -> 37.5 us
  starting transfers between devices: 36.9 us -> 48.1 us
  local copies, waits for them, and re-layouts: 8.97 us -> 1.85 us
  Pallas kernels: 37.6 us -> 44.3 us
    ppermute x44 -> x34, waiting for transfers between devices: 59.2 us -> 37.5 us  [exchange(): lax.ppermute(value, axis, [(member, member ^ mask) for member in range(to...]
    ppermute x44 -> x34, starting transfers between devices: 36.9 us -> 48.1 us  [exchange(): lax.ppermute(value, axis, [(member, member ^ mask) for member in range(to...]
    pallas_call x6 -> x10, Pallas kernels: 37.6 us -> 44.3 us  [call(): pl.pallas_call(body, out_shape=outs, in_specs=[pl.BlockSpec(memory_space=...]
    unnamed x20 -> x10, local copies, waits for them, and re-layouts: 6.37 us -> 1.1 us
    dynamic_slice x1 -> x0, local copies, waits for them, and re-layouts: 1.8 us -> none  [on_device(): lax.dynamic_slice(w_gateup[0], (0, side * ff), (width, ff))]
  transfers between devices with their start and end apart: 44 -> 34, of which waited for: 19 -> 15; matrix products, arithmetic and copies ran while one was open for 6% -> 1% of each run, Pallas kernels for 18% -> 23%
where the time goes in v3:
time: 135 us
  starting transfers between devices  48.1 us (36%)
  Pallas kernels  44.3 us (33%)
  waiting for transfers between devices  37.5 us (28%)
  local copies, waits for them, and re-layouts  1.85 us (1%)
  between operations  1.54 us (1%)
    ppermute x34, starting transfers between devices, exchange(): lax.ppermute(value, axis, [(member, member ^ mask) for member in range(to...  48.1 us
    pallas_call x10, Pallas kernels, call(): pl.pallas_call(body, out_shape=outs, in_specs=[pl.BlockSpec(memory_space=...  44.3 us
    ppermute x34, waiting for transfers between devices, exchange(): lax.ppermute(value, axis, [(member, member ^ mask) for member in range(to...  37.5 us
  transfers between devices with their start and end apart: 34, of which 15 were waited for; matrix products, arithmetic and copies ran while one was open for 1% of the time, Pallas kernels for 23%

profile of v3, /device:TPU:0, one launch (start us, length us, event | category | flops | bytes accessed | tf_op | source)
XLA Modules:
  0.0 134.6 jit_solution(8771513186254529701)
XLA Ops:
  1.9 3.4 %shard_map.178 = (bf16[528,576]{1,0:T(8,128)(2,1)}, bf16[336,576]{1,0:T(8,128)(2,1)}, bf16[144,1536]{1,0:T(8,128)(2,1)}, bf16[128,576]{1,0:T(8,128)(2,1)}) custom-call(s32[3]{0:T(128)} %pad_add_fusion.idx, bf16[144,576]{1,0:T(8,128)(2,1)} %bitcast.27, bf16[144,384]{1,0:T(8,128)(2,1)} %bitcast.31, bf16[144,576]{1,0:T(8,128)(2,1)} %bitcast.28, ...), custom_call_target="tpu_custom_call" | custom-call | flops 1000000000 | bytes 1048576 | tf_op jit(solution)/shard_map/pallas_call | solution.py:535
  5.3 3.0 %collective-permute-start.2 = (bf16[336,576]{1,0:T(8,128)(2,1)}, bf16[336,576]{1,0:T(8,128)(2,1)S(1)}, u32[]{:S(2)}, u32[]{:S(2)}) collective-permute-start(bf16[336,576]{1,0:T(8,128)(2,1)} %get-tuple-element.70), channel_id=1, source_target_pairs={{0,2},{1,3},{2,0},{3,1},{4,6},{5,7},{6,4},{7,5},{8,10},{9,11},{10,... | collective-permute-start | bytes 1161224 | tf_op jit(solution)/shard_map/ppermute | solution.py:551
  8.5 10.8 %collective-permute-done.2.refs_2_ = bf16[336,576]{1,0:T(8,128)(2,1)S(1)} collective-permute-done((bf16[336,576]{1,0:T(8,128)(2,1)}, bf16[336,576]{1,0:T(8,128)(2,1)S(1)}, u32[]{:S(2)}, u32[]{:S(2)}) %collective-permute-start.2) | collective-permute-done | bytes 387104 | tf_op jit(solution)/shard_map/ppermute | solution.py:551
  19.3 2.2 %collective-permute-start.3 = (bf16[192,576]{1,0:T(8,128)(2,1)S(1)}, bf16[192,576]{1,0:T(8,128)(2,1)S(1)}, u32[]{:S(2)}, u32[]{:S(2)}) collective-permute-start(bf16[192,576]{1,0:T(8,128)(2,1)S(1)} %slice.60), channel_id=1, source_target_pairs={{0,4},{4,0},{8,12},{12,8},{16,20},{20,16},{24,28},{28,24},{1,5},{5... | collective-permute-start | bytes 663560 | tf_op jit(solution)/shard_map/ppermute | solution.py:551
  21.4 4.2 %collective-permute-done.3.refs_3_ = bf16[192,576]{1,0:T(8,128)(2,1)S(1)} collective-permute-done((bf16[192,576]{1,0:T(8,128)(2,1)S(1)}, bf16[192,576]{1,0:T(8,128)(2,1)S(1)}, u32[]{:S(2)}, u32[]{:S(2)}) %collective-permute-start.3) | collective-permute-done | bytes 221216 | tf_op jit(solution)/shard_map/ppermute | solution.py:551
  25.7 1.9 %collective-permute-start.7 = (bf16[128,576]{1,0:T(8,128)(2,1)}, bf16[128,576]{1,0:T(8,128)(2,1)S(1)}, u32[]{:S(2)}, u32[]{:S(2)}) collective-permute-start(bf16[128,576]{1,0:T(8,128)(2,1)} %get-tuple-element.77.refs_4_), channel_id=1, source_target_pairs={{0,2},{1,3},{2,0},{3,1},{4,6},{5,7},{6,4},{7,5},{8,10},{9,11},{10,... | collective-permute-start | bytes 442376 | tf_op jit(solution)/shard_map/ppermute | solution.py:551
  27.9 1.7 %collective-permute-start.8 = (bf16[576,384]{1,0:T(8,128)(2,1)S(1)}, bf16[576,384]{1,0:T(8,128)(2,1)S(1)}, u32[]{:S(2)}, u32[]{:S(2)}) collective-permute-start(bf16[576,384]{1,0:T(8,128)(2,1)S(1)} %bitcast.24), channel_id=1, source_target_pairs={{0,2},{1,3},{2,0},{3,1},{4,6},{5,7},{6,4},{7,5},{8,10},{9,11},{10,... | collective-permute-start | bytes 1327112 | tf_op jit(solution)/shard_map/ppermute | solution.py:551
  32.3 8.6 %shard_map.179 = (bf16[512,576]{1,0:T(8,128)(2,1)S(1)}, bf16[512,576]{1,0:T(8,128)(2,1)S(1)}, bf16[512,640]{1,0:T(8,128)(2,1)S(1)}, bf16[512,384]{1,0:T(8,128)(2...) custom-call(s32[3]{0:T(128)S(1)} %copy-done, ...), custom_call_target="tpu_custom_call" | custom-call | flops 7000000000 | bytes 1048576 | tf_op jit(solution)/shard_map/pallas_call | solution.py:535
  43.3 3.5 %collective-permute-done.10.refs_5_ = bf16[128,576]{1,0:T(8,128)(2,1)S(1)} collective-permute-done((bf16[128,576]{1,0:T(8,128)(2,1)S(1)}, bf16[128,576]{1,0:T(8,128)(2,1)S(1)}, u32[]{:S(2)}, u32[]{:S(2)}) %collective-permute-start.10) | collective-permute-done | bytes 147488 | tf_op jit(solution)/shard_map/ppermute | solution.py:551
  48.1 7.6 %shard_map.180 = (f32[128,576]{1,0:T(8,128)S(1)}, f32[512,576]{1,0:T(8,128)S(1)}, bf16[4,144,384]{2,1,0:T(8,128)(2,1)S(1)}, bf16[4,144,384]{2,1,0:T(8,128)(2,1)S...) custom-call(s32[3]{0:T(128)S(1)} %copy-done, ...), custom_call_target="tpu_custom_call" | custom-call | flops 6000000000 | bytes 1048576 | tf_op jit(solution)/shard_map/pallas_call | solution.py:535
  55.9 1.8 %collective-permute-start.16 = (bf16[4,144,384]{2,1,0:T(8,128)(2,1)S(1)}, bf16[4,144,384]{2,1,0:T(8,128)(2,1)S(1)}, u32[]{:S(2)}, u32[]{:S(2)}) collective-permute-start(bf16[4,144,384]{2,1,0:T(8,128)(2,1)S(1)} %get-tuple-element.99), channel_id=1, source_target_pairs={{0,4},{4,0},{8,12},{12,8},{16,20},{20,16},{24,28},{28,24},{1,5},{5... | collective-permute-start | bytes 1327112 | tf_op jit(solution)/shard_map/ppermute | solution.py:551
  57.7 6.0 %shard_map.181 = (f32[576,128]{1,0:T(8,128)}, f32[512,576]{1,0:T(8,128)S(1)}, bf16[4,72,384]{2,1,0:T(8,128)(2,1)S(1)}, bf16[4,72,384]{2,1,0:T(8,128)(2,1)S(1)}) custom-call(s32[3]{0:T(128)S(1)} %copy-done, bf16[512,576]{1,0:T(8,128)(2,1)S(1)} %get-tuple-element.71.refs_0_, f32[128,576]{1,0:T(8,128)S(1)} %get-tuple-element.82.refs_1_, ...), custom_call_target="tpu_custom_call" | custom-call | flops 6000000000 | bytes 1048576 | tf_op jit(solution)/shard_map/pallas_call | solution.py:535
  63.8 1.7 %collective-permute-start.19 = (bf16[4,72,384]{2,1,0:T(8,128)(2,1)S(1)}, bf16[4,72,384]{2,1,0:T(8,128)(2,1)S(1)}, u32[]{:S(2)}, u32[]{:S(2)}) collective-permute-start(bf16[4,72,384]{2,1,0:T(8,128)(2,1)S(1)} %get-tuple-element.101), channel_id=1, source_target_pairs={{0,4},{4,0},{8,12},{12,8},{16,20},{20,16},{24,28},{28,24},{1,5},{5... | collective-permute-start | bytes 663560 | tf_op jit(solution)/shard_map/ppermute | solution.py:551
  65.5 3.5 %collective-permute-done.16 = bf16[4,144,384]{2,1,0:T(8,128)(2,1)S(1)} collective-permute-done((bf16[4,144,384]{2,1,0:T(8,128)(2,1)S(1)}, bf16[4,144,384]{2,1,0:T(8,128)(2,1)S(1)}, u32[]{:S(2)}, u32[]{:S(2)}) %collective-permute-start.16) | collective-permute-done | bytes 442400 | tf_op jit(solution)/shard_map/ppermute | solution.py:551
  69.1 1.9 %collective-permute-start.17 = (bf16[2,144,384]{2,1,0:T(8,128)(2,1)S(1)}, bf16[2,144,384]{2,1,0:T(8,128)(2,1)S(1)}, u32[]{:S(2)}, u32[]{:S(2)}) collective-permute-start(bf16[2,144,384]{2,1,0:T(8,128)(2,1)S(1)} %slice.62), channel_id=1, source_target_pairs={{0,8},{4,12},{8,0},{12,4},{16,24},{20,28},{24,16},{28,20},{1,9},{5... | collective-permute-start | bytes 663560 | tf_op jit(solution)/shard_map/ppermute | solution.py:551
  71.0 2.9 %shard_map.182 = (bf16[512,576]{1,0:T(8,128)(2,1)}, bf16[512,640]{1,0:T(8,128)(2,1)S(1)}, f32[128,576]{1,0:T(8,128)S(1)}, f32[144,576]{1,0:T(8,128)S(1)}, f32[8,576]{1,0:T(8,128)S(1)}) custom-call(s32[3]{0:T(128)S(1)} %copy-done, f32[512,576]{1,0:T(8,128)S(1)} %get-tuple-element.72.refs_1_.mid_ref, f32[512,576]{1,0:T(8,128)S(1)} %get-tuple-element.94.dn_ref, ...), custom_call_target="tpu_custom_call" | custom-call | flops 3000000000 | bytes 1048576 | tf_op jit(solution)/shard_map/pallas_call | solution.py:535
  73.8 3.9 %shard_map.183 = (bf16[256,640]{1,0:T(8,128)(2,1)S(1)}, bf16[256,384]{1,0:T(8,128)(2,1)S(1)}) custom-call(s32[3]{0:T(128)S(1)} %copy-done, bf16[512,640]{1,0:T(8,128)(2,1)S(1)} %get-tuple-element.105.q_ref, bf16[512,384]{1,0:T(8,128)(2,1)S(1)} %get-tuple-element.106.kv_ref, bf16[512,640]{1,0:T(8,128)(2,1)S(1)} %get-tuple-element.112.dmix_ref, ...), custom_call_target="tpu_custom_call" | custom-call | flops 4000000000 | bytes 1048576 | tf_op jit(solution)/shard_map/pallas_call | solution.py:535
  78.2 2.9 %collective-permute-start.18 = (bf16[1,144,384]{2,1,0:T(8,128)(2,1)S(1)}, bf16[1,144,384]{2,1,0:T(8,128)(2,1)S(1)}, u32[]{:S(2)}, u32[]{:S(2)}) collective-permute-start(bf16[1,144,384]{2,1,0:T(8,128)(2,1)S(1)} %slice.64), channel_id=1, source_target_pairs={{0,16},{4,20},{8,24},{12,28},{16,0},{20,4},{24,8},{28,12},{1,17},{... | collective-permute-start | bytes 331784 | tf_op jit(solution)/shard_map/ppermute | solution.py:551
  81.1 3.9 %shard_map.184 = (bf16[256,640]{1,0:T(8,128)(2,1)S(1)}, bf16[256,384]{1,0:T(8,128)(2,1)S(1)}) custom-call(s32[3]{0:T(128)S(1)} %copy-done, bf16[512,640]{1,0:T(8,128)(2,1)S(1)} %get-tuple-element.105.q_ref, bf16[512,384]{1,0:T(8,128)(2,1)S(1)} %get-tuple-element.106.kv_ref, bf16[512,640]{1,0:T(8,128)(2,1)S(1)} %get-tuple-element.112.dmix_ref, ...), custom_call_target="tpu_custom_call" | custom-call | flops 4000000000 | bytes 1048576 | tf_op jit(solution)/shard_map/pallas_call | solution.py:535
  85.5 4.0 %shard_map.185 = (f32[576,128]{1,0:T(8,128)}, bf16[4,56,576]{2,1,0:T(8,128)(2,1)S(1)}, bf16[4,56,576]{2,1,0:T(8,128)(2,1)S(1)}) custom-call(s32[3]{0:T(128)S(1)} %copy-done, bf16[512,576]{1,0:T(8,128)(2,1)S(1)} %get-tuple-element.90.x_ref, bf16[512,576]{1,0:T(8,128)(2,1)S(1)} %get-tuple-element.91.nrm_ref, f32[16,576]{1,0:T(8,128)S(1)} %get-tuple-element.75.gain_ref, ...), custom_call_target="tpu_custom_call" | custom-call | flops 4000000000 | bytes 1048576 | tf_op jit(solution)/shard_map/pallas_call | solution.py:535
  91.1 2.6 %collective-permute-start.31 = (bf16[1,72,384]{2,1,0:T(8,128)(2,1)S(1)}, bf16[1,72,384]{2,1,0:T(8,128)(2,1)S(1)}, u32[]{:S(2)}, u32[]{:S(2)}) collective-permute-start(bf16[1,72,384]{2,1,0:T(8,128)(2,1)S(1)} %add_convert_fusion.8), channel_id=1, source_target_pairs={{0,16},{4,20},{8,24},{12,28},{16,0},{20,4},{24,8},{28,12},{1,17},{... | collective-permute-start | bytes 165896 | tf_op jit(solution)/shard_map/ppermute | solution.py:551
  93.7 2.4 %collective-permute-done.21 = bf16[4,56,576]{2,1,0:T(8,128)(2,1)S(1)} collective-permute-done((bf16[4,56,576]{2,1,0:T(8,128)(2,1)S(1)}, bf16[4,56,576]{2,1,0:T(8,128)(2,1)S(1)}, u32[]{:S(2)}, u32[]{:S(2)}) %collective-permute-start.21) | collective-permute-done | bytes 258080 | tf_op jit(solution)/shard_map/ppermute | solution.py:551
  96.2 1.8 %collective-permute-start.22 = (bf16[2,56,576]{2,1,0:T(8,128)(2,1)S(1)}, bf16[2,56,576]{2,1,0:T(8,128)(2,1)S(1)}, u32[]{:S(2)}, u32[]{:S(2)}) collective-permute-start(bf16[2,56,576]{2,1,0:T(8,128)(2,1)S(1)} %slice.68), channel_id=1, source_target_pairs={{0,8},{4,12},{8,0},{12,4},{16,24},{20,28},{24,16},{28,20},{1,9},{5... | collective-permute-start | bytes 387080 | tf_op jit(solution)/shard_map/ppermute | solution.py:551
  98.0 3.4 %collective-permute-start.27 = (bf16[1,144,384]{2,1,0:T(8,128)(2,1)S(1)}, bf16[1,144,384]{2,1,0:T(8,128)(2,1)S(1)}, u32[]{:S(2)}, u32[]{:S(2)}) collective-permute-start(bf16[1,144,384]{2,1,0:T(8,128)(2,1)S(1)} %add_convert_fusion.6), channel_id=1, source_target_pairs={{0,16},{4,20},{8,24},{12,28},{16,0},{20,4},{24,8},{28,12},{1,17},{... | collective-permute-start | bytes 331784 | tf_op jit(solution)/shard_map/ppermute | solution.py:551
  102.9 3.0 %collective-permute-start.23 = (bf16[1,56,576]{2,1,0:T(8,128)(2,1)S(1)}, bf16[1,56,576]{2,1,0:T(8,128)(2,1)S(1)}, u32[]{:S(2)}, u32[]{:S(2)}) collective-permute-start(bf16[1,56,576]{2,1,0:T(8,128)(2,1)S(1)} %slice.70), channel_id=1, source_target_pairs={{0,16},{4,20},{8,24},{12,28},{16,0},{20,4},{24,8},{28,12},{1,17},{... | collective-permute-start | bytes 193544 | tf_op jit(solution)/shard_map/ppermute | solution.py:551
  105.9 2.6 %collective-permute-start.28 = (bf16[2,144,384]{2,1,0:T(8,128)(2,1)S(1)}, bf16[2,144,384]{2,1,0:T(8,128)(2,1)S(1)}, u32[]{:S(2)}, u32[]{:S(2)}) collective-permute-start(bf16[2,144,384]{2,1,0:T(8,128)(2,1)S(1)} %pad_maximum_fusion.2), channel_id=1, source_target_pairs={{0,8},{4,12},{8,0},{12,4},{16,24},{20,28},{24,16},{28,20},{1,9},{5... | collective-permute-start | bytes 663560 | tf_op jit(solution)/shard_map/ppermute | solution.py:551
  108.7 3.5 %collective-permute-start.24 = (bf16[1,56,576]{2,1,0:T(8,128)(2,1)S(1)}, bf16[1,56,576]{2,1,0:T(8,128)(2,1)S(1)}, u32[]{:S(2)}, u32[]{:S(2)}) collective-permute-start(bf16[1,56,576]{2,1,0:T(8,128)(2,1)S(1)} %add_convert_fusion.7), channel_id=1, source_target_pairs={{0,16},{4,20},{8,24},{12,28},{16,0},{20,4},{24,8},{28,12},{1,17},{... | collective-permute-start | bytes 193544 | tf_op jit(solution)/shard_map/ppermute | solution.py:551
  114.7 3.7 %collective-permute-start.25 = (bf16[2,56,576]{2,1,0:T(8,128)(2,1)S(1)}, bf16[2,56,576]{2,1,0:T(8,128)(2,1)S(1)}, u32[]{:S(2)}, u32[]{:S(2)}) collective-permute-start(bf16[2,56,576]{2,1,0:T(8,128)(2,1)S(1)} %pad_maximum_fusion.4), channel_id=1, source_target_pairs={{0,8},{4,12},{8,0},{12,4},{16,24},{20,28},{24,16},{28,20},{1,9},{5... | collective-permute-start | bytes 387080 | tf_op jit(solution)/shard_map/ppermute | solution.py:551
  118.4 1.7 %collective-permute-start.33 = (bf16[4,72,384]{2,1,0:T(8,128)(2,1)S(1)}, bf16[4,72,384]{2,1,0:T(8,128)(2,1)S(1)}, u32[]{:S(2)}, u32[]{:S(2)}) collective-permute-start(bf16[4,72,384]{2,1,0:T(8,128)(2,1)S(1)} %pad_maximum_fusion.3.two_lo), channel_id=1, source_target_pairs={{0,4},{4,0},{8,12},{12,8},{16,20},{20,16},{24,28},{28,24},{1,5},{5... | collective-permute-start | bytes 663560 | tf_op jit(solution)/shard_map/ppermute | solution.py:551
  121.5 1.7 %collective-permute-start.26 = (bf16[4,56,576]{2,1,0:T(8,128)(2,1)S(1)}, bf16[4,56,576]{2,1,0:T(8,128)(2,1)S(1)}, u32[]{:S(2)}, u32[]{:S(2)}) collective-permute-start(bf16[4,56,576]{2,1,0:T(8,128)(2,1)S(1)} %pad_maximum_fusion.1.first), channel_id=1, source_target_pairs={{0,4},{4,0},{8,12},{12,8},{16,20},{20,16},{24,28},{28,24},{1,5},{5... | collective-permute-start | bytes 774152 | tf_op jit(solution)/shard_map/ppermute | solution.py:551
  123.2 6.0 %collective-permute-done.33.two_hi = bf16[4,72,384]{2,1,0:T(8,128)(2,1)S(1)} collective-permute-done((bf16[4,72,384]{2,1,0:T(8,128)(2,1)S(1)}, bf16[4,72,384]{2,1,0:T(8,128)(2,1)S(1)}, u32[]{:S(2)}, u32[]{:S(2)}) %collective-permute-start.33) | collective-permute-done | bytes 221216 | tf_op jit(solution)/shard_map/ppermute | solution.py:551
  129.2 2.3 %shard_map.187 = (f32[576,384]{1,0:T(8,128)}, f32[144,3072]{1,0:T(8,128)}) custom-call(s32[3]{0:T(128)S(1)} %copy-done, bf16[4,144,384]{2,1,0:T(8,128)(2,1)S(1)} %pad_maximum_fusion.one_lo, bf16[4,144,384]{2,1,0:T(8,128)(2,1)S(1)} %collective-permute-done.29.one_hi, bf16[4,72,384]{2,1,0:T(8,128)(2,1)S(1)} %pad_maximum_fusion.3.two_lo, ...), custom_call_target="tpu_custom_call" | custom-call | flops 3000000000 | bytes 1048576 | tf_op jit(solution)/shard_map/pallas_call | solution.py:535
  (80 shorter events, 18.9 us)
Async XLA Ops:
  5.3 13.9 %collective-permute-start.2 = (bf16[336,576]{1,0:T(8,128)(2,1)}, bf16[336,576]{1,0:T(8,128)(2,1)S(1)}, u32[]{:S(2)}, u32[]{:S(2)}) collective-permute-start(bf16[336,576]{1,0:T(8,128)(2,1)} %get-tuple-element.70), channel_id=1, source_target_pairs={{0,2},{1,3},{2,0},{3,1},{4,6},{5,7},{6,4},{7,5},{8,10},{9,11},{10,... | collective-permute-start | bytes 1161224 | tf_op jit(solution)/shard_map/ppermute | solution.py:551
  8.3 21.3 %collective-permute-start.1 = (bf16[528,576]{1,0:T(8,128)(2,1)}, bf16[528,576]{1,0:T(8,128)(2,1)S(1)}, u32[]{:S(2)}, u32[]{:S(2)}) collective-permute-start(bf16[528,576]{1,0:T(8,128)(2,1)} %get-tuple-element.69.refs_0_), channel_id=1, source_target_pairs={{0,1},{1,0},{2,3},{3,2},{4,5},{5,4},{6,7},{7,6},{8,9},{9,8},{10,11... | collective-permute-start | bytes 1824776 | tf_op jit(solution)/shard_map/ppermute | solution.py:551
  8.3 19.6 %collective-permute-start = (bf16[144,1536]{1,0:T(8,128)(2,1)}, bf16[144,1536]{1,0:T(8,128)(2,1)S(1)}, u32[]{:S(2)}, u32[]{:S(2)}) collective-permute-start(bf16[144,1536]{1,0:T(8,128)(2,1)} %get-tuple-element.67), channel_id=1, source_target_pairs={{0,2},{1,3},{2,0},{3,1},{4,6},{5,7},{6,4},{7,5},{8,10},{9,11},{10,... | collective-permute-start | bytes 1327112 | tf_op jit(solution)/shard_map/ppermute | solution.py:551
  19.3 6.4 %collective-permute-start.3 = (bf16[192,576]{1,0:T(8,128)(2,1)S(1)}, bf16[192,576]{1,0:T(8,128)(2,1)S(1)}, u32[]{:S(2)}, u32[]{:S(2)}) collective-permute-start(bf16[192,576]{1,0:T(8,128)(2,1)S(1)} %slice.60), channel_id=1, source_target_pairs={{0,4},{4,0},{8,12},{12,8},{16,20},{20,16},{24,28},{28,24},{1,5},{5... | collective-permute-start | bytes 663560 | tf_op jit(solution)/shard_map/ppermute | solution.py:551
  21.4 9.7 %collective-permute-start.4 = (bf16[336,576]{1,0:T(8,128)(2,1)S(1)}, bf16[336,576]{1,0:T(8,128)(2,1)S(1)}, u32[]{:S(2)}, u32[]{:S(2)}) collective-permute-start(bf16[336,576]{1,0:T(8,128)(2,1)S(1)} %collective-permute-done.2.refs_2_), channel_id=1, source_target_pairs={{0,1},{1,0},{2,3},{3,2},{4,5},{5,4},{6,7},{7,6},{8,9},{9,8},{10,11... | collective-permute-start | bytes 1161224 | tf_op jit(solution)/shard_map/ppermute | solution.py:551
  25.6 5.5 %collective-permute-start.5 = (bf16[192,576]{1,0:T(8,128)(2,1)S(1)}, bf16[192,576]{1,0:T(8,128)(2,1)S(1)}, u32[]{:S(2)}, u32[]{:S(2)}) collective-permute-start(bf16[192,576]{1,0:T(8,128)(2,1)S(1)} %collective-permute-done.3.refs_3_), channel_id=1, source_target_pairs={{0,1},{1,0},{2,3},{3,2},{4,5},{5,4},{6,7},{7,6},{8,9},{9,8},{10,11... | collective-permute-start | bytes 663560 | tf_op jit(solution)/shard_map/ppermute | solution.py:551
  25.7 15.2 %collective-permute-start.7 = (bf16[128,576]{1,0:T(8,128)(2,1)}, bf16[128,576]{1,0:T(8,128)(2,1)S(1)}, u32[]{:S(2)}, u32[]{:S(2)}) collective-permute-start(bf16[128,576]{1,0:T(8,128)(2,1)} %get-tuple-element.77.refs_4_), channel_id=1, source_target_pairs={{0,2},{1,3},{2,0},{3,1},{4,6},{5,7},{6,4},{7,5},{8,10},{9,11},{10,... | collective-permute-start | bytes 442376 | tf_op jit(solution)/shard_map/ppermute | solution.py:551
  27.9 14.3 %collective-permute-start.8 = (bf16[576,384]{1,0:T(8,128)(2,1)S(1)}, bf16[576,384]{1,0:T(8,128)(2,1)S(1)}, u32[]{:S(2)}, u32[]{:S(2)}) collective-permute-start(bf16[576,384]{1,0:T(8,128)(2,1)S(1)} %bitcast.24), channel_id=1, source_target_pairs={{0,2},{1,3},{2,0},{3,1},{4,6},{5,7},{6,4},{7,5},{8,10},{9,11},{10,... | collective-permute-start | bytes 1327112 | tf_op jit(solution)/shard_map/ppermute | solution.py:551
  29.6 12.5 %collective-permute-start.6 = (bf16[144,1536]{1,0:T(8,128)(2,1)S(1)}, bf16[144,1536]{1,0:T(8,128)(2,1)S(1)}, u32[]{:S(2)}, u32[]{:S(2)}) collective-permute-start(bf16[144,1536]{1,0:T(8,128)(2,1)S(1)} %collective-permute-done.refs_10_), channel_id=1, source_target_pairs={{0,4},{4,0},{8,12},{12,8},{16,20},{20,16},{24,28},{28,24},{1,5},{5... | collective-permute-start | bytes 1327112 | tf_op jit(solution)/shard_map/ppermute | solution.py:551
  42.2 6.0 %collective-permute-start.12 = (bf16[144,3072]{1,0:T(8,128)(2,1)S(1)}, bf16[144,3072]{1,0:T(8,128)(2,1)S(1)}, u32[]{:S(2)}, u32[]{:S(2)}) collective-permute-start(bf16[144,3072]{1,0:T(8,128)(2,1)S(1)} %bitcast.22), channel_id=1, source_target_pairs={{0,1},{1,0},{2,3},{3,2},{4,5},{5,4},{6,7},{7,6},{8,9},{9,8},{10,11... | collective-permute-start | bytes 2654216 | tf_op jit(solution)/shard_map/ppermute | solution.py:551
  42.2 5.9 %collective-permute-start.13 = (bf16[144,1536]{1,0:T(8,128)(2,1)S(1)}, bf16[144,1536]{1,0:T(8,128)(2,1)S(1)}, u32[]{:S(2)}, u32[]{:S(2)}) collective-permute-start(bf16[144,1536]{1,0:T(8,128)(2,1)S(1)} %collective-permute-done.refs_10_), channel_id=1, source_target_pairs={{0,1},{1,0},{2,3},{3,2},{4,5},{5,4},{6,7},{7,6},{8,9},{9,8},{10,11... | collective-permute-start | bytes 1327112 | tf_op jit(solution)/shard_map/ppermute | solution.py:551
  42.7 5.4 %collective-permute-start.14 = (bf16[144,1536]{1,0:T(8,128)(2,1)S(1)}, bf16[144,1536]{1,0:T(8,128)(2,1)S(1)}, u32[]{:S(2)}, u32[]{:S(2)}) collective-permute-start(bf16[144,1536]{1,0:T(8,128)(2,1)S(1)} %collective-permute-done.6.refs_11_), channel_id=1, source_target_pairs={{0,1},{1,0},{2,3},{3,2},{4,5},{5,4},{6,7},{7,6},{8,9},{9,8},{10,11... | collective-permute-start | bytes 1327112 | tf_op jit(solution)/shard_map/ppermute | solution.py:551
  42.7 5.4 %collective-permute-start.9 = (bf16[576,384]{1,0:T(8,128)(2,1)S(1)}, bf16[576,384]{1,0:T(8,128)(2,1)S(1)}, u32[]{:S(2)}, u32[]{:S(2)}) collective-permute-start(bf16[576,384]{1,0:T(8,128)(2,1)S(1)} %bitcast.25), channel_id=1, source_target_pairs={{0,1},{1,0},{2,3},{3,2},{4,5},{5,4},{6,7},{7,6},{8,9},{9,8},{10,11... | collective-permute-start | bytes 1327112 | tf_op jit(solution)/shard_map/ppermute | solution.py:551
  43.2 3.5 %collective-permute-start.10 = (bf16[128,576]{1,0:T(8,128)(2,1)S(1)}, bf16[128,576]{1,0:T(8,128)(2,1)S(1)}, u32[]{:S(2)}, u32[]{:S(2)}) collective-permute-start(bf16[128,576]{1,0:T(8,128)(2,1)S(1)} %copy-done.4), channel_id=1, source_target_pairs={{0,1},{1,0},{2,3},{3,2},{4,5},{5,4},{6,7},{7,6},{8,9},{9,8},{10,11... | collective-permute-start | bytes 442376 | tf_op jit(solution)/shard_map/ppermute | solution.py:551
  55.9 13.0 %collective-permute-start.16 = (bf16[4,144,384]{2,1,0:T(8,128)(2,1)S(1)}, bf16[4,144,384]{2,1,0:T(8,128)(2,1)S(1)}, u32[]{:S(2)}, u32[]{:S(2)}) collective-permute-start(bf16[4,144,384]{2,1,0:T(8,128)(2,1)S(1)} %get-tuple-element.99), channel_id=1, source_target_pairs={{0,4},{4,0},{8,12},{12,8},{16,20},{20,16},{24,28},{28,24},{1,5},{5... | collective-permute-start | bytes 1327112 | tf_op jit(solution)/shard_map/ppermute | solution.py:551
  63.8 14.0 %collective-permute-start.19 = (bf16[4,72,384]{2,1,0:T(8,128)(2,1)S(1)}, bf16[4,72,384]{2,1,0:T(8,128)(2,1)S(1)}, u32[]{:S(2)}, u32[]{:S(2)}) collective-permute-start(bf16[4,72,384]{2,1,0:T(8,128)(2,1)S(1)} %get-tuple-element.101), channel_id=1, source_target_pairs={{0,4},{4,0},{8,12},{12,8},{16,20},{20,16},{24,28},{28,24},{1,5},{5... | collective-permute-start | bytes 663560 | tf_op jit(solution)/shard_map/ppermute | solution.py:551
  69.1 9.0 %collective-permute-start.17 = (bf16[2,144,384]{2,1,0:T(8,128)(2,1)S(1)}, bf16[2,144,384]{2,1,0:T(8,128)(2,1)S(1)}, u32[]{:S(2)}, u32[]{:S(2)}) collective-permute-start(bf16[2,144,384]{2,1,0:T(8,128)(2,1)S(1)} %slice.62), channel_id=1, source_target_pairs={{0,8},{4,12},{8,0},{12,4},{16,24},{20,28},{24,16},{28,20},{1,9},{5... | collective-permute-start | bytes 663560 | tf_op jit(solution)/shard_map/ppermute | solution.py:551
  77.9 7.2 %collective-permute-start.20 = (bf16[2,72,384]{2,1,0:T(8,128)(2,1)S(1)}, bf16[2,72,384]{2,1,0:T(8,128)(2,1)S(1)}, u32[]{:S(2)}, u32[]{:S(2)}) collective-permute-start(bf16[2,72,384]{2,1,0:T(8,128)(2,1)S(1)} %slice.66), channel_id=1, source_target_pairs={{0,8},{4,12},{8,0},{12,4},{16,24},{20,28},{24,16},{28,20},{1,9},{5... | collective-permute-start | bytes 331784 | tf_op jit(solution)/shard_map/ppermute | solution.py:551
  78.2 7.3 %collective-permute-start.18 = (bf16[1,144,384]{2,1,0:T(8,128)(2,1)S(1)}, bf16[1,144,384]{2,1,0:T(8,128)(2,1)S(1)}, u32[]{:S(2)}, u32[]{:S(2)}) collective-permute-start(bf16[1,144,384]{2,1,0:T(8,128)(2,1)S(1)} %slice.64), channel_id=1, source_target_pairs={{0,16},{4,20},{8,24},{12,28},{16,0},{20,4},{24,8},{28,12},{1,17},{... | collective-permute-start | bytes 331784 | tf_op jit(solution)/shard_map/ppermute | solution.py:551
  85.1 5.9 %collective-permute-start.30 = (bf16[1,72,384]{2,1,0:T(8,128)(2,1)S(1)}, bf16[1,72,384]{2,1,0:T(8,128)(2,1)S(1)}, u32[]{:S(2)}, u32[]{:S(2)}) collective-permute-start(bf16[1,72,384]{2,1,0:T(8,128)(2,1)S(1)} %slice.72), channel_id=1, source_target_pairs={{0,16},{4,20},{8,24},{12,28},{16,0},{20,4},{24,8},{28,12},{1,17},{... | collective-permute-start | bytes 165896 | tf_op jit(solution)/shard_map/ppermute | solution.py:551
  89.5 6.6 %collective-permute-start.21 = (bf16[4,56,576]{2,1,0:T(8,128)(2,1)S(1)}, bf16[4,56,576]{2,1,0:T(8,128)(2,1)S(1)}, u32[]{:S(2)}, u32[]{:S(2)}) collective-permute-start(bf16[4,56,576]{2,1,0:T(8,128)(2,1)S(1)} %get-tuple-element.118), channel_id=1, source_target_pairs={{0,4},{4,0},{8,12},{12,8},{16,20},{20,16},{24,28},{28,24},{1,5},{5... | collective-permute-start | bytes 774152 | tf_op jit(solution)/shard_map/ppermute | solution.py:551
  91.1 10.4 %collective-permute-start.31 = (bf16[1,72,384]{2,1,0:T(8,128)(2,1)S(1)}, bf16[1,72,384]{2,1,0:T(8,128)(2,1)S(1)}, u32[]{:S(2)}, u32[]{:S(2)}) collective-permute-start(bf16[1,72,384]{2,1,0:T(8,128)(2,1)S(1)} %add_convert_fusion.8), channel_id=1, source_target_pairs={{0,16},{4,20},{8,24},{12,28},{16,0},{20,4},{24,8},{28,12},{1,17},{... | collective-permute-start | bytes 165896 | tf_op jit(solution)/shard_map/ppermute | solution.py:551
  96.2 6.6 %collective-permute-start.22 = (bf16[2,56,576]{2,1,0:T(8,128)(2,1)S(1)}, bf16[2,56,576]{2,1,0:T(8,128)(2,1)S(1)}, u32[]{:S(2)}, u32[]{:S(2)}) collective-permute-start(bf16[2,56,576]{2,1,0:T(8,128)(2,1)S(1)} %slice.68), channel_id=1, source_target_pairs={{0,8},{4,12},{8,0},{12,4},{16,24},{20,28},{24,16},{28,20},{1,9},{5... | collective-permute-start | bytes 387080 | tf_op jit(solution)/shard_map/ppermute | solution.py:551
  98.0 7.8 %collective-permute-start.27 = (bf16[1,144,384]{2,1,0:T(8,128)(2,1)S(1)}, bf16[1,144,384]{2,1,0:T(8,128)(2,1)S(1)}, u32[]{:S(2)}, u32[]{:S(2)}) collective-permute-start(bf16[1,144,384]{2,1,0:T(8,128)(2,1)S(1)} %add_convert_fusion.6), channel_id=1, source_target_pairs={{0,16},{4,20},{8,24},{12,28},{16,0},{20,4},{24,8},{28,12},{1,17},{... | collective-permute-start | bytes 331784 | tf_op jit(solution)/shard_map/ppermute | solution.py:551
  101.4 16.9 %collective-permute-start.32 = (bf16[2,72,384]{2,1,0:T(8,128)(2,1)S(1)}, bf16[2,72,384]{2,1,0:T(8,128)(2,1)S(1)}, u32[]{:S(2)}, u32[]{:S(2)}) collective-permute-start(bf16[2,72,384]{2,1,0:T(8,128)(2,1)S(1)} %pad_maximum_fusion.5), channel_id=1, source_target_pairs={{0,8},{4,12},{8,0},{12,4},{16,24},{20,28},{24,16},{28,20},{1,9},{5... | collective-permute-start | bytes 331784 | tf_op jit(solution)/shard_map/ppermute | solution.py:551
  102.9 5.8 %collective-permute-start.23 = (bf16[1,56,576]{2,1,0:T(8,128)(2,1)S(1)}, bf16[1,56,576]{2,1,0:T(8,128)(2,1)S(1)}, u32[]{:S(2)}, u32[]{:S(2)}) collective-permute-start(bf16[1,56,576]{2,1,0:T(8,128)(2,1)S(1)} %slice.70), channel_id=1, source_target_pairs={{0,16},{4,20},{8,24},{12,28},{16,0},{20,4},{24,8},{28,12},{1,17},{... | collective-permute-start | bytes 193544 | tf_op jit(solution)/shard_map/ppermute | solution.py:551
  105.9 6.6 %collective-permute-start.28 = (bf16[2,144,384]{2,1,0:T(8,128)(2,1)S(1)}, bf16[2,144,384]{2,1,0:T(8,128)(2,1)S(1)}, u32[]{:S(2)}, u32[]{:S(2)}) collective-permute-start(bf16[2,144,384]{2,1,0:T(8,128)(2,1)S(1)} %pad_maximum_fusion.2), channel_id=1, source_target_pairs={{0,8},{4,12},{8,0},{12,4},{16,24},{20,28},{24,16},{28,20},{1,9},{5... | collective-permute-start | bytes 663560 | tf_op jit(solution)/shard_map/ppermute | solution.py:551
  108.7 5.9 %collective-permute-start.24 = (bf16[1,56,576]{2,1,0:T(8,128)(2,1)S(1)}, bf16[1,56,576]{2,1,0:T(8,128)(2,1)S(1)}, u32[]{:S(2)}, u32[]{:S(2)}) collective-permute-start(bf16[1,56,576]{2,1,0:T(8,128)(2,1)S(1)} %add_convert_fusion.7), channel_id=1, source_target_pairs={{0,16},{4,20},{8,24},{12,28},{16,0},{20,4},{24,8},{28,12},{1,17},{... | collective-permute-start | bytes 193544 | tf_op jit(solution)/shard_map/ppermute | solution.py:551
  112.5 16.7 %collective-permute-start.29 = (bf16[4,144,384]{2,1,0:T(8,128)(2,1)S(1)}, bf16[4,144,384]{2,1,0:T(8,128)(2,1)S(1)}, u32[]{:S(2)}, u32[]{:S(2)}) collective-permute-start(bf16[4,144,384]{2,1,0:T(8,128)(2,1)S(1)} %pad_maximum_fusion.one_lo), channel_id=1, source_target_pairs={{0,4},{4,0},{8,12},{12,8},{16,20},{20,16},{24,28},{28,24},{1,5},{5... | collective-permute-start | bytes 1327112 | tf_op jit(solution)/shard_map/ppermute | solution.py:551
  114.7 6.8 %collective-permute-start.25 = (bf16[2,56,576]{2,1,0:T(8,128)(2,1)S(1)}, bf16[2,56,576]{2,1,0:T(8,128)(2,1)S(1)}, u32[]{:S(2)}, u32[]{:S(2)}) collective-permute-start(bf16[2,56,576]{2,1,0:T(8,128)(2,1)S(1)} %pad_maximum_fusion.4), channel_id=1, source_target_pairs={{0,8},{4,12},{8,0},{12,4},{16,24},{20,28},{24,16},{28,20},{1,9},{5... | collective-permute-start | bytes 387080 | tf_op jit(solution)/shard_map/ppermute | solution.py:551
  118.4 10.8 %collective-permute-start.33 = (bf16[4,72,384]{2,1,0:T(8,128)(2,1)S(1)}, bf16[4,72,384]{2,1,0:T(8,128)(2,1)S(1)}, u32[]{:S(2)}, u32[]{:S(2)}) collective-permute-start(bf16[4,72,384]{2,1,0:T(8,128)(2,1)S(1)} %pad_maximum_fusion.3.two_lo), channel_id=1, source_target_pairs={{0,4},{4,0},{8,12},{12,8},{16,20},{20,16},{24,28},{28,24},{1,5},{5... | collective-permute-start | bytes 663560 | tf_op jit(solution)/shard_map/ppermute | solution.py:551
  121.5 10.8 %collective-permute-start.26 = (bf16[4,56,576]{2,1,0:T(8,128)(2,1)S(1)}, bf16[4,56,576]{2,1,0:T(8,128)(2,1)S(1)}, u32[]{:S(2)}, u32[]{:S(2)}) collective-permute-start(bf16[4,56,576]{2,1,0:T(8,128)(2,1)S(1)} %pad_maximum_fusion.1.first), channel_id=1, source_target_pairs={{0,4},{4,0},{8,12},{12,8},{16,20},{20,16},{24,28},{28,24},{1,5},{5... | collective-permute-start | bytes 774152 | tf_op jit(solution)/shard_map/ppermute | solution.py:551
  (7 other events, 85.0 us)

commit v4 on v3

--- a/solution.py
+++ b/solution.py
@@ -19,7 +19,9 @@
 QW = PAIRS * 128
 GROUP = 4
 PREPARE_VMEM = 60
-MICROS = (7, 6, 6, 3, 4, 4)
+TURNED = (0, 0, 0)
+TIES = ((1, 0), (1, 1), (2, 1))
+MICROS = (1, 6, 6, 3, 4, 4)
 F32 = jnp.float32
 BF16 = jnp.bfloat16
 
@@ -96,19 +98,20 @@
 
 
 def prepare_kernel(idx, wq, wkv, wo, wgu, tokens, grad, positions, gain_attn, gain_mlp,
-                   own_ref, send_ref, gu_ref, cot_ref, kv_all, tok_all, grad_all, codes, sem):
+                   own_ref, send_ref, gu_one, gu_two, cot_ref, kv_all, tok_all, grad_all, codes, sem):
     width, kv_width = wkv.shape
     model = own_ref.shape[1]
     side = idx[1] & 1
-    ff = gu_ref.shape[1]
-    across = pl.ds(pl.multiple_of(side * ff, 128), ff)
+    part = gu_one.shape[1]
+    across = [pl.ds(pl.multiple_of((2 * side + number) * part, 128), part) for number in range(2)]
     waits = [
         pltpu.make_async_copy(wkv, kv_all, sem.at[0]),
         pltpu.make_async_copy(wq, own_ref.at[pl.ds(0, width)], sem.at[1]),
         pltpu.make_async_copy(wo, own_ref.at[pl.ds(width, width)], sem.at[2]),
         pltpu.make_async_copy(tokens, tok_all, sem.at[3]),
         pltpu.make_async_copy(grad, grad_all, sem.at[4]),
-        pltpu.make_async_copy(wgu.at[:, across], gu_ref, sem.at[5]),
+        pltpu.make_async_copy(wgu.at[:, across[0]], gu_one, sem.at[5]),
+        pltpu.make_async_copy(wgu.at[:, across[1]], gu_two, sem.at[6]),
     ]
     for wait in waits:
         wait.start()
@@ -137,6 +140,7 @@
     waits[4].wait()
     cot_ref[...] = (grad_all[...].T.astype(F32) * live_rows(idx)).astype(BF16)
     waits[5].wait()
+    waits[6].wait()
 
 
 def live_rows(idx):
@@ -248,18 +252,22 @@
     nmid_ref[...] = (stream_mid * inverse_rms(stream_mid) * gain_mlp).astype(BF16)
 
 
-def bit_reverse(value, total):
+def masks(total, turned):
+    steps = []
+    while 2 ** len(steps) < total:
+        steps.append(2 ** len(steps))
+    return steps[turned:] + steps[:turned]
+
+
+def slab_place(value, steps):
     result = jnp.zeros_like(value)
-    bit = 1
-    while bit < total:
-        result = result * 2 + (value & 1)
-        value = value >> 1
-        bit *= 2
+    for mask in steps:
+        result = result * 2 + ((value & mask) != 0).astype(jnp.int32)
     return result
 
 
-def spread(target, member, n_rep, first_row, slab, value):
-    to = bit_reverse(member ^ slab, n_rep)
+def spread(target, member, steps, first_row, slab, value):
+    to = slab_place(member ^ slab, steps)
     target[to, first_row : first_row + value.shape[0], :] = value.astype(BF16)
 
 
@@ -274,6 +282,7 @@
     shard = idx[0]
     member = idx[1]
     first = 0 if first_call else 2
+    steps = masks(n_rep, TURNED[0] if first_call else TURNED[1])
     model = nmid_ref.shape[1]
     ff = w_full.shape[1] // 2
     chunk = ff // n_shard
@@ -284,14 +293,18 @@
     if first_call:
         width = model // n_shard
         side = member & 1
-        pieces = [(0, wgu[0], None), (1, wgu[1], None), (2, wgu[2], side), (2, wgu[3], 1 - side),
-                  (3, wgu[4], side), (3, wgu[5], 1 - side)]
+        pieces = [(0, wgu[0], None), (1, wgu[1], None)]
+        for number in range(8):
+            part, rest = divmod(number, 4)
+            which = side if rest < 2 else 1 - side
+            pieces.append((2 + part, wgu[2 + number], 2 * which + rest % 2))
         for number, (part, source, which) in enumerate(pieces):
             down = pl.ds(pl.multiple_of((shard ^ part) * width, 16), width)
             if which is None:
                 target = w_full.at[down]
             else:
-                target = w_full.at[down, pl.ds(pl.multiple_of(which * ff, 128), ff)]
+                size = ff // 2
+                target = w_full.at[down, pl.ds(pl.multiple_of(which * size, 128), size)]
             waits.append(pltpu.make_async_copy(source, target, sem.at[number]))
         for part in range(n_shard):
             waits.append(
@@ -323,13 +336,13 @@
         rows = rows // 2
         grad_down = mm_tn(d_branch, own_hidden)
         for slab in range(n_rep):
-            spread(all_ref, member, n_rep, rows, slab, grad_down[slab * rows : (slab + 1) * rows])
+            spread(all_ref, member, steps, rows, slab, grad_down[slab * rows : (slab + 1) * rows])
     slab = 0
     for piece in (d_gate, d_up):
         grad = mm_tn(own_ref[...], piece)
         for column in range(0, 2 * chunk, chunk):
             for row in range(0, grad.shape[0], rows):
-                spread(all_ref, member, n_rep, 0, slab, grad[row : row + rows, column : column + chunk])
+                spread(all_ref, member, steps, 0, slab, grad[row : row + rows, column : column + chunk])
                 slab += 1
     middle = n_rep // 2
     lo_ref[...] = all_ref[:middle]
@@ -451,7 +464,7 @@
     rows = a_all.shape[0] // n_rep
     middle = n_rep // 2
     for slab in range(n_rep):
-        to = bit_reverse(idx[1] ^ slab, n_rep)
+        to = slab_place(idx[1] ^ slab, masks(n_rep, TURNED[2]))
         piece = a_all[slab * rows : (slab + 1) * rows, :].astype(BF16)
 
         @pl.when(to < middle)
@@ -472,23 +485,22 @@
     ).T
 
 
-def fetch(first, second, member, slab, n_rep, target, rows):
-    at = bit_reverse(member ^ slab, n_rep)
-    middle = n_rep // 2
+def fetch(first, second, slab, steps, place):
+    at = slab_place(slab, steps)
+    middle = first.shape[0]
 
     @pl.when(at < middle)
     def _():
-        target[pl.ds(slab * rows, rows), :] = first[at].astype(F32)
+        place(first[at].astype(F32))
 
     @pl.when(at >= middle)
     def _():
-        target[pl.ds(slab * rows, rows), :] = second[at - middle].astype(F32)
+        place(second[at - middle].astype(F32))
 
 
 def unpack_mlp_kernel(n_rep, n_shard, idx, one_lo, one_hi, two_lo, two_hi, down_ref, gu_ref):
     shard = idx[0]
     member = idx[1]
-    middle = n_rep // 2
     rows, chunk = two_lo.shape[1:]
     ff = gu_ref.shape[1] // 2
     groups = gu_ref.shape[0] // rows
@@ -499,33 +511,29 @@
         base = ((shard ^ (2 * pair)) >> 1) * 2 * chunk + column * chunk + up * ff
         gu_ref[group * rows : (group + 1) * rows, pl.ds(pl.multiple_of(base, 128), chunk)] = piece
 
+    def place_one(slab, piece):
+        place_gateup(slab, 0, piece[:rows])
+        down_ref[slab * rows : (slab + 1) * rows, :] = piece[rows:]
+
     for slab in range(n_rep):
-        at = bit_reverse(member ^ slab, n_rep)
-
-        def place(one, two, where):
-            piece = one[where].astype(F32)
-            place_gateup(slab, 0, piece[:rows])
-            down_ref[slab * rows : (slab + 1) * rows, :] = piece[rows:]
-            place_gateup(slab, 1, two[where].astype(F32))
-
-        @pl.when(at < middle)
-        def _():
-            place(one_lo, two_lo, at)
-
-        @pl.when(at >= middle)
-        def _():
-            place(one_hi, two_hi, at - middle)
+        fetch(one_lo, one_hi, member ^ slab, masks(n_rep, TURNED[0]), functools.partial(place_one, slab))
+        fetch(two_lo, two_hi, member ^ slab, masks(n_rep, TURNED[1]), functools.partial(place_gateup, slab, 1))
 
 
 def unpack_attn_kernel(n_rep, idx, first, second, q_ref, kv_ref, o_ref, gain_ref, a_all):
     rows = first.shape[1]
+
+    def place(slab, piece):
+        a_all[slab * rows : (slab + 1) * rows, :] = piece
+
     for slab in range(n_rep):
-        fetch(first, second, idx[1], slab, n_rep, a_all, rows)
+        fetch(first, second, idx[1] ^ slab, masks(n_rep, TURNED[2]), functools.partial(place, slab))
     width = q_ref.shape[0]
     q_ref[...] = a_all[:width, :]
     o_ref[...] = a_all[width : 2 * width, :]
     kv_ref[...] = a_all[2 * width : 3 * width, : kv_ref.shape[1]]
-    gain_ref[...] = a_all[3 * width : 3 * width + 8, :]
+    rows = a_all[3 * width :, :].astype(BF16)
+    gain_ref[...] = mm(rows, own_columns(idx[0], rows.shape[1], width))
 
 
 def call(body, operands, outs, scratch=(), micros=1, vmem=24, raw=()):
@@ -551,21 +559,17 @@
     return lax.ppermute(value, axis, [(member, member ^ mask) for member in range(total)])
 
 
-def replica_steps(low, high, total):
-    mask = 1
-    while True:
+def replica_steps(low, high, total, turned):
+    steps = masks(total, turned)
+    for mask in steps:
         arrived = exchange(high, "rep", total, mask)
         held = (low.astype(F32) + arrived.astype(F32)).astype(BF16)
-        yield held
-        mask *= 2
-        if mask == total:
-            break
+        waited = yield held
+        held = held if waited is None else after(held, *waited)
         low, high = held[: held.shape[0] // 2], held[held.shape[0] // 2 :]
-    mask = total // 2
-    while True:
+    for mask in reversed(steps):
         arrived = exchange(held, "rep", total, mask)
-        mask //= 2
-        if mask == 0:
+        if mask == steps[0]:
             yield held, arrived
             return
         held = jnp.concatenate([held, arrived], axis=0)
@@ -593,14 +597,15 @@
     member = lax.axis_index("rep").astype(jnp.int32)
     idx = jnp.stack([shard, member, seq_count[0]])
     pack_rows = 2 * width + width * kv_width // model
-    own_full, half_full, gu_half, cotangent = call(
+    own_full, half_full, gu_one, gu_two, cotangent = call(
         prepare_kernel,
         [idx, w_query[0], w_keyval[0], w_out[0], w_gateup[0], tokens.T, out_grad.T, positions[None], gain_attn,
          gain_mlp],
         (
             shape((pack_rows + row_count + 16, model), BF16),
             shape((pack_rows // 2 + row_count + 16, model), BF16),
-            shape((width, ff), BF16),
+            shape((width, ff // 2), BF16),
+            shape((width, ff // 2), BF16),
             shape((row_count, model), BF16),
         ),
         [
@@ -608,19 +613,21 @@
             pltpu.VMEM((model, row_count), BF16),
             pltpu.VMEM((model, row_count), BF16),
             pltpu.VMEM((16, model), F32),
-            pltpu.SemaphoreType.DMA((6,)),
+            pltpu.SemaphoreType.DMA((7,)),
         ],
         micros=1,
         vmem=PREPARE_VMEM,
         raw=range(1, 7),
     )
     direct = exchange(half_full, "fsdp", n_shard, 2)
-    around = exchange(direct[: pack_rows // 2], "rep", n_rep, 1)
+    direct_one = exchange(gu_one, "fsdp", n_shard, 2)
+    around = exchange((direct[: pack_rows // 2]), "rep", n_rep, 1)
     packs = [own_full, exchange(own_full, "fsdp", n_shard, 1), direct, around,
              exchange(direct, "fsdp", n_shard, 1), exchange(around, "fsdp", n_shard, 1)]
-    gu_direct = exchange(gu_half, "fsdp", n_shard, 2)
-    idx_late, gu_direct = lax.optimization_barrier((idx, gu_direct))
-    gu_around = exchange(gu_direct, "rep", n_rep, 1)
+    direct_two = exchange(gu_two, "fsdp", n_shard, 2)
+    idx_late = after(idx, direct_one, direct_two)
+    around_one = exchange(direct_one, "rep", n_rep, 1)
+    around_two = exchange(direct_two, "rep", n_rep, 1)
     cot_across = exchange(cotangent, "fsdp", n_shard, 2)
     down_across = exchange(w_down[0].T, "fsdp", n_shard, 2)
     (x_all, normed, query, keyval, mixed, mid, normed_mid, cosine, sine, gains, wq_full, wkv_full, wo_full) = call(
@@ -658,11 +665,12 @@
     slab_rows = width * 4 // n_rep
     a_rows = 3 * width + 16
     a_slab = (a_rows // n_rep, model)
-    gu_own, cot_own, down_own, gu_direct, gu_around, cot_across, down_across, _ = lax.optimization_barrier(
-        (w_gateup[0], cotangent, w_down[0].T, gu_direct, gu_around, cot_across, down_across, gains)
-    )
-    gu = [gu_own, exchange(gu_own, "fsdp", n_shard, 1), gu_direct, gu_around,
-          exchange(gu_direct, "fsdp", n_shard, 1), exchange(gu_around, "fsdp", n_shard, 1)]
+    gu_beside = [exchange(piece, "fsdp", n_shard, 1) for piece in (w_gateup[0], direct_one, direct_two)]
+    cot_own, down_own, cot_across, down_across, around_one, around_two, _ = lax.optimization_barrier(
+        (cotangent, w_down[0].T, cot_across, down_across, around_one, around_two, gains)
+    )
+    around_beside = [exchange(piece, "fsdp", n_shard, 1) for piece in (around_one, around_two)]
+    gu = [w_gateup[0], gu_beside[0], direct_one, direct_two, around_one, around_two] + gu_beside[1:] + around_beside
     cot = [cot_own, exchange(cot_own, "fsdp", n_shard, 1), cot_across, exchange(cot_across, "fsdp", n_shard, 1)]
     down_beside = exchange(down_own, "fsdp", n_shard, 1)
     half_act, half_dn, one_lo, one_hi, dcot, gu_full, own_mid = call(
@@ -681,12 +689,12 @@
             pltpu.VMEM((n_rep, 2 * slab_rows, chunk), BF16),
             pltpu.VMEM((model, 2 * chunk), BF16),
             pltpu.VMEM((group_rows, 2 * chunk), BF16),
-            pltpu.SemaphoreType.DMA((6,)),
+            pltpu.SemaphoreType.DMA((10,)),
             pltpu.SemaphoreType.DMA((2,)),
             pltpu.SemaphoreType.DMA((n_shard,)),
         ],
         micros=MICROS[1],
-        raw=range(3, 5 + 2 * n_shard + 2),
+        raw=range(3, 15 + n_shard),
     )
     down_across, _ = lax.optimization_barrier((down_across, half_act))
     down_corner = exchange(down_across, "fsdp", n_shard, 1)
@@ -707,8 +715,8 @@
         micros=MICROS[2],
         raw=(3, 4),
     )
-    one = replica_steps(one_lo, one_hi, n_rep)
-    two = replica_steps(two_lo, two_hi, n_rep)
+    one = replica_steps(one_lo, one_hi, n_rep, TURNED[0])
+    two = replica_steps(two_lo, two_hi, n_rep, TURNED[1])
     d_attn, d_mixed, d_mid, part_out, part_gain = call(
         functools.partial(residual_backward_kernel, n_shard),
         [idx, mid, d_normed_mid, dcot, mixed, gains, wo_full],
@@ -721,9 +729,19 @@
         ),
         micros=MICROS[3],
     )
+    reached = [0, 0]
+    results = {}
+
+    def advance(kernel):
+        for chain, steps in enumerate((one, two)):
+            while reached[chain] < TIES[kernel][chain]:
+                results[chain] = next(steps)
+                reached[chain] += 1
+        return [results[chain] for chain in results]
+
     halves = []
     for first_row in (0, group_rows // 2):
-        d_mixed = after(d_mixed, *([next(one)] if first_row == 0 else [next(one), next(two), halves[0][0]]))
+        d_mixed = after(d_mixed, *advance(len(halves)), *(half[0] for half in halves))
         halves.append(
             call(
                 functools.partial(heads_backward_kernel, first_row),
@@ -732,7 +750,7 @@
                 micros=MICROS[4],
             )
         )
-    d_mid = after(d_mid, next(one), next(two))
+    d_mid = after(d_mid, *advance(2))
     in_grad, a_lo, a_hi = call(
         functools.partial(input_backward_kernel, n_shard, n_rep),
         [idx, x_all, normed, gains, wq_full, wkv_full, d_mid, part_out, part_gain,
@@ -750,26 +768,25 @@
         micros=MICROS[5],
     )
     one, two = last_of(one), last_of(two)
-    attn = last_of(replica_steps(a_lo, a_hi, n_rep))
+    attn = last_of(replica_steps(a_lo, a_hi, n_rep, TURNED[2]))
     grad_down, grad_gateup = call(
         functools.partial(unpack_mlp_kernel, n_rep, n_shard),
         [idx] + list(one) + list(two),
         (shape((model, chunk), F32), shape((width, 2 * ff), F32)),
         micros=3,
     )
-    grad_query, grad_keyval, grad_out, gain_rows = call(
+    grad_query, grad_keyval, grad_out, own_gains = call(
         functools.partial(unpack_attn_kernel, n_rep),
         [idx] + list(attn),
         (
             shape((width, model), F32),
             shape((width, kv_width), F32),
             shape((width, model), F32),
-            shape((8, model), F32),
+            shape((a_rows - 3 * width, width), F32),
         ),
         [pltpu.VMEM((a_rows, model), F32)],
         micros=2,
     )
-    own_gains = lax.dynamic_slice(gain_rows, (0, shard * width), (2, width))
     return (
         out_act.T,
         in_grad.T,
@@ -779,7 +796,7 @@
         grad_gateup[None],
         grad_down.T[None],
         own_gains[:1],
-        own_gains[1:],
+        own_gains[1:2],
     )
 
 

time: 135 us -> 133 us (0.985)
  starting transfers between devices: 48.1 us -> 31.1 us
  waiting for transfers between devices: 37.5 us -> 52.9 us
    ppermute x34 -> x38, starting transfers between devices: 48.1 us -> 31.1 us  [exchange(): lax.ppermute(value, axis, [(member, member ^ mask) for member in range(to...]
    ppermute x34 -> x38, waiting for transfers between devices: 37.5 us -> 52.9 us  [exchange(): lax.ppermute(value, axis, [(member, member ^ mask) for member in range(to...]
  transfers between devices with their start and end apart: 34 -> 38, of which waited for: 15 -> 21; matrix products, arithmetic and copies ran while one was open for 1% -> 1% of each run, Pallas kernels for 23% -> 24%
where the time goes in v4:
time: 133 us
  waiting for transfers between devices  52.9 us (40%)
  Pallas kernels  44.5 us (33%)
  starting transfers between devices  31.1 us (23%)
  local copies, waits for them, and re-layouts  1.78 us (1%)
  between operations  1.56 us (1%)
    ppermute x38, waiting for transfers between devices, exchange(): lax.ppermute(value, axis, [(member, member ^ mask) for member in range(to...  52.9 us
    pallas_call x10, Pallas kernels, call(): pl.pallas_call(body, out_shape=outs, in_specs=[pl.BlockSpec(memory_space=...  44.5 us
    ppermute x38, starting transfers between devices, exchange(): lax.ppermute(value, axis, [(member, member ^ mask) for member in range(to...  31.1 us
  transfers between devices with their start and end apart: 38, of which 21 were waited for; matrix products, arithmetic and copies ran while one was open for 1% of the time, Pallas kernels for 24%

profile of v4, /device:TPU:0, one launch (start us, length us, event | category | flops | bytes accessed | tf_op | source)
XLA Modules:
  0.0 133.1 jit_solution(2558632830161115738)
XLA Ops:
  1.9 3.4 %shard_map.178 = (bf16[528,576]{1,0:T(8,128)(2,1)}, bf16[336,576]{1,0:T(8,128)(2,1)}, bf16[144,768]{1,0:T(8,128)(2,1)}, bf16[144,768]{1,0:T(8,128)(2,1)}, bf16[128,576]{1,0:T(8,128)(2,1)}) custom-call(s32[3]{0:T(128)} %pad_add_fusion.idx, bf16[144,576]{1,0:T(8,128)(2,1)} %bitcast.27, bf16[144,384]{1,0:T(8,128)(2,1)} %bitcast.31, bf16[144,576]{1,0:T(8,128)(2,1)} %bitcast.28, ...), custom_call_target="tpu_custom_call" | custom-call | flops 1000000000 | bytes 1048576 | tf_op jit(solution)/shard_map/pallas_call | solution.py:543
  5.3 3.0 %collective-permute-start.3 = (bf16[336,576]{1,0:T(8,128)(2,1)}, bf16[336,576]{1,0:T(8,128)(2,1)S(1)}, u32[]{:S(2)}, u32[]{:S(2)}) collective-permute-start(bf16[336,576]{1,0:T(8,128)(2,1)} %get-tuple-element.70), channel_id=1, source_target_pairs={{0,2},{1,3},{2,0},{3,1},{4,6},{5,7},{6,4},{7,5},{8,10},{9,11},{10,... | collective-permute-start | bytes 1161224 | tf_op jit(solution)/shard_map/ppermute | solution.py:559
  8.5 1.9 %collective-permute-start.1 = (bf16[144,768]{1,0:T(8,128)(2,1)}, bf16[144,768]{1,0:T(8,128)(2,1)S(1)}, u32[]{:S(2)}, u32[]{:S(2)}) collective-permute-start(bf16[144,768]{1,0:T(8,128)(2,1)} %get-tuple-element.67), channel_id=1, source_target_pairs={{0,2},{1,3},{2,0},{3,1},{4,6},{5,7},{6,4},{7,5},{8,10},{9,11},{10,... | collective-permute-start | bytes 663560 | tf_op jit(solution)/shard_map/ppermute | solution.py:559
  10.4 8.9 %collective-permute-done.3.refs_2_ = bf16[336,576]{1,0:T(8,128)(2,1)S(1)} collective-permute-done((bf16[336,576]{1,0:T(8,128)(2,1)}, bf16[336,576]{1,0:T(8,128)(2,1)S(1)}, u32[]{:S(2)}, u32[]{:S(2)}) %collective-permute-start.3) | collective-permute-done | bytes 387104 | tf_op jit(solution)/shard_map/ppermute | solution.py:559
  19.3 2.2 %collective-permute-start.4 = (bf16[192,576]{1,0:T(8,128)(2,1)S(1)}, bf16[192,576]{1,0:T(8,128)(2,1)S(1)}, u32[]{:S(2)}, u32[]{:S(2)}) collective-permute-start(bf16[192,576]{1,0:T(8,128)(2,1)S(1)} %slice.60), channel_id=1, source_target_pairs={{0,4},{4,0},{8,12},{12,8},{16,20},{20,16},{24,28},{28,24},{1,5},{5... | collective-permute-start | bytes 663560 | tf_op jit(solution)/shard_map/ppermute | solution.py:559
  21.5 2.6 %collective-permute-done.refs_10_ = bf16[144,768]{1,0:T(8,128)(2,1)S(1)} collective-permute-done((bf16[144,768]{1,0:T(8,128)(2,1)}, bf16[144,768]{1,0:T(8,128)(2,1)S(1)}, u32[]{:S(2)}, u32[]{:S(2)}) %collective-permute-start) | collective-permute-done | bytes 221216 | tf_op jit(solution)/shard_map/ppermute | solution.py:559
  24.0 3.9 %collective-permute-done.1.refs_11_ = bf16[144,768]{1,0:T(8,128)(2,1)S(1)} collective-permute-done((bf16[144,768]{1,0:T(8,128)(2,1)}, bf16[144,768]{1,0:T(8,128)(2,1)S(1)}, u32[]{:S(2)}, u32[]{:S(2)}) %collective-permute-start.1) | collective-permute-done | bytes 221216 | tf_op jit(solution)/shard_map/ppermute | solution.py:559
  27.9 1.7 %collective-permute-start.8 = (bf16[576,384]{1,0:T(8,128)(2,1)S(1)}, bf16[576,384]{1,0:T(8,128)(2,1)S(1)}, u32[]{:S(2)}, u32[]{:S(2)}) collective-permute-start(bf16[576,384]{1,0:T(8,128)(2,1)S(1)} %bitcast.24), channel_id=1, source_target_pairs={{0,2},{1,3},{2,0},{3,1},{4,6},{5,7},{6,4},{7,5},{8,10},{9,11},{10,... | collective-permute-start | bytes 1327112 | tf_op jit(solution)/shard_map/ppermute | solution.py:559
  29.7 1.6 %collective-permute-start.9 = (bf16[144,768]{1,0:T(8,128)(2,1)S(1)}, bf16[144,768]{1,0:T(8,128)(2,1)S(1)}, u32[]{:S(2)}, u32[]{:S(2)}) collective-permute-start(bf16[144,768]{1,0:T(8,128)(2,1)S(1)} %collective-permute-done.refs_10_), channel_id=1, source_target_pairs={{0,4},{4,0},{8,12},{12,8},{16,20},{20,16},{24,28},{28,24},{1,5},{5... | collective-permute-start | bytes 663560 | tf_op jit(solution)/shard_map/ppermute | solution.py:559
  33.2 8.6 %shard_map.179 = (bf16[512,576]{1,0:T(8,128)(2,1)S(1)}, bf16[512,576]{1,0:T(8,128)(2,1)S(1)}, bf16[512,640]{1,0:T(8,128)(2,1)S(1)}, bf16[512,384]{1,0:T(8,128)(2...) custom-call(s32[3]{0:T(128)S(1)} %copy-done, ...), custom_call_target="tpu_custom_call" | custom-call | flops 1000000000 | bytes 1048576 | tf_op jit(solution)/shard_map/pallas_call | solution.py:543
  46.9 7.7 %shard_map.180 = (f32[128,576]{1,0:T(8,128)S(1)}, f32[512,576]{1,0:T(8,128)S(1)}, bf16[4,144,384]{2,1,0:T(8,128)(2,1)S(1)}, bf16[4,144,384]{2,1,0:T(8,128)(2,1)S...) custom-call(s32[3]{0:T(128)S(1)} %copy-done, ...), custom_call_target="tpu_custom_call" | custom-call | flops 6000000000 | bytes 1048576 | tf_op jit(solution)/shard_map/pallas_call | solution.py:543
  56.5 6.0 %shard_map.181 = (f32[576,128]{1,0:T(8,128)}, f32[512,576]{1,0:T(8,128)S(1)}, bf16[4,72,384]{2,1,0:T(8,128)(2,1)S(1)}, bf16[4,72,384]{2,1,0:T(8,128)(2,1)S(1)}) custom-call(s32[3]{0:T(128)S(1)} %copy-done, bf16[512,576]{1,0:T(8,128)(2,1)S(1)} %get-tuple-element.71.refs_0_, f32[128,576]{1,0:T(8,128)S(1)} %get-tuple-element.80.refs_1_, ...), custom_call_target="tpu_custom_call" | custom-call | flops 6000000000 | bytes 1048576 | tf_op jit(solution)/shard_map/pallas_call | solution.py:543
  62.5 1.5 %collective-permute-start.22 = (bf16[4,72,384]{2,1,0:T(8,128)(2,1)S(1)}, bf16[4,72,384]{2,1,0:T(8,128)(2,1)S(1)}, u32[]{:S(2)}, u32[]{:S(2)}) collective-permute-start(bf16[4,72,384]{2,1,0:T(8,128)(2,1)S(1)} %get-tuple-element.99), channel_id=1, source_target_pairs={{0,4},{4,0},{8,12},{12,8},{16,20},{20,16},{24,28},{28,24},{1,5},{5... | collective-permute-start | bytes 663560 | tf_op jit(solution)/shard_map/ppermute | solution.py:559
  64.0 4.0 %collective-permute-done.20 = bf16[4,144,384]{2,1,0:T(8,128)(2,1)S(1)} collective-permute-done((bf16[4,144,384]{2,1,0:T(8,128)(2,1)S(1)}, bf16[4,144,384]{2,1,0:T(8,128)(2,1)S(1)}, u32[]{:S(2)}, u32[]{:S(2)}) %collective-permute-start.20) | collective-permute-done | bytes 442400 | tf_op jit(solution)/shard_map/ppermute | solution.py:559
  68.1 2.9 %shard_map.182 = (bf16[512,576]{1,0:T(8,128)(2,1)}, bf16[512,640]{1,0:T(8,128)(2,1)S(1)}, f32[128,576]{1,0:T(8,128)S(1)}, f32[144,576]{1,0:T(8,128)S(1)}, f32[8,576]{1,0:T(8,128)S(1)}) custom-call(s32[3]{0:T(128)S(1)} %copy-done, f32[512,576]{1,0:T(8,128)S(1)} %get-tuple-element.72.refs_1_.mid_ref, f32[512,576]{1,0:T(8,128)S(1)} %get-tuple-element.92.dn_ref, ...), custom_call_target="tpu_custom_call" | custom-call | flops 3000000000 | bytes 1048576 | tf_op jit(solution)/shard_map/pallas_call | solution.py:543
  72.5 3.9 %shard_map.183 = (bf16[256,640]{1,0:T(8,128)(2,1)S(1)}, bf16[256,384]{1,0:T(8,128)(2,1)S(1)}) custom-call(s32[3]{0:T(128)S(1)} %copy-done, bf16[512,640]{1,0:T(8,128)(2,1)S(1)} %get-tuple-element.103.q_ref, bf16[512,384]{1,0:T(8,128)(2,1)S(1)} %get-tuple-element.104.kv_ref, bf16[512,640]{1,0:T(8,128)(2,1)S(1)} %get-tuple-element.110.dmix_ref, ...), custom_call_target="tpu_custom_call" | custom-call | flops 4000000000 | bytes 1048576 | tf_op jit(solution)/shard_map/pallas_call | solution.py:543
  77.0 3.9 %shard_map.184 = (bf16[256,640]{1,0:T(8,128)(2,1)S(1)}, bf16[256,384]{1,0:T(8,128)(2,1)S(1)}) custom-call(s32[3]{0:T(128)S(1)} %copy-done, bf16[512,640]{1,0:T(8,128)(2,1)S(1)} %get-tuple-element.103.q_ref, bf16[512,384]{1,0:T(8,128)(2,1)S(1)} %get-tuple-element.104.kv_ref, bf16[512,640]{1,0:T(8,128)(2,1)S(1)} %get-tuple-element.110.dmix_ref, ...), custom_call_target="tpu_custom_call" | custom-call | flops 4000000000 | bytes 1048576 | tf_op jit(solution)/shard_map/pallas_call | solution.py:543
  81.3 2.7 %collective-permute-start.34 = (bf16[1,72,384]{2,1,0:T(8,128)(2,1)S(1)}, bf16[1,72,384]{2,1,0:T(8,128)(2,1)S(1)}, u32[]{:S(2)}, u32[]{:S(2)}) collective-permute-start(bf16[1,72,384]{2,1,0:T(8,128)(2,1)S(1)} %slice.72), channel_id=1, source_target_pairs={{0,16},{4,20},{8,24},{12,28},{16,0},{20,4},{24,8},{28,12},{1,17},{... | collective-permute-start | bytes 165896 | tf_op jit(solution)/shard_map/ppermute | solution.py:559
  84.0 4.0 %shard_map.185 = (f32[576,128]{1,0:T(8,128)}, bf16[4,56,576]{2,1,0:T(8,128)(2,1)S(1)}, bf16[4,56,576]{2,1,0:T(8,128)(2,1)S(1)}) custom-call(s32[3]{0:T(128)S(1)} %copy-done, bf16[512,576]{1,0:T(8,128)(2,1)S(1)} %get-tuple-element.88.x_ref, bf16[512,576]{1,0:T(8,128)(2,1)S(1)} %get-tuple-element.89.nrm_ref, f32[16,576]{1,0:T(8,128)S(1)} %get-tuple-element.74.gain_ref, ...), custom_call_target="tpu_custom_call" | custom-call | flops 4000000000 | bytes 1048576 | tf_op jit(solution)/shard_map/pallas_call | solution.py:543
  88.0 1.5 %collective-permute-start.23 = (bf16[4,56,576]{2,1,0:T(8,128)(2,1)S(1)}, bf16[4,56,576]{2,1,0:T(8,128)(2,1)S(1)}, u32[]{:S(2)}, u32[]{:S(2)}) collective-permute-start(bf16[4,56,576]{2,1,0:T(8,128)(2,1)S(1)} %get-tuple-element.116), channel_id=1, source_target_pairs={{0,4},{4,0},{8,12},{12,8},{16,20},{20,16},{24,28},{28,24},{1,5},{5... | collective-permute-start | bytes 774152 | tf_op jit(solution)/shard_map/ppermute | solution.py:559
  89.9 2.7 %collective-permute-start.35 = (bf16[1,72,384]{2,1,0:T(8,128)(2,1)S(1)}, bf16[1,72,384]{2,1,0:T(8,128)(2,1)S(1)}, u32[]{:S(2)}, u32[]{:S(2)}) collective-permute-start(bf16[1,72,384]{2,1,0:T(8,128)(2,1)S(1)} %add_convert_fusion.8), channel_id=1, source_target_pairs={{0,16},{4,20},{8,24},{12,28},{16,0},{20,4},{24,8},{28,12},{1,17},{... | collective-permute-start | bytes 165896 | tf_op jit(solution)/shard_map/ppermute | solution.py:559
  92.6 2.0 %collective-permute-done.23 = bf16[4,56,576]{2,1,0:T(8,128)(2,1)S(1)} collective-permute-done((bf16[4,56,576]{2,1,0:T(8,128)(2,1)S(1)}, bf16[4,56,576]{2,1,0:T(8,128)(2,1)S(1)}, u32[]{:S(2)}, u32[]{:S(2)}) %collective-permute-start.23) | collective-permute-done | bytes 258080 | tf_op jit(solution)/shard_map/ppermute | solution.py:559
  96.5 2.8 %collective-permute-done.35 = bf16[1,72,384]{2,1,0:T(8,128)(2,1)S(1)} collective-permute-done((bf16[1,72,384]{2,1,0:T(8,128)(2,1)S(1)}, bf16[1,72,384]{2,1,0:T(8,128)(2,1)S(1)}, u32[]{:S(2)}, u32[]{:S(2)}) %collective-permute-start.35) | collective-permute-done | bytes 55328 | tf_op jit(solution)/shard_map/ppermute | solution.py:559
  99.4 2.6 %collective-permute-done.24 = bf16[2,56,576]{2,1,0:T(8,128)(2,1)S(1)} collective-permute-done((bf16[2,56,576]{2,1,0:T(8,128)(2,1)S(1)}, bf16[2,56,576]{2,1,0:T(8,128)(2,1)S(1)}, u32[]{:S(2)}, u32[]{:S(2)}) %collective-permute-start.24) | collective-permute-done | bytes 129056 | tf_op jit(solution)/shard_map/ppermute | solution.py:559
  102.2 2.4 %collective-permute-done.30 = bf16[1,144,384]{2,1,0:T(8,128)(2,1)S(1)} collective-permute-done((bf16[1,144,384]{2,1,0:T(8,128)(2,1)S(1)}, bf16[1,144,384]{2,1,0:T(8,128)(2,1)S(1)}, u32[]{:S(2)}, u32[]{:S(2)}) %collective-permute-start.30) | collective-permute-done | bytes 110624 | tf_op jit(solution)/shard_map/ppermute | solution.py:559
  104.7 4.8 %collective-permute-done.25 = bf16[1,56,576]{2,1,0:T(8,128)(2,1)S(1)} collective-permute-done((bf16[1,56,576]{2,1,0:T(8,128)(2,1)S(1)}, bf16[1,56,576]{2,1,0:T(8,128)(2,1)S(1)}, u32[]{:S(2)}, u32[]{:S(2)}) %collective-permute-start.25) | collective-permute-done | bytes 64544 | tf_op jit(solution)/shard_map/ppermute | solution.py:559
  109.6 2.3 %collective-permute-done.31 = bf16[2,144,384]{2,1,0:T(8,128)(2,1)S(1)} collective-permute-done((bf16[2,144,384]{2,1,0:T(8,128)(2,1)S(1)}, bf16[2,144,384]{2,1,0:T(8,128)(2,1)S(1)}, u32[]{:S(2)}, u32[]{:S(2)}) %collective-permute-start.31) | collective-permute-done | bytes 221216 | tf_op jit(solution)/shard_map/ppermute | solution.py:559
  112.8 2.0 %collective-permute-done.26 = bf16[1,56,576]{2,1,0:T(8,128)(2,1)S(1)} collective-permute-done((bf16[1,56,576]{2,1,0:T(8,128)(2,1)S(1)}, bf16[1,56,576]{2,1,0:T(8,128)(2,1)S(1)}, u32[]{:S(2)}, u32[]{:S(2)}) %collective-permute-start.26) | collective-permute-done | bytes 64544 | tf_op jit(solution)/shard_map/ppermute | solution.py:559
  116.2 3.8 %collective-permute-done.27 = bf16[2,56,576]{2,1,0:T(8,128)(2,1)S(1)} collective-permute-done((bf16[2,56,576]{2,1,0:T(8,128)(2,1)S(1)}, bf16[2,56,576]{2,1,0:T(8,128)(2,1)S(1)}, u32[]{:S(2)}, u32[]{:S(2)}) %collective-permute-start.27) | collective-permute-done | bytes 129056 | tf_op jit(solution)/shard_map/ppermute | solution.py:559
  121.3 6.5 %collective-permute-done.37.two_hi = bf16[4,72,384]{2,1,0:T(8,128)(2,1)S(1)} collective-permute-done((bf16[4,72,384]{2,1,0:T(8,128)(2,1)S(1)}, bf16[4,72,384]{2,1,0:T(8,128)(2,1)S(1)}, u32[]{:S(2)}, u32[]{:S(2)}) %collective-permute-start.37) | collective-permute-done | bytes 221216 | tf_op jit(solution)/shard_map/ppermute | solution.py:559
  127.7 2.4 %shard_map.187 = (f32[576,384]{1,0:T(8,128)}, f32[144,3072]{1,0:T(8,128)}) custom-call(s32[3]{0:T(128)S(1)} %copy-done, bf16[4,144,384]{2,1,0:T(8,128)(2,1)S(1)} %pad_maximum_fusion.one_lo, bf16[4,144,384]{2,1,0:T(8,128)(2,1)S(1)} %collective-permute-done.32.one_hi, bf16[4,72,384]{2,1,0:T(8,128)(2,1)S(1)} %pad_maximum_fusion.3.two_lo, ...), custom_call_target="tpu_custom_call" | custom-call | flops 3000000000 | bytes 1048576 | tf_op jit(solution)/shard_map/pallas_call | solution.py:543
  130.8 1.8 %shard_map.186 = (f32[144,576]{1,0:T(8,128)}, f32[144,384]{1,0:T(8,128)}, f32[144,576]{1,0:T(8,128)}, f32[16,144]{1,0:T(8,128)S(1)}) custom-call(s32[3]{0:T(128)S(1)} %copy-done, bf16[4,56,576]{2,1,0:T(8,128)(2,1)S(1)} %pad_maximum_fusion.1.first, bf16[4,56,576]{2,1,0:T(8,128)(2,1)S(1)} %collective-permute-done.28.second), custom_call_target="tpu_custom_call" | custom-call | flops 2000000000 | bytes 1048576 | tf_op jit(solution)/shard_map/pallas_call | solution.py:543
  (88 shorter events, 19.8 us)
Async XLA Ops:
  5.3 13.9 %collective-permute-start.3 = (bf16[336,576]{1,0:T(8,128)(2,1)}, bf16[336,576]{1,0:T(8,128)(2,1)S(1)}, u32[]{:S(2)}, u32[]{:S(2)}) collective-permute-start(bf16[336,576]{1,0:T(8,128)(2,1)} %get-tuple-element.70), channel_id=1, source_target_pairs={{0,2},{1,3},{2,0},{3,1},{4,6},{5,7},{6,4},{7,5},{8,10},{9,11},{10,... | collective-permute-start | bytes 1161224 | tf_op jit(solution)/shard_map/ppermute | solution.py:559
  8.3 21.3 %collective-permute-start.2 = (bf16[528,576]{1,0:T(8,128)(2,1)}, bf16[528,576]{1,0:T(8,128)(2,1)S(1)}, u32[]{:S(2)}, u32[]{:S(2)}) collective-permute-start(bf16[528,576]{1,0:T(8,128)(2,1)} %get-tuple-element.69.refs_0_), channel_id=1, source_target_pairs={{0,1},{1,0},{2,3},{3,2},{4,5},{5,4},{6,7},{7,6},{8,9},{9,8},{10,11... | collective-permute-start | bytes 1824776 | tf_op jit(solution)/shard_map/ppermute | solution.py:559
  8.3 15.7 %collective-permute-start = (bf16[144,768]{1,0:T(8,128)(2,1)}, bf16[144,768]{1,0:T(8,128)(2,1)S(1)}, u32[]{:S(2)}, u32[]{:S(2)}) collective-permute-start(bf16[144,768]{1,0:T(8,128)(2,1)} %get-tuple-element.66), channel_id=1, source_target_pairs={{0,2},{1,3},{2,0},{3,1},{4,6},{5,7},{6,4},{7,5},{8,10},{9,11},{10,... | collective-permute-start | bytes 663560 | tf_op jit(solution)/shard_map/ppermute | solution.py:559
  8.5 19.4 %collective-permute-start.1 = (bf16[144,768]{1,0:T(8,128)(2,1)}, bf16[144,768]{1,0:T(8,128)(2,1)S(1)}, u32[]{:S(2)}, u32[]{:S(2)}) collective-permute-start(bf16[144,768]{1,0:T(8,128)(2,1)} %get-tuple-element.67), channel_id=1, source_target_pairs={{0,2},{1,3},{2,0},{3,1},{4,6},{5,7},{6,4},{7,5},{8,10},{9,11},{10,... | collective-permute-start | bytes 663560 | tf_op jit(solution)/shard_map/ppermute | solution.py:559
  19.3 12.0 %collective-permute-start.5 = (bf16[336,576]{1,0:T(8,128)(2,1)S(1)}, bf16[336,576]{1,0:T(8,128)(2,1)S(1)}, u32[]{:S(2)}, u32[]{:S(2)}) collective-permute-start(bf16[336,576]{1,0:T(8,128)(2,1)S(1)} %collective-permute-done.3.refs_2_), channel_id=1, source_target_pairs={{0,1},{1,0},{2,3},{3,2},{4,5},{5,4},{6,7},{7,6},{8,9},{9,8},{10,11... | collective-permute-start | bytes 1161224 | tf_op jit(solution)/shard_map/ppermute | solution.py:559
  19.3 10.4 %collective-permute-start.4 = (bf16[192,576]{1,0:T(8,128)(2,1)S(1)}, bf16[192,576]{1,0:T(8,128)(2,1)S(1)}, u32[]{:S(2)}, u32[]{:S(2)}) collective-permute-start(bf16[192,576]{1,0:T(8,128)(2,1)S(1)} %slice.60), channel_id=1, source_target_pairs={{0,4},{4,0},{8,12},{12,8},{16,20},{20,16},{24,28},{28,24},{1,5},{5... | collective-permute-start | bytes 663560 | tf_op jit(solution)/shard_map/ppermute | solution.py:559
  24.0 21.5 %collective-permute-start.14 = (bf16[144,3072]{1,0:T(8,128)(2,1)S(1)}, bf16[144,3072]{1,0:T(8,128)(2,1)S(1)}, u32[]{:S(2)}, u32[]{:S(2)}) collective-permute-start(bf16[144,3072]{1,0:T(8,128)(2,1)S(1)} %bitcast.22), channel_id=1, source_target_pairs={{0,1},{1,0},{2,3},{3,2},{4,5},{5,4},{6,7},{7,6},{8,9},{9,8},{10,11... | collective-permute-start | bytes 2654216 | tf_op jit(solution)/shard_map/ppermute | solution.py:559
  27.9 14.9 %collective-permute-start.8 = (bf16[576,384]{1,0:T(8,128)(2,1)S(1)}, bf16[576,384]{1,0:T(8,128)(2,1)S(1)}, u32[]{:S(2)}, u32[]{:S(2)}) collective-permute-start(bf16[576,384]{1,0:T(8,128)(2,1)S(1)} %bitcast.24), channel_id=1, source_target_pairs={{0,2},{1,3},{2,0},{3,1},{4,6},{5,7},{6,4},{7,5},{8,10},{9,11},{10,... | collective-permute-start | bytes 1327112 | tf_op jit(solution)/shard_map/ppermute | solution.py:559
  29.7 13.1 %collective-permute-start.9 = (bf16[144,768]{1,0:T(8,128)(2,1)S(1)}, bf16[144,768]{1,0:T(8,128)(2,1)S(1)}, u32[]{:S(2)}, u32[]{:S(2)}) collective-permute-start(bf16[144,768]{1,0:T(8,128)(2,1)S(1)} %collective-permute-done.refs_10_), channel_id=1, source_target_pairs={{0,4},{4,0},{8,12},{12,8},{16,20},{20,16},{24,28},{28,24},{1,5},{5... | collective-permute-start | bytes 663560 | tf_op jit(solution)/shard_map/ppermute | solution.py:559
  31.3 11.5 %collective-permute-start.10 = (bf16[144,768]{1,0:T(8,128)(2,1)S(1)}, bf16[144,768]{1,0:T(8,128)(2,1)S(1)}, u32[]{:S(2)}, u32[]{:S(2)}) collective-permute-start(bf16[144,768]{1,0:T(8,128)(2,1)S(1)} %collective-permute-done.1.refs_11_), channel_id=1, source_target_pairs={{0,4},{4,0},{8,12},{12,8},{16,20},{20,16},{24,28},{28,24},{1,5},{5... | collective-permute-start | bytes 663560 | tf_op jit(solution)/shard_map/ppermute | solution.py:559
  31.8 11.0 %collective-permute-start.7 = (bf16[128,576]{1,0:T(8,128)(2,1)}, bf16[128,576]{1,0:T(8,128)(2,1)S(1)}, u32[]{:S(2)}, u32[]{:S(2)}) collective-permute-start(bf16[128,576]{1,0:T(8,128)(2,1)} %get-tuple-element.76.refs_4_), channel_id=1, source_target_pairs={{0,2},{1,3},{2,0},{3,1},{4,6},{5,7},{6,4},{7,5},{8,10},{9,11},{10,... | collective-permute-start | bytes 442376 | tf_op jit(solution)/shard_map/ppermute | solution.py:559
  42.8 4.1 %collective-permute-start.11 = (bf16[576,384]{1,0:T(8,128)(2,1)S(1)}, bf16[576,384]{1,0:T(8,128)(2,1)S(1)}, u32[]{:S(2)}, u32[]{:S(2)}) collective-permute-start(bf16[576,384]{1,0:T(8,128)(2,1)S(1)} %bitcast.25), channel_id=1, source_target_pairs={{0,1},{1,0},{2,3},{3,2},{4,5},{5,4},{6,7},{7,6},{8,9},{9,8},{10,11... | collective-permute-start | bytes 1327112 | tf_op jit(solution)/shard_map/ppermute | solution.py:559
  43.5 3.4 %collective-permute-start.17 = (bf16[144,768]{1,0:T(8,128)(2,1)S(1)}, bf16[144,768]{1,0:T(8,128)(2,1)S(1)}, u32[]{:S(2)}, u32[]{:S(2)}) collective-permute-start(bf16[144,768]{1,0:T(8,128)(2,1)S(1)} %collective-permute-done.9.refs_12_), channel_id=1, source_target_pairs={{0,1},{1,0},{2,3},{3,2},{4,5},{5,4},{6,7},{7,6},{8,9},{9,8},{10,11... | collective-permute-start | bytes 663560 | tf_op jit(solution)/shard_map/ppermute | solution.py:559
  44.3 2.6 %collective-permute-start.18 = (bf16[144,768]{1,0:T(8,128)(2,1)S(1)}, bf16[144,768]{1,0:T(8,128)(2,1)S(1)}, u32[]{:S(2)}, u32[]{:S(2)}) collective-permute-start(bf16[144,768]{1,0:T(8,128)(2,1)S(1)} %collective-permute-done.10.refs_13_), channel_id=1, source_target_pairs={{0,1},{1,0},{2,3},{3,2},{4,5},{5,4},{6,7},{7,6},{8,9},{9,8},{10,11... | collective-permute-start | bytes 663560 | tf_op jit(solution)/shard_map/ppermute | solution.py:559
  54.9 13.0 %collective-permute-start.20 = (bf16[4,144,384]{2,1,0:T(8,128)(2,1)S(1)}, bf16[4,144,384]{2,1,0:T(8,128)(2,1)S(1)}, u32[]{:S(2)}, u32[]{:S(2)}) collective-permute-start(bf16[4,144,384]{2,1,0:T(8,128)(2,1)S(1)} %get-tuple-element.97), channel_id=1, source_target_pairs={{0,4},{4,0},{8,12},{12,8},{16,20},{20,16},{24,28},{28,24},{1,5},{5... | collective-permute-start | bytes 1327112 | tf_op jit(solution)/shard_map/ppermute | solution.py:559
  62.5 13.9 %collective-permute-start.22 = (bf16[4,72,384]{2,1,0:T(8,128)(2,1)S(1)}, bf16[4,72,384]{2,1,0:T(8,128)(2,1)S(1)}, u32[]{:S(2)}, u32[]{:S(2)}) collective-permute-start(bf16[4,72,384]{2,1,0:T(8,128)(2,1)S(1)} %get-tuple-element.99), channel_id=1, source_target_pairs={{0,4},{4,0},{8,12},{12,8},{16,20},{20,16},{24,28},{28,24},{1,5},{5... | collective-permute-start | bytes 663560 | tf_op jit(solution)/shard_map/ppermute | solution.py:559
  71.0 10.0 %collective-permute-start.21 = (bf16[2,144,384]{2,1,0:T(8,128)(2,1)S(1)}, bf16[2,144,384]{2,1,0:T(8,128)(2,1)S(1)}, u32[]{:S(2)}, u32[]{:S(2)}) collective-permute-start(bf16[2,144,384]{2,1,0:T(8,128)(2,1)S(1)} %slice.62), channel_id=1, source_target_pairs={{0,8},{4,12},{8,0},{12,4},{16,24},{20,28},{24,16},{28,20},{1,9},{5... | collective-permute-start | bytes 663560 | tf_op jit(solution)/shard_map/ppermute | solution.py:559
  76.5 4.8 %collective-permute-start.33 = (bf16[2,72,384]{2,1,0:T(8,128)(2,1)S(1)}, bf16[2,72,384]{2,1,0:T(8,128)(2,1)S(1)}, u32[]{:S(2)}, u32[]{:S(2)}) collective-permute-start(bf16[2,72,384]{2,1,0:T(8,128)(2,1)S(1)} %slice.70), channel_id=1, source_target_pairs={{0,8},{4,12},{8,0},{12,4},{16,24},{20,28},{24,16},{28,20},{1,9},{5... | collective-permute-start | bytes 331784 | tf_op jit(solution)/shard_map/ppermute | solution.py:559
  81.3 8.6 %collective-permute-start.34 = (bf16[1,72,384]{2,1,0:T(8,128)(2,1)S(1)}, bf16[1,72,384]{2,1,0:T(8,128)(2,1)S(1)}, u32[]{:S(2)}, u32[]{:S(2)}) collective-permute-start(bf16[1,72,384]{2,1,0:T(8,128)(2,1)S(1)} %slice.72), channel_id=1, source_target_pairs={{0,16},{4,20},{8,24},{12,28},{16,0},{20,4},{24,8},{28,12},{1,17},{... | collective-permute-start | bytes 165896 | tf_op jit(solution)/shard_map/ppermute | solution.py:559
  88.0 6.6 %collective-permute-start.23 = (bf16[4,56,576]{2,1,0:T(8,128)(2,1)S(1)}, bf16[4,56,576]{2,1,0:T(8,128)(2,1)S(1)}, u32[]{:S(2)}, u32[]{:S(2)}) collective-permute-start(bf16[4,56,576]{2,1,0:T(8,128)(2,1)S(1)} %get-tuple-element.116), channel_id=1, source_target_pairs={{0,4},{4,0},{8,12},{12,8},{16,20},{20,16},{24,28},{28,24},{1,5},{5... | collective-permute-start | bytes 774152 | tf_op jit(solution)/shard_map/ppermute | solution.py:559
  89.5 6.6 %collective-permute-start.29 = (bf16[1,144,384]{2,1,0:T(8,128)(2,1)S(1)}, bf16[1,144,384]{2,1,0:T(8,128)(2,1)S(1)}, u32[]{:S(2)}, u32[]{:S(2)}) collective-permute-start(bf16[1,144,384]{2,1,0:T(8,128)(2,1)S(1)} %slice.68), channel_id=1, source_target_pairs={{0,16},{4,20},{8,24},{12,28},{16,0},{20,4},{24,8},{28,12},{1,17},{... | collective-permute-start | bytes 331784 | tf_op jit(solution)/shard_map/ppermute | solution.py:559
  89.9 9.4 %collective-permute-start.35 = (bf16[1,72,384]{2,1,0:T(8,128)(2,1)S(1)}, bf16[1,72,384]{2,1,0:T(8,128)(2,1)S(1)}, u32[]{:S(2)}, u32[]{:S(2)}) collective-permute-start(bf16[1,72,384]{2,1,0:T(8,128)(2,1)S(1)} %add_convert_fusion.8), channel_id=1, source_target_pairs={{0,16},{4,20},{8,24},{12,28},{16,0},{20,4},{24,8},{28,12},{1,17},{... | collective-permute-start | bytes 165896 | tf_op jit(solution)/shard_map/ppermute | solution.py:559
  94.7 7.3 %collective-permute-start.24 = (bf16[2,56,576]{2,1,0:T(8,128)(2,1)S(1)}, bf16[2,56,576]{2,1,0:T(8,128)(2,1)S(1)}, u32[]{:S(2)}, u32[]{:S(2)}) collective-permute-start(bf16[2,56,576]{2,1,0:T(8,128)(2,1)S(1)} %slice.64), channel_id=1, source_target_pairs={{0,8},{4,12},{8,0},{12,4},{16,24},{20,28},{24,16},{28,20},{1,9},{5... | collective-permute-start | bytes 387080 | tf_op jit(solution)/shard_map/ppermute | solution.py:559
  96.1 8.4 %collective-permute-start.30 = (bf16[1,144,384]{2,1,0:T(8,128)(2,1)S(1)}, bf16[1,144,384]{2,1,0:T(8,128)(2,1)S(1)}, u32[]{:S(2)}, u32[]{:S(2)}) collective-permute-start(bf16[1,144,384]{2,1,0:T(8,128)(2,1)S(1)} %add_convert_fusion.6), channel_id=1, source_target_pairs={{0,16},{4,20},{8,24},{12,28},{16,0},{20,4},{24,8},{28,12},{1,17},{... | collective-permute-start | bytes 331784 | tf_op jit(solution)/shard_map/ppermute | solution.py:559
  99.3 15.6 %collective-permute-start.36 = (bf16[2,72,384]{2,1,0:T(8,128)(2,1)S(1)}, bf16[2,72,384]{2,1,0:T(8,128)(2,1)S(1)}, u32[]{:S(2)}, u32[]{:S(2)}) collective-permute-start(bf16[2,72,384]{2,1,0:T(8,128)(2,1)S(1)} %pad_maximum_fusion.5), channel_id=1, source_target_pairs={{0,8},{4,12},{8,0},{12,4},{16,24},{20,28},{24,16},{28,20},{1,9},{5... | collective-permute-start | bytes 331784 | tf_op jit(solution)/shard_map/ppermute | solution.py:559
  102.1 7.4 %collective-permute-start.25 = (bf16[1,56,576]{2,1,0:T(8,128)(2,1)S(1)}, bf16[1,56,576]{2,1,0:T(8,128)(2,1)S(1)}, u32[]{:S(2)}, u32[]{:S(2)}) collective-permute-start(bf16[1,56,576]{2,1,0:T(8,128)(2,1)S(1)} %slice.66), channel_id=1, source_target_pairs={{0,16},{4,20},{8,24},{12,28},{16,0},{20,4},{24,8},{28,12},{1,17},{... | collective-permute-start | bytes 193544 | tf_op jit(solution)/shard_map/ppermute | solution.py:559
  104.6 7.3 %collective-permute-start.31 = (bf16[2,144,384]{2,1,0:T(8,128)(2,1)S(1)}, bf16[2,144,384]{2,1,0:T(8,128)(2,1)S(1)}, u32[]{:S(2)}, u32[]{:S(2)}) collective-permute-start(bf16[2,144,384]{2,1,0:T(8,128)(2,1)S(1)} %pad_maximum_fusion.2), channel_id=1, source_target_pairs={{0,8},{4,12},{8,0},{12,4},{16,24},{20,28},{24,16},{28,20},{1,9},{5... | collective-permute-start | bytes 663560 | tf_op jit(solution)/shard_map/ppermute | solution.py:559
  109.5 5.3 %collective-permute-start.26 = (bf16[1,56,576]{2,1,0:T(8,128)(2,1)S(1)}, bf16[1,56,576]{2,1,0:T(8,128)(2,1)S(1)}, u32[]{:S(2)}, u32[]{:S(2)}) collective-permute-start(bf16[1,56,576]{2,1,0:T(8,128)(2,1)S(1)} %add_convert_fusion.7), channel_id=1, source_target_pairs={{0,16},{4,20},{8,24},{12,28},{16,0},{20,4},{24,8},{28,12},{1,17},{... | collective-permute-start | bytes 193544 | tf_op jit(solution)/shard_map/ppermute | solution.py:559
  112.0 15.8 %collective-permute-start.32 = (bf16[4,144,384]{2,1,0:T(8,128)(2,1)S(1)}, bf16[4,144,384]{2,1,0:T(8,128)(2,1)S(1)}, u32[]{:S(2)}, u32[]{:S(2)}) collective-permute-start(bf16[4,144,384]{2,1,0:T(8,128)(2,1)S(1)} %pad_maximum_fusion.one_lo), channel_id=1, source_target_pairs={{0,4},{4,0},{8,12},{12,8},{16,20},{20,16},{24,28},{28,24},{1,5},{5... | collective-permute-start | bytes 1327112 | tf_op jit(solution)/shard_map/ppermute | solution.py:559
  114.8 5.2 %collective-permute-start.27 = (bf16[2,56,576]{2,1,0:T(8,128)(2,1)S(1)}, bf16[2,56,576]{2,1,0:T(8,128)(2,1)S(1)}, u32[]{:S(2)}, u32[]{:S(2)}) collective-permute-start(bf16[2,56,576]{2,1,0:T(8,128)(2,1)S(1)} %pad_maximum_fusion.4), channel_id=1, source_target_pairs={{0,8},{4,12},{8,0},{12,4},{16,24},{20,28},{24,16},{28,20},{1,9},{5... | collective-permute-start | bytes 387080 | tf_op jit(solution)/shard_map/ppermute | solution.py:559
  115.0 12.8 %collective-permute-start.37 = (bf16[4,72,384]{2,1,0:T(8,128)(2,1)S(1)}, bf16[4,72,384]{2,1,0:T(8,128)(2,1)S(1)}, u32[]{:S(2)}, u32[]{:S(2)}) collective-permute-start(bf16[4,72,384]{2,1,0:T(8,128)(2,1)S(1)} %pad_maximum_fusion.3.two_lo), channel_id=1, source_target_pairs={{0,4},{4,0},{8,12},{12,8},{16,20},{20,16},{24,28},{28,24},{1,5},{5... | collective-permute-start | bytes 663560 | tf_op jit(solution)/shard_map/ppermute | solution.py:559
  120.1 10.7 %collective-permute-start.28 = (bf16[4,56,576]{2,1,0:T(8,128)(2,1)S(1)}, bf16[4,56,576]{2,1,0:T(8,128)(2,1)S(1)}, u32[]{:S(2)}, u32[]{:S(2)}) collective-permute-start(bf16[4,56,576]{2,1,0:T(8,128)(2,1)S(1)} %pad_maximum_fusion.1.first), channel_id=1, source_target_pairs={{0,4},{4,0},{8,12},{12,8},{16,20},{20,16},{24,28},{28,24},{1,5},{5... | collective-permute-start | bytes 774152 | tf_op jit(solution)/shard_map/ppermute | solution.py:559
  (11 other events, 101.6 us)

commit v5 on v4

--- a/solution.py
+++ b/solution.py
@@ -498,7 +498,7 @@
         place(second[at - middle].astype(F32))
 
 
-def unpack_mlp_kernel(n_rep, n_shard, idx, one_lo, one_hi, two_lo, two_hi, down_ref, gu_ref):
+def unpack_mlp_kernel(n_rep, n_shard, idx, one_lo, one_hi, two_lo, two_hi, gu_ref):
     shard = idx[0]
     member = idx[1]
     rows, chunk = two_lo.shape[1:]
@@ -513,14 +513,23 @@
 
     def place_one(slab, piece):
         place_gateup(slab, 0, piece[:rows])
-        down_ref[slab * rows : (slab + 1) * rows, :] = piece[rows:]
 
     for slab in range(n_rep):
         fetch(one_lo, one_hi, member ^ slab, masks(n_rep, TURNED[0]), functools.partial(place_one, slab))
         fetch(two_lo, two_hi, member ^ slab, masks(n_rep, TURNED[1]), functools.partial(place_gateup, slab, 1))
 
 
-def unpack_attn_kernel(n_rep, idx, first, second, q_ref, kv_ref, o_ref, gain_ref, a_all):
+def unpack_down_kernel(n_rep, idx, first, second, down_ref):
+    rows = first.shape[1] // 2
+
+    def place(slab, piece):
+        down_ref[slab * rows : (slab + 1) * rows, :] = piece[rows:]
+
+    for slab in range(n_rep):
+        fetch(first, second, idx[1] ^ slab, masks(n_rep, TURNED[0]), functools.partial(place, slab))
+
+
+def unpack_attn_kernel(n_rep, idx, first, second, q_ref, kv_ref, o_ref, gain_attn_ref, gain_mlp_ref, a_all):
     rows = first.shape[1]
 
     def place(slab, piece):
@@ -533,7 +542,9 @@
     o_ref[...] = a_all[width : 2 * width, :]
     kv_ref[...] = a_all[2 * width : 3 * width, : kv_ref.shape[1]]
     rows = a_all[3 * width :, :].astype(BF16)
-    gain_ref[...] = mm(rows, own_columns(idx[0], rows.shape[1], width))
+    own = mm(rows, own_columns(idx[0], rows.shape[1], width))
+    gain_attn_ref[...] = own[0:1]
+    gain_mlp_ref[...] = own[1:2]
 
 
 def call(body, operands, outs, scratch=(), micros=1, vmem=24, raw=()):
@@ -769,20 +780,27 @@
     )
     one, two = last_of(one), last_of(two)
     attn = last_of(replica_steps(a_lo, a_hi, n_rep, TURNED[2]))
-    grad_down, grad_gateup = call(
+    grad_down = call(
+        functools.partial(unpack_down_kernel, n_rep),
+        [idx] + list(one),
+        shape((model, chunk), F32),
+        micros=1,
+    )
+    grad_gateup = call(
         functools.partial(unpack_mlp_kernel, n_rep, n_shard),
         [idx] + list(one) + list(two),
-        (shape((model, chunk), F32), shape((width, 2 * ff), F32)),
-        micros=3,
-    )
-    grad_query, grad_keyval, grad_out, own_gains = call(
+        shape((width, 2 * ff), F32),
+        micros=2,
+    )
+    grad_query, grad_keyval, grad_out, own_gain_attn, own_gain_mlp = call(
         functools.partial(unpack_attn_kernel, n_rep),
         [idx] + list(attn),
         (
             shape((width, model), F32),
             shape((width, kv_width), F32),
             shape((width, model), F32),
-            shape((a_rows - 3 * width, width), F32),
+            shape((1, width), F32),
+            shape((1, width), F32),
         ),
         [pltpu.VMEM((a_rows, model), F32)],
         micros=2,
@@ -795,8 +813,8 @@
         grad_out[None],
         grad_gateup[None],
         grad_down.T[None],
-        own_gains[:1],
-        own_gains[1:2],
+        own_gain_attn,
+        own_gain_mlp,
     )
 
 

time: 133 us -> 130 us (0.977)
  waiting for transfers between devices: 52.9 us -> 46.9 us
  starting transfers between devices: 31.1 us -> 32.6 us
    ppermute x38, waiting for transfers between devices: 52.9 us -> 46.9 us  [exchange(): lax.ppermute(value, axis, [(member, member ^ mask) for member in range(to...]
    ppermute x38, starting transfers between devices: 31.1 us -> 32.6 us  [exchange(): lax.ppermute(value, axis, [(member, member ^ mask) for member in range(to...]
    pallas_call x10 -> x11, Pallas kernels: 44.5 us -> 45.8 us  [call(): pl.pallas_call(body, out_shape=outs, in_specs=[pl.BlockSpec(memory_space=...]
  transfers between devices with their start and end apart: 38 -> 38, of which waited for: 21 -> 19; matrix products, arithmetic and copies ran while one was open for 1% -> 1% of each run, Pallas kernels for 24% -> 25%
where the time goes in v5:
time: 130 us; the launch traced here: 129 us
  waiting for transfers between devices  46.9 us (36%)
  Pallas kernels  45.8 us (35%)
  starting transfers between devices  32.6 us (25%)
  between operations  1.55 us (1%)
    ppermute x38, waiting for transfers between devices, exchange(): lax.ppermute(value, axis, [(member, member ^ mask) for member in range(to...  46.9 us
    pallas_call x11, Pallas kernels, call(): pl.pallas_call(body, out_shape=outs, in_specs=[pl.BlockSpec(memory_space=...  45.8 us
    ppermute x38, starting transfers between devices, exchange(): lax.ppermute(value, axis, [(member, member ^ mask) for member in range(to...  32.6 us
  transfers between devices with their start and end apart: 38, of which 19 were waited for; matrix products, arithmetic and copies ran while one was open for 1% of the time, Pallas kernels for 25%

profile of v5, /device:TPU:0, one launch (start us, length us, event | category | flops | bytes accessed | tf_op | source)
XLA Modules:
  0.0 129.3 jit_solution(8678710644984854880)
XLA Ops:
  1.9 3.4 %shard_map.178 = (bf16[528,576]{1,0:T(8,128)(2,1)}, bf16[336,576]{1,0:T(8,128)(2,1)}, bf16[144,768]{1,0:T(8,128)(2,1)}, bf16[144,768]{1,0:T(8,128)(2,1)}, bf16[128,576]{1,0:T(8,128)(2,1)}) custom-call(s32[3]{0:T(128)} %pad_add_fusion.idx, bf16[144,576]{1,0:T(8,128)(2,1)} %bitcast.27, bf16[144,384]{1,0:T(8,128)(2,1)} %bitcast.31, bf16[144,576]{1,0:T(8,128)(2,1)} %bitcast.28, ...), custom_call_target="tpu_custom_call" | custom-call | flops 1000000000 | bytes 1048576 | tf_op jit(solution)/shard_map/pallas_call | solution.py:554
  5.3 3.0 %collective-permute-start.3 = (bf16[336,576]{1,0:T(8,128)(2,1)}, bf16[336,576]{1,0:T(8,128)(2,1)S(1)}, u32[]{:S(2)}, u32[]{:S(2)}) collective-permute-start(bf16[336,576]{1,0:T(8,128)(2,1)} %get-tuple-element.69), channel_id=1, source_target_pairs={{0,2},{1,3},{2,0},{3,1},{4,6},{5,7},{6,4},{7,5},{8,10},{9,11},{10,... | collective-permute-start | bytes 1161224 | tf_op jit(solution)/shard_map/ppermute | solution.py:570
  8.5 1.9 %collective-permute-start.1 = (bf16[144,768]{1,0:T(8,128)(2,1)}, bf16[144,768]{1,0:T(8,128)(2,1)S(1)}, u32[]{:S(2)}, u32[]{:S(2)}) collective-permute-start(bf16[144,768]{1,0:T(8,128)(2,1)} %get-tuple-element.66), channel_id=1, source_target_pairs={{0,2},{1,3},{2,0},{3,1},{4,6},{5,7},{6,4},{7,5},{8,10},{9,11},{10,... | collective-permute-start | bytes 663560 | tf_op jit(solution)/shard_map/ppermute | solution.py:570
  10.4 8.9 %collective-permute-done.3.refs_2_ = bf16[336,576]{1,0:T(8,128)(2,1)S(1)} collective-permute-done((bf16[336,576]{1,0:T(8,128)(2,1)}, bf16[336,576]{1,0:T(8,128)(2,1)S(1)}, u32[]{:S(2)}, u32[]{:S(2)}) %collective-permute-start.3) | collective-permute-done | bytes 387104 | tf_op jit(solution)/shard_map/ppermute | solution.py:570
  19.3 2.2 %collective-permute-start.4 = (bf16[192,576]{1,0:T(8,128)(2,1)S(1)}, bf16[192,576]{1,0:T(8,128)(2,1)S(1)}, u32[]{:S(2)}, u32[]{:S(2)}) collective-permute-start(bf16[192,576]{1,0:T(8,128)(2,1)S(1)} %slice.52), channel_id=1, source_target_pairs={{0,4},{4,0},{8,12},{12,8},{16,20},{20,16},{24,28},{28,24},{1,5},{5... | collective-permute-start | bytes 663560 | tf_op jit(solution)/shard_map/ppermute | solution.py:570
  21.5 2.6 %collective-permute-done.refs_10_ = bf16[144,768]{1,0:T(8,128)(2,1)S(1)} collective-permute-done((bf16[144,768]{1,0:T(8,128)(2,1)}, bf16[144,768]{1,0:T(8,128)(2,1)S(1)}, u32[]{:S(2)}, u32[]{:S(2)}) %collective-permute-start) | collective-permute-done | bytes 221216 | tf_op jit(solution)/shard_map/ppermute | solution.py:570
  24.0 3.9 %collective-permute-done.1.refs_11_ = bf16[144,768]{1,0:T(8,128)(2,1)S(1)} collective-permute-done((bf16[144,768]{1,0:T(8,128)(2,1)}, bf16[144,768]{1,0:T(8,128)(2,1)S(1)}, u32[]{:S(2)}, u32[]{:S(2)}) %collective-permute-start.1) | collective-permute-done | bytes 221216 | tf_op jit(solution)/shard_map/ppermute | solution.py:570
  27.9 1.7 %collective-permute-start.8 = (bf16[576,384]{1,0:T(8,128)(2,1)S(1)}, bf16[576,384]{1,0:T(8,128)(2,1)S(1)}, u32[]{:S(2)}, u32[]{:S(2)}) collective-permute-start(bf16[576,384]{1,0:T(8,128)(2,1)S(1)} %bitcast.24), channel_id=1, source_target_pairs={{0,2},{1,3},{2,0},{3,1},{4,6},{5,7},{6,4},{7,5},{8,10},{9,11},{10,... | collective-permute-start | bytes 1327112 | tf_op jit(solution)/shard_map/ppermute | solution.py:570
  29.7 1.6 %collective-permute-start.9 = (bf16[144,768]{1,0:T(8,128)(2,1)S(1)}, bf16[144,768]{1,0:T(8,128)(2,1)S(1)}, u32[]{:S(2)}, u32[]{:S(2)}) collective-permute-start(bf16[144,768]{1,0:T(8,128)(2,1)S(1)} %collective-permute-done.refs_10_), channel_id=1, source_target_pairs={{0,4},{4,0},{8,12},{12,8},{16,20},{20,16},{24,28},{28,24},{1,5},{5... | collective-permute-start | bytes 663560 | tf_op jit(solution)/shard_map/ppermute | solution.py:570
  33.2 8.6 %shard_map.179 = (bf16[512,576]{1,0:T(8,128)(2,1)S(1)}, bf16[512,576]{1,0:T(8,128)(2,1)S(1)}, bf16[512,640]{1,0:T(8,128)(2,1)S(1)}, bf16[512,384]{1,0:T(8,128)(2...) custom-call(s32[3]{0:T(128)S(1)} %copy-done, ...), custom_call_target="tpu_custom_call" | custom-call | flops 1000000000 | bytes 1048576 | tf_op jit(solution)/shard_map/pallas_call | solution.py:554
  46.9 7.7 %shard_map.180 = (f32[128,576]{1,0:T(8,128)S(1)}, f32[512,576]{1,0:T(8,128)S(1)}, bf16[4,144,384]{2,1,0:T(8,128)(2,1)S(1)}, bf16[4,144,384]{2,1,0:T(8,128)(2,1)S...) custom-call(s32[3]{0:T(128)S(1)} %copy-done, ...), custom_call_target="tpu_custom_call" | custom-call | flops 6000000000 | bytes 1048576 | tf_op jit(solution)/shard_map/pallas_call | solution.py:554
  56.5 6.0 %shard_map.181 = (f32[576,128]{1,0:T(8,128)}, f32[512,576]{1,0:T(8,128)S(1)}, bf16[4,72,384]{2,1,0:T(8,128)(2,1)S(1)}, bf16[4,72,384]{2,1,0:T(8,128)(2,1)S(1)}) custom-call(s32[3]{0:T(128)S(1)} %copy-done, bf16[512,576]{1,0:T(8,128)(2,1)S(1)} %get-tuple-element.70.refs_0_, f32[128,576]{1,0:T(8,128)S(1)} %get-tuple-element.79.refs_1_, ...), custom_call_target="tpu_custom_call" | custom-call | flops 6000000000 | bytes 1048576 | tf_op jit(solution)/shard_map/pallas_call | solution.py:554
  64.0 4.0 %collective-permute-done.20 = bf16[4,144,384]{2,1,0:T(8,128)(2,1)S(1)} collective-permute-done((bf16[4,144,384]{2,1,0:T(8,128)(2,1)S(1)}, bf16[4,144,384]{2,1,0:T(8,128)(2,1)S(1)}, u32[]{:S(2)}, u32[]{:S(2)}) %collective-permute-start.20) | collective-permute-done | bytes 442400 | tf_op jit(solution)/shard_map/ppermute | solution.py:570
  68.1 2.9 %shard_map.182 = (bf16[512,576]{1,0:T(8,128)(2,1)}, bf16[512,640]{1,0:T(8,128)(2,1)S(1)}, f32[128,576]{1,0:T(8,128)S(1)}, f32[144,576]{1,0:T(8,128)S(1)}, f32[8,576]{1,0:T(8,128)S(1)}) custom-call(s32[3]{0:T(128)S(1)} %copy-done, f32[512,576]{1,0:T(8,128)S(1)} %get-tuple-element.71.refs_1_.mid_ref, f32[512,576]{1,0:T(8,128)S(1)} %get-tuple-element.91.dn_ref, ...), custom_call_target="tpu_custom_call" | custom-call | flops 3000000000 | bytes 1048576 | tf_op jit(solution)/shard_map/pallas_call | solution.py:554
  72.5 3.9 %shard_map.183 = (bf16[256,640]{1,0:T(8,128)(2,1)S(1)}, bf16[256,384]{1,0:T(8,128)(2,1)S(1)}) custom-call(s32[3]{0:T(128)S(1)} %copy-done, bf16[512,640]{1,0:T(8,128)(2,1)S(1)} %get-tuple-element.102.q_ref, bf16[512,384]{1,0:T(8,128)(2,1)S(1)} %get-tuple-element.103.kv_ref, bf16[512,640]{1,0:T(8,128)(2,1)S(1)} %get-tuple-element.109.dmix_ref, ...), custom_call_target="tpu_custom_call" | custom-call | flops 4000000000 | bytes 1048576 | tf_op jit(solution)/shard_map/pallas_call | solution.py:554
  77.2 2.6 %collective-permute-start.29 = (bf16[1,144,384]{2,1,0:T(8,128)(2,1)S(1)}, bf16[1,144,384]{2,1,0:T(8,128)(2,1)S(1)}, u32[]{:S(2)}, u32[]{:S(2)}) collective-permute-start(bf16[1,144,384]{2,1,0:T(8,128)(2,1)S(1)} %slice.60), channel_id=1, source_target_pairs={{0,16},{4,20},{8,24},{12,28},{16,0},{20,4},{24,8},{28,12},{1,17},{... | collective-permute-start | bytes 331784 | tf_op jit(solution)/shard_map/ppermute | solution.py:570
  79.7 3.9 %shard_map.184 = (bf16[256,640]{1,0:T(8,128)(2,1)S(1)}, bf16[256,384]{1,0:T(8,128)(2,1)S(1)}) custom-call(s32[3]{0:T(128)S(1)} %copy-done, bf16[512,640]{1,0:T(8,128)(2,1)S(1)} %get-tuple-element.102.q_ref, bf16[512,384]{1,0:T(8,128)(2,1)S(1)} %get-tuple-element.103.kv_ref, bf16[512,640]{1,0:T(8,128)(2,1)S(1)} %get-tuple-element.109.dmix_ref, ...), custom_call_target="tpu_custom_call" | custom-call | flops 4000000000 | bytes 1048576 | tf_op jit(solution)/shard_map/pallas_call | solution.py:554
  83.6 4.0 %shard_map.185 = (f32[576,128]{1,0:T(8,128)}, bf16[4,56,576]{2,1,0:T(8,128)(2,1)S(1)}, bf16[4,56,576]{2,1,0:T(8,128)(2,1)S(1)}) custom-call(s32[3]{0:T(128)S(1)} %copy-done, bf16[512,576]{1,0:T(8,128)(2,1)S(1)} %get-tuple-element.87.x_ref, bf16[512,576]{1,0:T(8,128)(2,1)S(1)} %get-tuple-element.88.nrm_ref, f32[16,576]{1,0:T(8,128)S(1)} %get-tuple-element.73.gain_ref, ...), custom_call_target="tpu_custom_call" | custom-call | flops 4000000000 | bytes 1048576 | tf_op jit(solution)/shard_map/pallas_call | solution.py:554
  89.7 2.7 %collective-permute-start.30 = (bf16[1,144,384]{2,1,0:T(8,128)(2,1)S(1)}, bf16[1,144,384]{2,1,0:T(8,128)(2,1)S(1)}, u32[]{:S(2)}, u32[]{:S(2)}) collective-permute-start(bf16[1,144,384]{2,1,0:T(8,128)(2,1)S(1)} %add_convert_fusion.6), channel_id=1, source_target_pairs={{0,16},{4,20},{8,24},{12,28},{16,0},{20,4},{24,8},{28,12},{1,17},{... | collective-permute-start | bytes 331784 | tf_op jit(solution)/shard_map/ppermute | solution.py:570
  92.3 2.0 %collective-permute-done.23 = bf16[4,56,576]{2,1,0:T(8,128)(2,1)S(1)} collective-permute-done((bf16[4,56,576]{2,1,0:T(8,128)(2,1)S(1)}, bf16[4,56,576]{2,1,0:T(8,128)(2,1)S(1)}, u32[]{:S(2)}, u32[]{:S(2)}) %collective-permute-start.23) | collective-permute-done | bytes 258080 | tf_op jit(solution)/shard_map/ppermute | solution.py:570
  94.4 2.1 %collective-permute-start.24 = (bf16[2,56,576]{2,1,0:T(8,128)(2,1)S(1)}, bf16[2,56,576]{2,1,0:T(8,128)(2,1)S(1)}, u32[]{:S(2)}, u32[]{:S(2)}) collective-permute-start(bf16[2,56,576]{2,1,0:T(8,128)(2,1)S(1)} %slice.56), channel_id=1, source_target_pairs={{0,8},{4,12},{8,0},{12,4},{16,24},{20,28},{24,16},{28,20},{1,9},{5... | collective-permute-start | bytes 387080 | tf_op jit(solution)/shard_map/ppermute | solution.py:570
  96.8 1.8 %collective-permute-done.30 = bf16[1,144,384]{2,1,0:T(8,128)(2,1)S(1)} collective-permute-done((bf16[1,144,384]{2,1,0:T(8,128)(2,1)S(1)}, bf16[1,144,384]{2,1,0:T(8,128)(2,1)S(1)}, u32[]{:S(2)}, u32[]{:S(2)}) %collective-permute-start.30) | collective-permute-done | bytes 110624 | tf_op jit(solution)/shard_map/ppermute | solution.py:570
  98.7 4.5 %collective-permute-done.24 = bf16[2,56,576]{2,1,0:T(8,128)(2,1)S(1)} collective-permute-done((bf16[2,56,576]{2,1,0:T(8,128)(2,1)S(1)}, bf16[2,56,576]{2,1,0:T(8,128)(2,1)S(1)}, u32[]{:S(2)}, u32[]{:S(2)}) %collective-permute-start.24) | collective-permute-done | bytes 129056 | tf_op jit(solution)/shard_map/ppermute | solution.py:570
  103.3 2.3 %collective-permute-done.31 = bf16[2,144,384]{2,1,0:T(8,128)(2,1)S(1)} collective-permute-done((bf16[2,144,384]{2,1,0:T(8,128)(2,1)S(1)}, bf16[2,144,384]{2,1,0:T(8,128)(2,1)S(1)}, u32[]{:S(2)}, u32[]{:S(2)}) %collective-permute-start.31) | collective-permute-done | bytes 221216 | tf_op jit(solution)/shard_map/ppermute | solution.py:570
  106.1 4.0 %collective-permute-done.25 = bf16[1,56,576]{2,1,0:T(8,128)(2,1)S(1)} collective-permute-done((bf16[1,56,576]{2,1,0:T(8,128)(2,1)S(1)}, bf16[1,56,576]{2,1,0:T(8,128)(2,1)S(1)}, u32[]{:S(2)}, u32[]{:S(2)}) %collective-permute-start.25) | collective-permute-done | bytes 64544 | tf_op jit(solution)/shard_map/ppermute | solution.py:570
  110.3 1.6 %collective-permute-start.36 = (bf16[2,72,384]{2,1,0:T(8,128)(2,1)S(1)}, bf16[2,72,384]{2,1,0:T(8,128)(2,1)S(1)}, u32[]{:S(2)}, u32[]{:S(2)}) collective-permute-start(bf16[2,72,384]{2,1,0:T(8,128)(2,1)S(1)} %pad_maximum_fusion.5), channel_id=1, source_target_pairs={{0,8},{4,12},{8,0},{12,4},{16,24},{20,28},{24,16},{28,20},{1,9},{5... | collective-permute-start | bytes 331784 | tf_op jit(solution)/shard_map/ppermute | solution.py:570
  111.9 3.7 %collective-permute-done.26 = bf16[1,56,576]{2,1,0:T(8,128)(2,1)S(1)} collective-permute-done((bf16[1,56,576]{2,1,0:T(8,128)(2,1)S(1)}, bf16[1,56,576]{2,1,0:T(8,128)(2,1)S(1)}, u32[]{:S(2)}, u32[]{:S(2)}) %collective-permute-start.26) | collective-permute-done | bytes 64544 | tf_op jit(solution)/shard_map/ppermute | solution.py:570
  117.5 3.3 %collective-permute-done.27 = bf16[2,56,576]{2,1,0:T(8,128)(2,1)S(1)} collective-permute-done((bf16[2,56,576]{2,1,0:T(8,128)(2,1)S(1)}, bf16[2,56,576]{2,1,0:T(8,128)(2,1)S(1)}, u32[]{:S(2)}, u32[]{:S(2)}) %collective-permute-start.27) | collective-permute-done | bytes 129056 | tf_op jit(solution)/shard_map/ppermute | solution.py:570
  121.8 1.7 %shard_map.188 = f32[576,384]{1,0:T(8,128)} custom-call(s32[3]{0:T(128)S(1)} %copy-done, bf16[4,144,384]{2,1,0:T(8,128)(2,1)S(1)} %pad_maximum_fusion.one_lo.first, bf16[4,144,384]{2,1,0:T(8,128)(2,1)S(1)} %collective-permute-done.32.one_hi.second), custom_call_target="tpu_custom_call" | custom-call | flops 1000000000 | bytes 1048576 | tf_op jit(solution)/shard_map/pallas_call | solution.py:554
  123.4 2.1 %shard_map.187 = f32[144,3072]{1,0:T(8,128)} custom-call(s32[3]{0:T(128)S(1)} %copy-done, bf16[4,144,384]{2,1,0:T(8,128)(2,1)S(1)} %pad_maximum_fusion.one_lo.first, bf16[4,144,384]{2,1,0:T(8,128)(2,1)S(1)} %collective-permute-done.32.one_hi.second, bf16[4,72,384]{2,1,0:T(8,128)(2,1)S(1)} %pad_maximum_fusion.3.two_lo, ...), custom_call_target="tpu_custom_call" | custom-call | flops 2000000000 | bytes 1048576 | tf_op jit(solution)/shard_map/pallas_call | solution.py:554
  125.5 2.1 %collective-permute-done.28.second = bf16[4,56,576]{2,1,0:T(8,128)(2,1)S(1)} collective-permute-done((bf16[4,56,576]{2,1,0:T(8,128)(2,1)S(1)}, bf16[4,56,576]{2,1,0:T(8,128)(2,1)S(1)}, u32[]{:S(2)}, u32[]{:S(2)}) %collective-permute-start.28) | collective-permute-done | bytes 258080 | tf_op jit(solution)/shard_map/ppermute | solution.py:570
  127.6 1.7 %shard_map.186 = (f32[144,576]{1,0:T(8,128)}, f32[144,384]{1,0:T(8,128)}, f32[144,576]{1,0:T(8,128)}, f32[1,144]{1,0:T(1,128)}, f32[1,144]{1,0:T(1,128)}) custom-call(s32[3]{0:T(128)S(1)} %copy-done, bf16[4,56,576]{2,1,0:T(8,128)(2,1)S(1)} %pad_maximum_fusion.1.first, bf16[4,56,576]{2,1,0:T(8,128)(2,1)S(1)} %collective-permute-done.28.second), custom_call_target="tpu_custom_call" | custom-call | flops 2000000000 | bytes 1048576 | tf_op jit(solution)/shard_map/pallas_call | solution.py:554
  (88 shorter events, 19.7 us)
Async XLA Ops:
  5.3 13.9 %collective-permute-start.3 = (bf16[336,576]{1,0:T(8,128)(2,1)}, bf16[336,576]{1,0:T(8,128)(2,1)S(1)}, u32[]{:S(2)}, u32[]{:S(2)}) collective-permute-start(bf16[336,576]{1,0:T(8,128)(2,1)} %get-tuple-element.69), channel_id=1, source_target_pairs={{0,2},{1,3},{2,0},{3,1},{4,6},{5,7},{6,4},{7,5},{8,10},{9,11},{10,... | collective-permute-start | bytes 1161224 | tf_op jit(solution)/shard_map/ppermute | solution.py:570
  8.3 21.3 %collective-permute-start.2 = (bf16[528,576]{1,0:T(8,128)(2,1)}, bf16[528,576]{1,0:T(8,128)(2,1)S(1)}, u32[]{:S(2)}, u32[]{:S(2)}) collective-permute-start(bf16[528,576]{1,0:T(8,128)(2,1)} %get-tuple-element.68.refs_0_), channel_id=1, source_target_pairs={{0,1},{1,0},{2,3},{3,2},{4,5},{5,4},{6,7},{7,6},{8,9},{9,8},{10,11... | collective-permute-start | bytes 1824776 | tf_op jit(solution)/shard_map/ppermute | solution.py:570
  8.3 15.7 %collective-permute-start = (bf16[144,768]{1,0:T(8,128)(2,1)}, bf16[144,768]{1,0:T(8,128)(2,1)S(1)}, u32[]{:S(2)}, u32[]{:S(2)}) collective-permute-start(bf16[144,768]{1,0:T(8,128)(2,1)} %get-tuple-element.65), channel_id=1, source_target_pairs={{0,2},{1,3},{2,0},{3,1},{4,6},{5,7},{6,4},{7,5},{8,10},{9,11},{10,... | collective-permute-start | bytes 663560 | tf_op jit(solution)/shard_map/ppermute | solution.py:570
  8.5 19.4 %collective-permute-start.1 = (bf16[144,768]{1,0:T(8,128)(2,1)}, bf16[144,768]{1,0:T(8,128)(2,1)S(1)}, u32[]{:S(2)}, u32[]{:S(2)}) collective-permute-start(bf16[144,768]{1,0:T(8,128)(2,1)} %get-tuple-element.66), channel_id=1, source_target_pairs={{0,2},{1,3},{2,0},{3,1},{4,6},{5,7},{6,4},{7,5},{8,10},{9,11},{10,... | collective-permute-start | bytes 663560 | tf_op jit(solution)/shard_map/ppermute | solution.py:570
  19.3 12.0 %collective-permute-start.5 = (bf16[336,576]{1,0:T(8,128)(2,1)S(1)}, bf16[336,576]{1,0:T(8,128)(2,1)S(1)}, u32[]{:S(2)}, u32[]{:S(2)}) collective-permute-start(bf16[336,576]{1,0:T(8,128)(2,1)S(1)} %collective-permute-done.3.refs_2_), channel_id=1, source_target_pairs={{0,1},{1,0},{2,3},{3,2},{4,5},{5,4},{6,7},{7,6},{8,9},{9,8},{10,11... | collective-permute-start | bytes 1161224 | tf_op jit(solution)/shard_map/ppermute | solution.py:570
  19.3 10.4 %collective-permute-start.4 = (bf16[192,576]{1,0:T(8,128)(2,1)S(1)}, bf16[192,576]{1,0:T(8,128)(2,1)S(1)}, u32[]{:S(2)}, u32[]{:S(2)}) collective-permute-start(bf16[192,576]{1,0:T(8,128)(2,1)S(1)} %slice.52), channel_id=1, source_target_pairs={{0,4},{4,0},{8,12},{12,8},{16,20},{20,16},{24,28},{28,24},{1,5},{5... | collective-permute-start | bytes 663560 | tf_op jit(solution)/shard_map/ppermute | solution.py:570
  24.0 21.5 %collective-permute-start.14 = (bf16[144,3072]{1,0:T(8,128)(2,1)S(1)}, bf16[144,3072]{1,0:T(8,128)(2,1)S(1)}, u32[]{:S(2)}, u32[]{:S(2)}) collective-permute-start(bf16[144,3072]{1,0:T(8,128)(2,1)S(1)} %bitcast.22), channel_id=1, source_target_pairs={{0,1},{1,0},{2,3},{3,2},{4,5},{5,4},{6,7},{7,6},{8,9},{9,8},{10,11... | collective-permute-start | bytes 2654216 | tf_op jit(solution)/shard_map/ppermute | solution.py:570
  27.9 14.9 %collective-permute-start.8 = (bf16[576,384]{1,0:T(8,128)(2,1)S(1)}, bf16[576,384]{1,0:T(8,128)(2,1)S(1)}, u32[]{:S(2)}, u32[]{:S(2)}) collective-permute-start(bf16[576,384]{1,0:T(8,128)(2,1)S(1)} %bitcast.24), channel_id=1, source_target_pairs={{0,2},{1,3},{2,0},{3,1},{4,6},{5,7},{6,4},{7,5},{8,10},{9,11},{10,... | collective-permute-start | bytes 1327112 | tf_op jit(solution)/shard_map/ppermute | solution.py:570
  29.7 13.1 %collective-permute-start.9 = (bf16[144,768]{1,0:T(8,128)(2,1)S(1)}, bf16[144,768]{1,0:T(8,128)(2,1)S(1)}, u32[]{:S(2)}, u32[]{:S(2)}) collective-permute-start(bf16[144,768]{1,0:T(8,128)(2,1)S(1)} %collective-permute-done.refs_10_), channel_id=1, source_target_pairs={{0,4},{4,0},{8,12},{12,8},{16,20},{20,16},{24,28},{28,24},{1,5},{5... | collective-permute-start | bytes 663560 | tf_op jit(solution)/shard_map/ppermute | solution.py:570
  31.3 11.5 %collective-permute-start.10 = (bf16[144,768]{1,0:T(8,128)(2,1)S(1)}, bf16[144,768]{1,0:T(8,128)(2,1)S(1)}, u32[]{:S(2)}, u32[]{:S(2)}) collective-permute-start(bf16[144,768]{1,0:T(8,128)(2,1)S(1)} %collective-permute-done.1.refs_11_), channel_id=1, source_target_pairs={{0,4},{4,0},{8,12},{12,8},{16,20},{20,16},{24,28},{28,24},{1,5},{5... | collective-permute-start | bytes 663560 | tf_op jit(solution)/shard_map/ppermute | solution.py:570
  31.8 11.0 %collective-permute-start.7 = (bf16[128,576]{1,0:T(8,128)(2,1)}, bf16[128,576]{1,0:T(8,128)(2,1)S(1)}, u32[]{:S(2)}, u32[]{:S(2)}) collective-permute-start(bf16[128,576]{1,0:T(8,128)(2,1)} %get-tuple-element.75.refs_4_), channel_id=1, source_target_pairs={{0,2},{1,3},{2,0},{3,1},{4,6},{5,7},{6,4},{7,5},{8,10},{9,11},{10,... | collective-permute-start | bytes 442376 | tf_op jit(solution)/shard_map/ppermute | solution.py:570
  42.8 4.1 %collective-permute-start.11 = (bf16[576,384]{1,0:T(8,128)(2,1)S(1)}, bf16[576,384]{1,0:T(8,128)(2,1)S(1)}, u32[]{:S(2)}, u32[]{:S(2)}) collective-permute-start(bf16[576,384]{1,0:T(8,128)(2,1)S(1)} %bitcast.25), channel_id=1, source_target_pairs={{0,1},{1,0},{2,3},{3,2},{4,5},{5,4},{6,7},{7,6},{8,9},{9,8},{10,11... | collective-permute-start | bytes 1327112 | tf_op jit(solution)/shard_map/ppermute | solution.py:570
  43.5 3.4 %collective-permute-start.17 = (bf16[144,768]{1,0:T(8,128)(2,1)S(1)}, bf16[144,768]{1,0:T(8,128)(2,1)S(1)}, u32[]{:S(2)}, u32[]{:S(2)}) collective-permute-start(bf16[144,768]{1,0:T(8,128)(2,1)S(1)} %collective-permute-done.9.refs_12_), channel_id=1, source_target_pairs={{0,1},{1,0},{2,3},{3,2},{4,5},{5,4},{6,7},{7,6},{8,9},{9,8},{10,11... | collective-permute-start | bytes 663560 | tf_op jit(solution)/shard_map/ppermute | solution.py:570
  44.3 2.6 %collective-permute-start.18 = (bf16[144,768]{1,0:T(8,128)(2,1)S(1)}, bf16[144,768]{1,0:T(8,128)(2,1)S(1)}, u32[]{:S(2)}, u32[]{:S(2)}) collective-permute-start(bf16[144,768]{1,0:T(8,128)(2,1)S(1)} %collective-permute-done.10.refs_13_), channel_id=1, source_target_pairs={{0,1},{1,0},{2,3},{3,2},{4,5},{5,4},{6,7},{7,6},{8,9},{9,8},{10,11... | collective-permute-start | bytes 663560 | tf_op jit(solution)/shard_map/ppermute | solution.py:570
  54.9 13.0 %collective-permute-start.20 = (bf16[4,144,384]{2,1,0:T(8,128)(2,1)S(1)}, bf16[4,144,384]{2,1,0:T(8,128)(2,1)S(1)}, u32[]{:S(2)}, u32[]{:S(2)}) collective-permute-start(bf16[4,144,384]{2,1,0:T(8,128)(2,1)S(1)} %get-tuple-element.96), channel_id=1, source_target_pairs={{0,4},{4,0},{8,12},{12,8},{16,20},{20,16},{24,28},{28,24},{1,5},{5... | collective-permute-start | bytes 1327112 | tf_op jit(solution)/shard_map/ppermute | solution.py:570
  62.5 13.9 %collective-permute-start.22 = (bf16[4,72,384]{2,1,0:T(8,128)(2,1)S(1)}, bf16[4,72,384]{2,1,0:T(8,128)(2,1)S(1)}, u32[]{:S(2)}, u32[]{:S(2)}) collective-permute-start(bf16[4,72,384]{2,1,0:T(8,128)(2,1)S(1)} %get-tuple-element.98), channel_id=1, source_target_pairs={{0,4},{4,0},{8,12},{12,8},{16,20},{20,16},{24,28},{28,24},{1,5},{5... | collective-permute-start | bytes 663560 | tf_op jit(solution)/shard_map/ppermute | solution.py:570
  71.0 6.1 %collective-permute-start.21 = (bf16[2,144,384]{2,1,0:T(8,128)(2,1)S(1)}, bf16[2,144,384]{2,1,0:T(8,128)(2,1)S(1)}, u32[]{:S(2)}, u32[]{:S(2)}) collective-permute-start(bf16[2,144,384]{2,1,0:T(8,128)(2,1)S(1)} %slice.54), channel_id=1, source_target_pairs={{0,8},{4,12},{8,0},{12,4},{16,24},{20,28},{24,16},{28,20},{1,9},{5... | collective-permute-start | bytes 663560 | tf_op jit(solution)/shard_map/ppermute | solution.py:570
  76.5 12.7 %collective-permute-start.33 = (bf16[2,72,384]{2,1,0:T(8,128)(2,1)S(1)}, bf16[2,72,384]{2,1,0:T(8,128)(2,1)S(1)}, u32[]{:S(2)}, u32[]{:S(2)}) collective-permute-start(bf16[2,72,384]{2,1,0:T(8,128)(2,1)S(1)} %slice.62), channel_id=1, source_target_pairs={{0,8},{4,12},{8,0},{12,4},{16,24},{20,28},{24,16},{28,20},{1,9},{5... | collective-permute-start | bytes 331784 | tf_op jit(solution)/shard_map/ppermute | solution.py:570
  77.2 12.5 %collective-permute-start.29 = (bf16[1,144,384]{2,1,0:T(8,128)(2,1)S(1)}, bf16[1,144,384]{2,1,0:T(8,128)(2,1)S(1)}, u32[]{:S(2)}, u32[]{:S(2)}) collective-permute-start(bf16[1,144,384]{2,1,0:T(8,128)(2,1)S(1)} %slice.60), channel_id=1, source_target_pairs={{0,16},{4,20},{8,24},{12,28},{16,0},{20,4},{24,8},{28,12},{1,17},{... | collective-permute-start | bytes 331784 | tf_op jit(solution)/shard_map/ppermute | solution.py:570
  87.6 6.7 %collective-permute-start.23 = (bf16[4,56,576]{2,1,0:T(8,128)(2,1)S(1)}, bf16[4,56,576]{2,1,0:T(8,128)(2,1)S(1)}, u32[]{:S(2)}, u32[]{:S(2)}) collective-permute-start(bf16[4,56,576]{2,1,0:T(8,128)(2,1)S(1)} %get-tuple-element.115), channel_id=1, source_target_pairs={{0,4},{4,0},{8,12},{12,8},{16,20},{20,16},{24,28},{28,24},{1,5},{5... | collective-permute-start | bytes 774152 | tf_op jit(solution)/shard_map/ppermute | solution.py:570
  89.2 7.2 %collective-permute-start.34 = (bf16[1,72,384]{2,1,0:T(8,128)(2,1)S(1)}, bf16[1,72,384]{2,1,0:T(8,128)(2,1)S(1)}, u32[]{:S(2)}, u32[]{:S(2)}) collective-permute-start(bf16[1,72,384]{2,1,0:T(8,128)(2,1)S(1)} %slice.64), channel_id=1, source_target_pairs={{0,16},{4,20},{8,24},{12,28},{16,0},{20,4},{24,8},{28,12},{1,17},{... | collective-permute-start | bytes 165896 | tf_op jit(solution)/shard_map/ppermute | solution.py:570
  89.7 8.9 %collective-permute-start.30 = (bf16[1,144,384]{2,1,0:T(8,128)(2,1)S(1)}, bf16[1,144,384]{2,1,0:T(8,128)(2,1)S(1)}, u32[]{:S(2)}, u32[]{:S(2)}) collective-permute-start(bf16[1,144,384]{2,1,0:T(8,128)(2,1)S(1)} %add_convert_fusion.6), channel_id=1, source_target_pairs={{0,16},{4,20},{8,24},{12,28},{16,0},{20,4},{24,8},{28,12},{1,17},{... | collective-permute-start | bytes 331784 | tf_op jit(solution)/shard_map/ppermute | solution.py:570
  94.4 8.8 %collective-permute-start.24 = (bf16[2,56,576]{2,1,0:T(8,128)(2,1)S(1)}, bf16[2,56,576]{2,1,0:T(8,128)(2,1)S(1)}, u32[]{:S(2)}, u32[]{:S(2)}) collective-permute-start(bf16[2,56,576]{2,1,0:T(8,128)(2,1)S(1)} %slice.56), channel_id=1, source_target_pairs={{0,8},{4,12},{8,0},{12,4},{16,24},{20,28},{24,16},{28,20},{1,9},{5... | collective-permute-start | bytes 387080 | tf_op jit(solution)/shard_map/ppermute | solution.py:570
  96.5 13.8 %collective-permute-start.35 = (bf16[1,72,384]{2,1,0:T(8,128)(2,1)S(1)}, bf16[1,72,384]{2,1,0:T(8,128)(2,1)S(1)}, u32[]{:S(2)}, u32[]{:S(2)}) collective-permute-start(bf16[1,72,384]{2,1,0:T(8,128)(2,1)S(1)} %add_convert_fusion.8), channel_id=1, source_target_pairs={{0,16},{4,20},{8,24},{12,28},{16,0},{20,4},{24,8},{28,12},{1,17},{... | collective-permute-start | bytes 165896 | tf_op jit(solution)/shard_map/ppermute | solution.py:570
  98.6 7.0 %collective-permute-start.31 = (bf16[2,144,384]{2,1,0:T(8,128)(2,1)S(1)}, bf16[2,144,384]{2,1,0:T(8,128)(2,1)S(1)}, u32[]{:S(2)}, u32[]{:S(2)}) collective-permute-start(bf16[2,144,384]{2,1,0:T(8,128)(2,1)S(1)} %pad_maximum_fusion.2), channel_id=1, source_target_pairs={{0,8},{4,12},{8,0},{12,4},{16,24},{20,28},{24,16},{28,20},{1,9},{5... | collective-permute-start | bytes 663560 | tf_op jit(solution)/shard_map/ppermute | solution.py:570
  103.2 6.9 %collective-permute-start.25 = (bf16[1,56,576]{2,1,0:T(8,128)(2,1)S(1)}, bf16[1,56,576]{2,1,0:T(8,128)(2,1)S(1)}, u32[]{:S(2)}, u32[]{:S(2)}) collective-permute-start(bf16[1,56,576]{2,1,0:T(8,128)(2,1)S(1)} %slice.58), channel_id=1, source_target_pairs={{0,16},{4,20},{8,24},{12,28},{16,0},{20,4},{24,8},{28,12},{1,17},{... | collective-permute-start | bytes 193544 | tf_op jit(solution)/shard_map/ppermute | solution.py:570
  105.7 16.1 %collective-permute-start.32 = (bf16[4,144,384]{2,1,0:T(8,128)(2,1)S(1)}, bf16[4,144,384]{2,1,0:T(8,128)(2,1)S(1)}, u32[]{:S(2)}, u32[]{:S(2)}) collective-permute-start(bf16[4,144,384]{2,1,0:T(8,128)(2,1)S(1)} %pad_maximum_fusion.one_lo.first), channel_id=1, source_target_pairs={{0,4},{4,0},{8,12},{12,8},{16,20},{20,16},{24,28},{28,24},{1,5},{5... | collective-permute-start | bytes 1327112 | tf_op jit(solution)/shard_map/ppermute | solution.py:570
  110.2 5.4 %collective-permute-start.26 = (bf16[1,56,576]{2,1,0:T(8,128)(2,1)S(1)}, bf16[1,56,576]{2,1,0:T(8,128)(2,1)S(1)}, u32[]{:S(2)}, u32[]{:S(2)}) collective-permute-start(bf16[1,56,576]{2,1,0:T(8,128)(2,1)S(1)} %add_convert_fusion.7), channel_id=1, source_target_pairs={{0,16},{4,20},{8,24},{12,28},{16,0},{20,4},{24,8},{28,12},{1,17},{... | collective-permute-start | bytes 193544 | tf_op jit(solution)/shard_map/ppermute | solution.py:570
  110.3 5.7 %collective-permute-start.36 = (bf16[2,72,384]{2,1,0:T(8,128)(2,1)S(1)}, bf16[2,72,384]{2,1,0:T(8,128)(2,1)S(1)}, u32[]{:S(2)}, u32[]{:S(2)}) collective-permute-start(bf16[2,72,384]{2,1,0:T(8,128)(2,1)S(1)} %pad_maximum_fusion.5), channel_id=1, source_target_pairs={{0,8},{4,12},{8,0},{12,4},{16,24},{20,28},{24,16},{28,20},{1,9},{5... | collective-permute-start | bytes 331784 | tf_op jit(solution)/shard_map/ppermute | solution.py:570
  115.6 5.2 %collective-permute-start.27 = (bf16[2,56,576]{2,1,0:T(8,128)(2,1)S(1)}, bf16[2,56,576]{2,1,0:T(8,128)(2,1)S(1)}, u32[]{:S(2)}, u32[]{:S(2)}) collective-permute-start(bf16[2,56,576]{2,1,0:T(8,128)(2,1)S(1)} %pad_maximum_fusion.4), channel_id=1, source_target_pairs={{0,8},{4,12},{8,0},{12,4},{16,24},{20,28},{24,16},{28,20},{1,9},{5... | collective-permute-start | bytes 387080 | tf_op jit(solution)/shard_map/ppermute | solution.py:570
  116.1 7.3 %collective-permute-start.37 = (bf16[4,72,384]{2,1,0:T(8,128)(2,1)S(1)}, bf16[4,72,384]{2,1,0:T(8,128)(2,1)S(1)}, u32[]{:S(2)}, u32[]{:S(2)}) collective-permute-start(bf16[4,72,384]{2,1,0:T(8,128)(2,1)S(1)} %pad_maximum_fusion.3.two_lo), channel_id=1, source_target_pairs={{0,4},{4,0},{8,12},{12,8},{16,20},{20,16},{24,28},{28,24},{1,5},{5... | collective-permute-start | bytes 663560 | tf_op jit(solution)/shard_map/ppermute | solution.py:570
  120.8 6.7 %collective-permute-start.28 = (bf16[4,56,576]{2,1,0:T(8,128)(2,1)S(1)}, bf16[4,56,576]{2,1,0:T(8,128)(2,1)S(1)}, u32[]{:S(2)}, u32[]{:S(2)}) collective-permute-start(bf16[4,56,576]{2,1,0:T(8,128)(2,1)S(1)} %pad_maximum_fusion.1.first), channel_id=1, source_target_pairs={{0,4},{4,0},{8,12},{12,8},{16,20},{20,16},{24,28},{28,24},{1,5},{5... | collective-permute-start | bytes 774152 | tf_op jit(solution)/shard_map/ppermute | solution.py:570
  (11 other events, 101.6 us)
